TPU v7x, 32 devices: a whole 2x2x4 slice. The times are simulated.
32 devices in a mesh: row: 8 (over z, x), col: 4 (over y, core).
Axes of the slice: x: 2, y: 2, z: 4, core: 2. Of those that a mesh axis runs over, the one named last changes fastest.
Arguments:
- tokens: bfloat16 [4096, 768], P(('row', 'col')), may hold values from -6 to 6
- w_qkv: bfloat16 [768, 3, 768], P('row', None, 'col'), may hold values from -0.21875 to 0.21875
- w_out: bfloat16 [768, 768], P('col', 'row'), may hold values from -2.5 to 2.5
- w_gate_up: bfloat16 [768, 2, 3072], P('row', None, 'col'), may hold values from -0.21875 to 0.21875
- w_down: bfloat16 [3072, 768], P('col', 'row'), may hold values from -0.109375 to 0.109375
- gain1: float32 [768], replicated, may hold values from 0.1 to 1.9
- bias1: float32 [768], replicated, may hold values from -1.8 to 1.8
- gain2: float32 [768], replicated, may hold values from 0.1 to 1.9
- bias2: float32 [768], replicated, may hold values from -1.8 to 1.8
- cotangent: bfloat16 [4096, 768], P(('row', 'col')), may hold values from -6 to 6
- seq_lengths: int32 [3], replicated, may hold values from 512 to 2048, as said below
- packed_order: int32 [4096], replicated, may hold values from 0 to 4095, each once
Outputs:
- output: bfloat16 [4096, 768], P(('row', 'col'))
- grad_tokens: float32 [4096, 768], P(('row', 'col'))
- grad_w_qkv: float32 [768, 3, 768], P('row', None, 'col')
- grad_w_out: float32 [768, 768], P('col', 'row')
- grad_w_gate_up: float32 [768, 2, 3072], P('row', None, 'col')
- grad_w_down: float32 [3072, 768], P('col', 'row')
- grad_gain1: float32 [768], replicated
- grad_bias1: float32 [768], replicated
- grad_gain2: float32 [768], replicated
- grad_bias2: float32 [768], replicated
Inputs may be any that keep to these rules, and one draw needn't show every extreme that they name: `seq_lengths`: 3 lengths that sum to 4096; the longest is exactly 2048.
All inputs are finite; a program needn't handle non-finite values.
Results may differ from a plain program's by a relative error of at most 0.024.
Values may be sent and summed in bfloat16 or wider, within the bound.
No kernel may reach another device: no remote copies, remote signals or barrier semaphores. Data moves between devices by JAX's collectives and lax.ppermute only.
A program may use at most 512 MiB of HBM per device.

v0:
```python
import functools
import math

import jax
import jax.numpy as jnp
from jax import lax
from jax.experimental import pallas as pl
from jax.experimental.pallas import tpu as pltpu
from jax.sharding import PartitionSpec as P

HEAD = 64
ROPE_BASE = 1000.0
NORM_EPS = 1e-12
FAR = -(2.0**100)
LOWEST = -1e30
AUX = 16
BF = jnp.bfloat16
F32 = jnp.float32

CYCLE = (0, 2, 4, 6, 7, 5, 3, 1)
OFFSETS = (0, 2, 1, 3)


def dot(a, b, contract, out=F32):
    return lax.dot_general(a, b, (contract, ((), ())), preferred_element_type=out)


COST = 0.02

NN = ((1,), (0,))
NT = ((1,), (1,))
TN = ((0,), (0,))


def forward_hop(v):
    n = len(CYCLE)
    return lax.ppermute(v, "row", [(CYCLE[i], CYCLE[(i + 1) % n]) for i in range(n)])


def backward_hop(v):
    n = len(CYCLE)
    return lax.ppermute(v, "row", [(CYCLE[(i + 1) % n], CYCLE[i]) for i in range(n)])


def col_swap(v, mask):
    count = lax.axis_size("col")
    return lax.ppermute(v, "col", [(i, i ^ mask) for i in range(count)])


def cycle_place():
    row = lax.axis_index("row")
    return sum(jnp.where(row == CYCLE[i], i, 0) for i in range(len(CYCLE))).astype(jnp.int32)


def cycle_rows(place, steps):
    places = lax.rem(place + jnp.array([s + len(CYCLE) for s in steps], jnp.int32), len(CYCLE))
    return sum(jnp.where(places == i, CYCLE[i], 0) for i in range(len(CYCLE))).astype(jnp.int32)


def after(value, *first):
    return lax.optimization_barrier((value, first))[0]


class Rounds:
    def __init__(self, block, axis):
        self.block, self.held, self.axis, self.done = block, (block, block), axis, []

    def step(self, *first):
        behind, ahead = after(self.held, first) if first else self.held
        if len(self.done) == 3:
            half = behind.shape[self.axis] // 2
            behind = lax.slice_in_dim(behind, 0, half, axis=self.axis)
            ahead = lax.slice_in_dim(ahead, half, 2 * half, axis=self.axis)
        self.held = forward_hop(behind), backward_hop(ahead)
        self.done.append(self.held)
        return self.held

    def pieces(self):
        while len(self.done) < 4:
            self.step()
        return [p for r in self.done for p in r]


ROUND_STEPS = (-1, 1, -2, 2, -3, 3, 4, 4)
BLOCK_STEPS = (0, 1, 2, 3, 4, 4, 5, 6, 7)


class RowSum:
    def __init__(self, blocks):
        self.blocks, self.hops, self.moving = blocks, 0, None
        if len(blocks) > 1:
            self.moving = blocks[4], blocks[5]

    def step(self):
        if len(self.blocks) == 1:
            return ()
        half = self.blocks[4].shape[0]

        def add(v, block):
            return (v.astype(F32) + block.astype(F32)).astype(BF)

        ahead, back = forward_hop(self.moving[0]), backward_hop(self.moving[1])
        up = (self.blocks[3], self.blocks[2], self.blocks[1], None)[self.hops]
        down = (self.blocks[6], self.blocks[7], self.blocks[8], None)[self.hops]
        if self.hops == 0:
            ahead = jnp.concatenate([add(ahead, up[:half]), up[half:]], axis=0)
            back = jnp.concatenate([down[:half], add(back, down[half:])], axis=0)
        elif up is not None:
            ahead, back = add(ahead, up), add(back, down)
        self.hops += 1
        self.moving = ahead, back
        return self.moving

    def result(self):
        if len(self.blocks) == 1:
            return lax.psum_scatter(self.blocks[0].astype(F32), "row", scatter_dimension=0, tiled=True)
        while self.hops < 4:
            self.step()
        ahead, back = self.moving
        return self.blocks[0].astype(F32) + ahead.astype(F32) + back.astype(F32)


def col_pieces(v, *first):
    side = col_swap(v, 2)
    return [v, side, col_swap(v, 1), col_swap(after(side, first), 1)]


def col_exchange(near, far):
    own = near.shape[0] // 2
    other = col_swap(far, 1)
    passed = (near[own:].astype(F32) + other[own:].astype(F32)).astype(BF)
    return (near, other, col_swap(passed, 2)), passed


def whole(shape):
    return pl.BlockSpec(shape, lambda *_: (0,) * len(shape))


ANY = pl.BlockSpec(memory_space=pl.ANY)


def call(kernel, name, args, outs, prefetch=(), scratch=(), specs=None, out_specs=None, aliases=None, grid=(1,), flops=0, exps=0, limit=20):
    args, outs = list(args), list(outs)
    moved = sum(a.size * a.dtype.itemsize for a in args) + sum(
        math.prod(o.shape) * o.dtype.itemsize for o in outs
    )
    return pl.pallas_call(
        kernel,
        grid_spec=pltpu.PrefetchScalarGridSpec(
            num_scalar_prefetch=len(prefetch),
            grid=grid,
            in_specs=specs or [whole(a.shape) for a in args],
            out_specs=out_specs or [whole(o.shape) for o in outs],
            scratch_shapes=list(scratch),
        ),
        out_shape=outs,
        input_output_aliases=aliases or {},
        cost_estimate=pl.CostEstimate(flops=int(flops * COST), bytes_accessed=int(moved * COST), transcendentals=int(exps * COST)),
        compiler_params=pltpu.CompilerParams(vmem_limit_bytes=limit << 20),
        name=name,
    )(*prefetch, *args)


def struct(shape, kind):
    return jax.ShapeDtypeStruct(tuple(shape), kind)


def rows_at(start, count):
    return pl.ds(pl.multiple_of(start, 4), count)


def assemble_kernel(split, cuts, starts, *refs):
    pieces, (mix, out, held) = refs[:-3], refs[-3:]
    for i, piece in enumerate(pieces):
        for begin, count, shift in cuts[i]:
            held[pl.ds(pl.multiple_of(starts[i] + shift, 16), count), :] = piece[begin : begin + count]
    mix[...] = held[:, :split].T
    out[...] = held[:, split:].T


def assemble(pieces, cuts, starts, split):
    width = pieces[0].shape[1]
    total = sum(c[1] for cut in cuts for c in cut)
    return call(
        functools.partial(assemble_kernel, split, cuts),
        "assemble",
        pieces,
        [struct((split, total), BF), struct((width - split, total), BF)],
        prefetch=[starts],
        scratch=[pltpu.VMEM((total, width), BF)],
    )


def project_into(pieces, weight, turn, marks, q_out, k_out, v_out, heads):
    half = HEAD // 2
    width = heads * HEAD
    begin = 0
    for piece in pieces:
        count = piece.shape[0]
        lanes = slice(begin, begin + count)
        begin += count
        mixed = dot(weight[...], piece[...], NT)
        cosine, sine = turn[:half, lanes], turn[half:, lanes]
        for h in range(heads):
            for base, out, scale, tail in (
                (0, q_out, 1.0 / math.sqrt(HEAD), AUX),
                (width, k_out, None, 0),
            ):
                at = base + h * HEAD
                first, second = mixed[at : at + half], mixed[at + half : at + HEAD]
                turned = jnp.concatenate(
                    [first * cosine - second * sine, second * cosine + first * sine], axis=0
                )
                if scale is not None:
                    turned = turned * scale
                out[h, :HEAD, lanes] = turned.astype(BF)
                out[h, HEAD:, lanes] = marks[tail : tail + AUX, lanes]
            at = 2 * width + h * HEAD
            v_out[h, :HEAD, lanes] = mixed[at : at + HEAD].astype(BF)
            v_out[h, HEAD:, lanes] = marks[2 * AUX : 3 * AUX, lanes]


def attend_kernel(mode, heads, count, slot, *refs):
    pieces, refs = refs[:count], refs[count:]
    weight, turn, marks = refs[:3]
    refs = refs[3:]
    if mode != "first":
        q_own, top_in, sum_in, acc_in = refs[:4]
        refs = refs[7:]
    if mode == "last":
        w_out, refs = refs[0], refs[1:]
    k, v, q = refs[:3]
    refs = refs[3:]
    project_into(pieces, weight, turn, marks, q, k, v, heads)
    if mode == "first":
        q_own, refs = refs[0], refs[1:]
        q_own[...] = q[...]
    each = range(heads)
    scores = [dot(k[h], q_own[h], TN) for h in each]
    news = [jnp.max(s, axis=0, keepdims=True) for s in scores]
    if mode != "first":
        olds = [top_in[h : h + 1] for h in each]
        news = [jnp.maximum(o, n) for o, n in zip(olds, news)]
        keeps = [jnp.exp(o - n) for o, n in zip(olds, news)]
    weights = [jnp.exp(s - n) for s, n in zip(scores, news)]
    sums = [jnp.sum(w, axis=0, keepdims=True) for w in weights]
    values = [dot(v[h, :HEAD, :], w.astype(BF), NN) for h, w in enumerate(weights)]
    if mode != "first":
        sums = [sum_in[h : h + 1] * keeps[h] + sums[h] for h in each]
        values = [acc_in[h] * keeps[h] + values[h] for h in each]
    if mode != "last":
        top, total, acc = refs
        for h in each:
            top[h : h + 1] = news[h]
            total[h : h + 1] = sums[h]
            acc[h] = values[h]
        return
    near, far, context_bf, context, log_total = refs
    for h in each:
        value = values[h] / sums[h]
        context[h] = value
        context_bf[h * HEAD : (h + 1) * HEAD] = value.astype(BF)
        log_total[h : h + 1] = news[h] + jnp.log(sums[h])
    attn = dot(context_bf[...], w_out[...], TN)
    half = near.shape[0]
    near[...] = attn[:half].astype(BF)
    far[...] = attn[half:].astype(BF)


def attend(mode, pieces, slot, weight, turn, marks, heads, total, group, carried=(), w_out=None):
    width = sum(p.shape[0] for p in pieces)
    rows = HEAD + AUX

    def lanes(*lead):
        return pl.BlockSpec((*lead, width), lambda i, s: (*(0,) * len(lead), s[0]))

    args = [*pieces, weight, turn, marks, *carried]
    specs = [whole(p.shape) for p in pieces]
    specs += [whole(weight.shape), lanes(turn.shape[0]), lanes(marks.shape[0])]
    buffers = [struct((heads, rows, total), BF)] * 3
    outs, out_specs = list(buffers), [lanes(heads, rows)] * 3
    aliases = {}
    if mode != "first":
        specs += [whole(c.shape) for c in carried[:4]] + [ANY] * 3
        base = 1 + len(pieces) + 3 + 4
        aliases = {base: 0, base + 1: 1, base + 2: 2}
    features = weight.shape[1]
    if mode == "last":
        args.append(w_out)
        specs.append(whole(w_out.shape))
        extra = [
            struct((group // 2, features), BF),
            struct((group // 2, features), BF),
            struct((heads * HEAD, group), BF),
            struct((heads, HEAD, group), F32),
            struct((heads, group), F32),
        ]
    else:
        extra = [
            struct((heads, group), F32),
            struct((heads, group), F32),
            struct((heads, HEAD, group), F32),
        ]
        if mode == "first":
            extra = [struct((heads, rows, group), BF)] + extra
    outs += extra
    out_specs += [whole(e.shape) for e in extra]
    scores = heads * width * group
    return call(
        functools.partial(attend_kernel, mode, heads, len(pieces)),
        "attend",
        args,
        outs,
        prefetch=[slot],
        specs=specs,
        out_specs=out_specs,
        aliases=aliases,
        flops=scores * 512,
        exps=scores,
    )


def with_terms(q, g):
    return jnp.concatenate([q[:HEAD], q[HEAD:] + g[HEAD:]], axis=0)


def query_grad_kernel(heads, q, g, k, v, out_in, out):
    @pl.when(pl.program_id(0) == 0)
    def _():
        out[...] = out_in[...]

    rows = HEAD + AUX
    each = range(heads)
    terms = [g[h * rows : (h + 1) * rows] for h in each]
    probs = [jnp.exp(dot(k[h], with_terms(q[h], terms[h]), TN)) for h in each]
    grads = [(probs[h] * dot(v[h], terms[h], TN)).astype(BF) for h in each]
    for h in each:
        out[h] += dot(k[h, :HEAD, :], grads[h], NN)


def query_grad(q, g, keys, values, heads, width, begin, steps, carried):
    rows = keys.shape[1]
    group = q.shape[2]
    each = pl.BlockSpec((heads, rows, width), lambda i: (0, 0, i + begin))
    scores = heads * group * steps * width
    return call(
        functools.partial(query_grad_kernel, heads),
        "query_grad",
        [q, g, keys, values, carried],
        [struct((heads, HEAD, group), F32)],
        specs=[whole(q.shape), whole(g.shape), each, each, whole(carried.shape)],
        grid=(steps,),
        flops=scores * 768,
        exps=scores,
    )[0]


def key_grad_kernel(heads, count, step, carried, slots, *refs):
    pieces, (q, k, v), refs = refs[:count], refs[count : count + 3], refs[count + 3 :]
    rows = HEAD + AUX
    each = range(heads)
    if carried:
        dk_in, dv_in = refs[:2]
        refs = refs[2:]
    dk, dv, norms = refs

    def of(h):
        if count == 1:
            return pieces[0][h * rows : (h + 1) * rows]
        lanes = [slice(i, i + step) for i in range(0, pieces[0].shape[1], step)]
        return jnp.concatenate([p[h * rows : (h + 1) * rows, n] for n in lanes for p in pieces], axis=1)

    terms = [of(h) for h in each]
    probs = [jnp.exp(dot(with_terms(q[h], terms[h]), k[h], TN)) for h in each]
    grads = [(probs[h] * dot(terms[h], v[h], TN)).astype(BF) for h in each]
    for h in each:
        value = dot(terms[h][:HEAD], probs[h].astype(BF), NN)
        key = dot(q[h, :HEAD, :], grads[h], NN)
        dv[h] = dv_in[h] + value if carried else value
        dk[h] = dk_in[h] + key if carried else key
    for i in range(norms.shape[0]):
        norms[i] = pieces[i][heads * rows : heads * rows + NORM_ROWS, :NORM_LANES].astype(F32)


NORM_LANES = 256


def key_grad(pieces, chunks, step, slots, q, keys, values, heads, group, sums=()):
    width = sum(p.shape[1] for p in pieces)
    rows = HEAD + AUX
    own = pl.BlockSpec((heads, rows, group), lambda i, s: (0, 0, s[1]))
    specs = [whole(p.shape) for p in pieces]
    specs += [pl.BlockSpec((heads, rows, width), lambda i, s: (0, 0, s[0])), own, own]
    specs += [whole(s.shape) for s in sums]
    scores = heads * group * width
    return call(
        functools.partial(key_grad_kernel, heads, len(pieces), step, bool(sums)),
        "key_grad",
        [*pieces, q, keys, values, *sums],
        [struct((heads, HEAD, group), F32)] * 2 + [struct((chunks, NORM_ROWS, NORM_LANES), F32)],
        prefetch=[slots],
        specs=specs,
        flops=scores * 1024,
        exps=scores,
    )


def norm_parts(values):
    centered = values - jnp.mean(values, axis=-1, keepdims=True)
    inverse = lax.rsqrt(jnp.mean(centered * centered, axis=-1, keepdims=True) + NORM_EPS)
    return centered * inverse, inverse


def norm_back(grad_out, normed, inverse, gain):
    scaled = grad_out * gain
    grad_in = inverse * (
        scaled
        - jnp.mean(scaled, axis=-1, keepdims=True)
        - normed * jnp.mean(scaled * normed, axis=-1, keepdims=True)
    )
    sums = [jnp.sum(grad_out * normed, axis=0, keepdims=True), jnp.sum(grad_out, axis=0, keepdims=True)]
    return grad_in, sums


def col_total(near, other, last):
    own = last.shape[0]
    return near[:own].astype(F32) + other[:own].astype(F32) + last[...].astype(F32)


def first_norm_kernel(near, other, last, tokens, gain, bias, residual, hidden):
    value = tokens[...].astype(F32) + col_total(near, other, last)
    residual[...] = value
    normed, _ = norm_parts(value)
    hidden[...] = (normed * gain[...] + bias[...]).astype(BF)


def second_norm_kernel(near, other, last, residual, gain1, bias1, gain2, bias2, cotangent, result, grad, grad_bf, sums):
    hidden = norm_parts(residual[...])[0] * gain1[...] + bias1[...]
    normed, inverse = norm_parts(hidden + col_total(near, other, last))
    result[...] = (normed * gain2[...] + bias2[...]).astype(BF)
    value, (dgain, dbias) = norm_back(cotangent[...].astype(F32), normed, inverse, gain2[...])
    grad[...] = value
    grad_bf[...] = value.astype(BF)
    sums[0:1] = dgain
    sums[1:2] = dbias


def first_norm_back_kernel(near, other, last, residual, gain, grad2, sums2, grad, package):
    normed, inverse = norm_parts(residual[...])
    grad_out = grad2[...] + col_total(near, other, last)
    value, (dgain, dbias) = norm_back(grad_out, normed, inverse, gain[...])
    grad[...] = value
    own = value.shape[0]
    package[:own] = value.astype(BF)
    sums = jnp.concatenate([dgain, dbias, sums2[0:1], sums2[1:2]], axis=0)
    high = sums.astype(BF)
    low = (sums - high.astype(F32)).astype(BF)
    blank = jnp.zeros((8, sums.shape[1]), F32)
    package[own:] = jnp.concatenate([high.astype(F32), low.astype(F32), blank], axis=0).astype(BF)


def stacked(refs, rows):
    return jnp.concatenate([r[:rows] for r in refs], axis=0)


def forward_kernel(count, units, starts, *refs):
    pieces, hidden, (gu, dn, gate_up, inner, near, far) = refs[:count], refs[count:-6], refs[-6:]
    for i, piece in enumerate(pieces):
        rows = pl.ds(pl.multiple_of(starts[i], 16), piece.shape[0])
        gu[rows, :] = piece[:, : 2 * units]
        dn[rows, :] = piece[:, 2 * units :]
    pairs = len(hidden) // 2
    for out, part in ((near, hidden[:pairs]), (far, hidden[pairs:])):
        x = stacked(part, part[0].shape[0])
        size = x.shape[0]
        begin = 0 if out is near else size
        both = dot(x, gu[...], NN)
        gate_up[begin : begin + size] = both
        up, gate = both[:, :units], both[:, units:]
        value = (gate * jax.nn.sigmoid(gate) * up).astype(BF)
        inner[begin : begin + size] = value
        out[...] = dot(value, dn[...], NT).astype(BF)


def backward_kernel(units, *refs):
    pieces, (gu, dn, gate_up, grads, near, far) = refs[:-6], refs[-6:]
    pairs = len(pieces) // 2
    for out, part in ((near, pieces[:pairs]), (far, pieces[pairs:])):
        g = stacked(part, part[0].shape[0])
        size = g.shape[0]
        begin = 0 if out is near else size
        grad_inner = dot(g, dn[...], NN)
        up = gate_up[begin : begin + size, :units]
        gate = gate_up[begin : begin + size, units:]
        sigma = jax.nn.sigmoid(gate)
        grads[begin : begin + size, :units] = (grad_inner * gate * sigma).astype(BF)
        grads[begin : begin + size, units:] = (
            grad_inner * up * sigma * (1.0 + gate * (1.0 - sigma))
        ).astype(BF)
        out[...] = dot(grads[begin : begin + size], gu[...], NT).astype(BF)


def write_blocks(held, starts, outs):
    for i, out in enumerate(outs):
        out[...] = held[pl.ds(pl.multiple_of(starts[i], 16), out.shape[0]), :]


def block_structs(features, width, ring):
    if not ring:
        return [struct((features, width), BF)]
    share = features // len(CYCLE)
    sizes = [share] * 4 + [share // 2] * 2 + [share] * 3
    return [struct((n, width), BF) for n in sizes]


def ffn_grad_kernel(units, n_blocks, starts, *refs):
    hidden, g, (grads, inner) = refs[:4], refs[4:8], refs[8:10]
    outs, held = refs[10 : 10 + n_blocks], refs[10 + n_blocks]
    own = hidden[0].shape[0]
    turned = stacked(hidden, own).T
    for t in range(0, 2 * units, units):
        held[:, t : t + units] = dot(turned, grads[:, t : t + units], NN).astype(BF)
    held[:, 2 * units :] = dot(stacked(g, own).T, inner[...], NN).astype(BF)
    write_blocks(held, starts, outs)


def prepare_kernel(heads, own, *refs):
    pieces, (w_out, context, log_total, package) = refs[:4], refs[4:]
    g = stacked(pieces, own)
    rows = HEAD + AUX
    grad = dot(w_out[...], g, NT).astype(BF)
    index = lax.broadcasted_iota(jnp.int32, (AUX, g.shape[0]), 0)
    for h in range(heads):
        part = grad[h * HEAD : (h + 1) * HEAD]
        package[h * rows : h * rows + HEAD] = part
        delta = jnp.sum(part.astype(F32) * context[h], axis=0, keepdims=True)
        tail = jnp.zeros(index.shape, F32)
        for at, value in ((8, -log_total[h : h + 1]), (11, -delta)):
            for j in range(3):
                high = value.astype(BF).astype(F32)
                tail = jnp.where(index == at + j, high, tail)
                value = value - high
        package[h * rows + HEAD : (h + 1) * rows] = tail.astype(BF)

    def sums(piece):
        both = piece[own : own + 16].astype(F32)
        return both[:4] + both[4:8]

    total = (sums(pieces[0]) + sums(pieces[1])) + (sums(pieces[2]) + sums(pieces[3]))
    high = total.astype(BF).astype(F32)
    both = jnp.concatenate([high, total - high], axis=0)
    base = heads * rows
    package[base:, NORM_LANES:] = jnp.zeros((package.shape[0] - base, package.shape[1] - NORM_LANES), BF)
    parts = [both[:, i * NORM_LANES : (i + 1) * NORM_LANES] for i in range(both.shape[1] // NORM_LANES)]
    parts.append(jnp.zeros((package.shape[0] - base - 8 * len(parts), NORM_LANES), F32))
    package[base:, :NORM_LANES] = jnp.concatenate(parts, axis=0).astype(BF)


def turn_back(first, second, cosine, sine):
    return jnp.concatenate([first * cosine + second * sine, second * cosine - first * sine], axis=0)


def early_grad_kernel(heads, own, n_x, slots, *refs):
    x_refs, g_refs, refs = refs[:n_x], refs[n_x : n_x + 4], refs[n_x + 4 :]
    grad_query, turn, context, mixed, held = refs
    half = HEAD // 2
    scale = 1.0 / math.sqrt(HEAD)
    for h in range(heads):
        value = grad_query[h] * scale
        mixed[h * HEAD : (h + 1) * HEAD] = turn_back(value[:half], value[half:], turn[:half], turn[half:]).astype(BF)
    x = stacked(x_refs, x_refs[0].shape[0])
    width = heads * HEAD
    held[:, :width] = dot(mixed[...], x, NN).T.astype(BF)
    held[:, width:] = dot(context[...], stacked(g_refs, own), NN).T.astype(BF)


def late_grad_kernel(heads, n_x, n_blocks, slots, starts, *refs):
    x_refs, refs = refs[:n_x], refs[n_x:]
    mixed_q, grad_key, grad_value, early, turn, weight, near, far, *refs = refs
    outs, held, mixed = refs[:n_blocks], refs[n_blocks], refs[n_blocks + 1]
    half = HEAD // 2
    width = heads * HEAD
    mixed[:width] = mixed_q[...]
    for h in range(heads):
        value = grad_key[h]
        mixed[width + h * HEAD : width + (h + 1) * HEAD] = turn_back(
            value[:half], value[half:], turn[:half], turn[half:]
        ).astype(BF)
        mixed[2 * width + h * HEAD : 2 * width + (h + 1) * HEAD] = grad_value[h].astype(BF)
    back = dot(mixed[...], weight[...], TN)
    size = near.shape[0]
    near[...] = back[:size].astype(BF)
    far[...] = back[size:].astype(BF)
    x = stacked(x_refs, x_refs[0].shape[0])
    held[:, : 2 * width] = early[...]
    held[:, 2 * width :] = dot(mixed[width:], x, NN).T.astype(BF)
    write_blocks(held, starts, outs)


NORM_ROWS = 24


def norm_total_kernel(rows, *refs):
    pieces, (out, held) = refs[:-2], refs[-2:]
    at = 0
    for piece in pieces:
        for i in range(piece.shape[0]):
            held[rows[at]] = piece[i]
            at += 1
    total = held[0]
    for r in range(1, at):
        total = total + held[r]
    for i in range(NORM_ROWS // 8):
        part = total[8 * i : 8 * i + 8]
        out[:, i * NORM_LANES : (i + 1) * NORM_LANES] = part[:4] + part[4:]


def slot_tables(seq_lengths, packed_order, wanted, local, waits):
    blocks = packed_order.reshape(-1, local)
    index = jnp.arange(blocks.shape[0], dtype=jnp.int32)
    slots = jnp.sum(
        jnp.where(wanted[:, None, None] == index[None, :, None], blocks[None], 0), axis=1
    ).reshape(1, -1)
    count = seq_lengths.shape[0]
    seq = jnp.zeros_like(slots)
    start = jnp.zeros_like(slots)
    end = jnp.int32(0)
    for s in range(count):
        end = end + seq_lengths[s]
        passed = slots >= end
        seq = seq + passed.astype(jnp.int32)
        start = jnp.where(passed, end, start)
    positions = after((slots - start).astype(F32), waits[0])
    half = HEAD // 2
    freqs = ROPE_BASE ** (-jnp.arange(half, dtype=F32) * 2.0 / HEAD)
    angles = positions * freqs[:, None]
    turn = jnp.concatenate([jnp.cos(angles), jnp.sin(angles)], axis=0)
    line = jnp.arange(3 * AUX, dtype=jnp.int32)[:, None]
    member = lax.rem(line, AUX) == after(seq, waits[1])
    ones = ((line >= 8) & (line < 11)) | ((line >= 2 * AUX + 11) & (line < 2 * AUX + 14))
    marks = jnp.where(ones, 1.0, 0.0)
    marks = jnp.where((line < 8) & member, 1.0, marks)
    marks = jnp.where((line >= AUX) & (line < AUX + 8) & ~member, FAR, marks)
    return turn, marks.astype(BF)


def local(
    tokens,
    w_qkv,
    w_out,
    w_gate_up,
    w_down,
    gain1,
    bias1,
    gain2,
    bias2,
    cotangent,
    seq_lengths,
    packed_order,
):
    rows = lax.axis_size("row")
    row, col = lax.axis_index("row"), lax.axis_index("col")
    ring = rows == len(CYCLE)
    own, features = tokens.shape
    group = own * lax.axis_size("col")
    total = group * rows
    share = w_qkv.shape[0]
    width = w_qkv.shape[2]
    heads = width // HEAD
    units = w_gate_up.shape[2]
    gains = [v.reshape(1, features) for v in (gain1, bias1, gain2, bias2)]

    early = jnp.concatenate([w_qkv.reshape(share, 3 * width), w_out.T], axis=1)
    late = jnp.concatenate([w_gate_up.reshape(share, 2 * units), w_down.T], axis=1)

    pair = jnp.concatenate([tokens, col_swap(tokens, 2)], axis=0)
    if ring:
        place = cycle_place()
        half = share // 2
        starts = cycle_rows(place, (0, *ROUND_STEPS)) * share + jnp.array([0] * 8 + [half], jnp.int32)
        block_starts = cycle_rows(place, BLOCK_STEPS) * share + jnp.array([0] * 5 + [half] + [0] * 3, jnp.int32)
        layout = [(ROUND_STEPS[2 * i + j], o) for i in range(3) for o in OFFSETS for j in range(2)]
        layout += [(step, o) for step in (0, 4) for o in OFFSETS]
        wanted = cycle_rows(place, [step for step, _ in layout]) * len(OFFSETS)
        wanted = wanted + (col ^ jnp.array([o for _, o in layout], jnp.int32))
        token_half = own // 2
        ring_early = Rounds(
            jnp.concatenate(
                [early[:half], tokens[:token_half], early[half:], tokens[token_half:]], axis=0
            ),
            0,
        )
        waits = [ring_early.step(), ring_early.step()]
        ring_early.step()
        ring_early.step()
        packed_order = after(packed_order, waits[0])

        def token_rows(v):
            step = half + token_half
            return [v[i + half : i + step] for i in range(0, v.shape[0], step)]

    else:
        starts = block_starts = jnp.zeros((1,), jnp.int32)
        wanted = jnp.arange(rows, dtype=jnp.int32)[:, None] * len(OFFSETS)
        wanted = (wanted + (col ^ jnp.array(OFFSETS, jnp.int32))[None, :]).reshape(-1)
        waits = (), ()
        early_full = lax.all_gather(early, "row", axis=0, tiled=True)
        w_mix, full_out = assemble([early_full], [[(0, features, 0)]], starts, 3 * width)

    turn, marks = slot_tables(seq_lengths, packed_order, wanted, own, waits)
    if ring:
        cuts = [[(0, half, 0), (half + token_half, half, half)]] * 7 + [[(0, half, 0)]] * 2
        w_mix, full_out = assemble([ring_early.block, *ring_early.pieces()], cuts, starts, 3 * width)
    fixed = (w_mix, turn, marks, heads, total, group)
    if ring:
        pair = after(pair, ring_early.done[3])
    x_pieces = [pair, col_swap(pair, 1)]

    def at(slot):
        return jnp.asarray(slot, jnp.int32).reshape(1)

    own_slot = at(6) if ring else at(row)
    keys, values, queries, own_q, *state = attend("first", x_pieces, own_slot, *fixed)
    if ring:
        late_ring = Rounds(late, 0)
        rounds = ring_early.done

        def side(held):
            both = jnp.concatenate([rows for v in held for rows in token_rows(v)], axis=0)
            return jnp.concatenate([both, col_swap(both, 2)], axis=0)

        def middle(i, chunk):
            return attend(
                "middle",
                [chunk, col_swap(chunk, 1)],
                at(i),
                *fixed,
                (own_q, *state, keys, values, queries),
            )

        one = side(rounds[0])
        two = side(after(rounds[1], one))
        three = side(after(rounds[2], two))
        late_ring.step(rounds[2])
        two = after(two, state[0])
        keys, values, queries, *state = middle(0, after(one, rounds[3]))
        far = side(after(rounds[3], three))
        three = after(three, state[0])
        keys, values, queries, *state = middle(1, after(two, late_ring.done[0]))
        late_ring.step()
        far = after(far, state[0])
        keys, values, queries, *state = middle(2, three)
        keys, values, queries, *finished = attend(
            "last",
            [far, col_swap(far, 1)],
            at(7),
            *fixed,
            (own_q, *state, keys, values, queries),
            full_out,
        )
    else:
        blocks = lax.all_gather(jnp.concatenate(x_pieces, axis=0), "row", axis=0, tiled=False)

        def block(i):
            slot = lax.rem(row + i, rows)
            return [lax.dynamic_index_in_dim(blocks, slot, 0, keepdims=False)], at(slot)

        def step(i, carried):
            *state, keys, values, queries = carried
            keys, values, queries, *state = attend(
                "middle", *block(i), *fixed, (own_q, *state, keys, values, queries)
            )
            return (*state, keys, values, queries)

        *state, keys, values, queries = lax.fori_loop(1, rows - 1, step, (*state, keys, values, queries))
        keys, values, queries, *finished = attend(
            "last", *block(rows - 1), *fixed, (own_q, *state, keys, values, queries), full_out
        )
    near, far, context_bf, context, log_total = finished

    if ring:
        near = after(near, late_ring.done[1])
        late_ring.step(near)
    else:
        late_pieces = [lax.all_gather(late, "row", axis=0, tiled=True)]

    part = struct((group // 2, features), BF)
    flat = struct((own, features), F32)
    residual1, hidden = call(
        first_norm_kernel,
        "first_norm",
        [*col_exchange(near, far)[0], tokens, *gains[:2]],
        [flat, struct((own, features), BF)],
    )
    if ring:
        hidden_pieces = col_pieces(hidden, late_ring.done[2])
        late_pieces = [late, *late_ring.pieces()]
    else:
        hidden_pieces = col_pieces(hidden)
    w_gu, w_dn, gate_up, inner, near, far = call(
        functools.partial(forward_kernel, len(late_pieces), units),
        "ffn_forward",
        [*late_pieces, *hidden_pieces],
        [
            struct((features, 2 * units), BF),
            struct((features, units), BF),
            struct((group, 2 * units), F32),
            struct((group, units), BF),
            part,
            part,
        ],
        prefetch=[starts],
        flops=6 * group * features * units,
    )
    result, grad_res2, grad_bf, sums2 = call(
        second_norm_kernel,
        "second_norm",
        [*col_exchange(near, far)[0], residual1, *gains, cotangent],
        [struct((own, features), BF), flat, struct((own, features), BF), struct((8, features), F32)],
    )
    grad_pieces = col_pieces(grad_bf)
    grad_gate_up, near, far = call(
        functools.partial(backward_kernel, units),
        "ffn_backward",
        [*grad_pieces, w_gu, w_dn, gate_up],
        [struct((group, 2 * units), BF), part, part],
        flops=6 * group * features * units,
    )
    exchanged, passed = col_exchange(near, far)
    grad_gate_up = after(grad_gate_up, passed)
    outs = block_structs(features, 3 * units, ring)
    blocks = call(
        functools.partial(ffn_grad_kernel, units, len(outs)),
        "ffn_grad",
        [*hidden_pieces, *grad_pieces, grad_gate_up, inner],
        outs,
        prefetch=[block_starts],
        scratch=[pltpu.VMEM((features, 3 * units), BF)],
        flops=6 * group * features * units,
    )
    residual1 = after(residual1, blocks)
    ffn_sum = RowSum(blocks)
    sent = ffn_sum.step()
    grad_res1, package = call(
        first_norm_back_kernel,
        "first_norm_back",
        [*exchanged, residual1, gains[0], grad_res2, sums2],
        [flat, struct((own + 16, features), BF)],
    )
    attn_pieces = col_pieces(package)
    (package,) = call(
        functools.partial(prepare_kernel, heads, own),
        "prepare",
        [*attn_pieces, full_out, context, log_total],
        [struct((heads * (HEAD + AUX) + 32, group), BF)],
        flops=2 * width * features * group,
    )
    span = min(2 * group, total)
    steps_all = total // span
    grad_query = jnp.zeros((heads, HEAD, group), F32)
    if ring:
        package_ring = Rounds(package, 1)
        package_ring.step()
        grad_query = after(grad_query, sent)
        ffn_sum.step()
    grad_query = query_grad(own_q, package, keys, values, heads, span, 0, steps_all, grad_query)
    own_turn = pl.BlockSpec((HEAD, group), lambda i, s, *_: (0, s[0]))
    args = [*x_pieces, *attn_pieces, grad_query, turn, context_bf]
    specs = [whole(a.shape) for a in args]
    specs[-2] = own_turn
    mixed_q, early_grad = call(
        functools.partial(early_grad_kernel, heads, own, len(x_pieces)),
        "early_grad",
        args,
        [struct((width, group), BF), struct((features, 2 * width), BF)],
        prefetch=[own_slot],
        specs=specs,
        flops=4 * width * features * group,
    )

    def key_step(pieces, chunks, slot, sums):
        slots = jnp.where(jnp.arange(2) == 0, at(slot), own_slot)
        step = own if chunks == 2 else pieces[0].shape[1]
        *sums, norms = key_grad(
            pieces, chunks, step, slots, queries, keys, values, heads, group, tuple(sums)
        )
        return sums, norms

    norm_out = struct((4, features), F32)
    if ring:
        package_ring.step(early_grad)
        sums, norms = key_step([after(package, early_grad, package_ring.done[0])], 1, 6, ())
        norm_pieces = [norms]
        for i in range(3):
            sums, norms = key_step(package_ring.done[i], 2, i, sums)
            norm_pieces.append(norms)
            if i < 2:
                package_ring.step(norms)
        ffn_sum.moving = after(ffn_sum.moving, norms)
        sums, norms = key_step(package_ring.done[3], 1, 7, sums)
        norm_pieces.append(norms)
        (norm_sums,) = call(
            norm_total_kernel,
            "norm_total",
            norm_pieces,
            [norm_out],
            prefetch=[cycle_rows(place, (0, *ROUND_STEPS[:7]))],
            scratch=[pltpu.VMEM((rows, NORM_ROWS, NORM_LANES), F32)],
        )
    else:
        packages = lax.all_gather(package, "row", axis=0, tiled=False)

        def step(i, carried):
            sums, norms = carried
            piece = lax.dynamic_index_in_dim(packages, i, 0, keepdims=False)
            sums, more = key_step([piece], 1, i, sums)
            return tuple(sums), norms + more

        zeros = jnp.zeros((heads, HEAD, group), F32)
        sums, norms = lax.fori_loop(
            0, rows, step, ((zeros, zeros), jnp.zeros((1, NORM_ROWS, NORM_LANES), F32))
        )
        (norm_sums,) = call(
            norm_total_kernel,
            "norm_total",
            [norms],
            [norm_out],
            prefetch=[jnp.zeros((1,), jnp.int32)],
            scratch=[pltpu.VMEM((1, NORM_ROWS, NORM_LANES), F32)],
        )
    args = [*x_pieces, mixed_q, *sums, early_grad, turn, w_mix]
    specs = [whole(a.shape) for a in args]
    specs[-2] = own_turn
    outs = block_structs(features, 4 * width, ring)
    near, far, *blocks = call(
        functools.partial(late_grad_kernel, heads, len(x_pieces), len(outs)),
        "late_grad",
        args,
        [part, part, *outs],
        prefetch=[own_slot, block_starts],
        scratch=[pltpu.VMEM((features, 4 * width), BF), pltpu.VMEM((3 * width, group), BF)],
        specs=specs,
        flops=10 * width * features * group,
    )
    late_grad = RowSum(blocks).result()
    near, other, last = col_exchange(near, far)[0]
    ffn_grad = ffn_sum.result()
    grad_tokens = grad_res1 + (
        near[:own].astype(F32) + other[:own].astype(F32) + last.astype(F32)
    )
    grad_mix = jnp.concatenate([late_grad[:, :width], late_grad[:, 2 * width :]], axis=1)
    return (
        result,
        grad_tokens,
        grad_mix.reshape(share, 3, width),
        late_grad[:, width : 2 * width].T,
        ffn_grad[:, : 2 * units].reshape(share, 2, units),
        ffn_grad[:, 2 * units :].T,
        norm_sums[0],
        norm_sums[1],
        norm_sums[2],
        norm_sums[3],
    )


def solution(mesh):
    placed = (
        P(("row", "col"), None),
        P("row", None, "col"),
        P("col", "row"),
        P("row", None, "col"),
        P("col", "row"),
        P(),
        P(),
        P(),
        P(),
        P(("row", "col"), None),
        P(),
        P(),
    )
    return jax.shard_map(
        local,
        mesh=mesh,
        in_specs=placed,
        out_specs=(
            P(("row", "col"), None),
            P(("row", "col"), None),
            P("row", None, "col"),
            P("col", "row"),
            P("row", None, "col"),
            P("col", "row"),
            P(),
            P(),
            P(),
            P(),
        ),
        check_vma=False,
    )
```

profile of v0, /device:TPU:0, one launch (start us, length us, event | category | flops | bytes accessed | tf_op | source)
XLA Modules:
  0.0 222.7 jit_solution(7391414825487469585)
XLA Ops:
  4.1 3.0 %collective-permute-start = (bf16[224,768]{1,0:T(8,128)(2,1)S(1)}, bf16[224,768]{1,0:T(8,128)(2,1)S(1)}, u32[]{:S(2)}, u32[]{:S(2)}) collective-permute-start(bf16[224,768]{1,0:T(8,128)(2,1)S(1)} %fusion.6.refs_0_), channel_id=1, source_target_pairs={{0,8},{8,16},{16,24},{24,28},{28,20},{20,12},{12,4},{4,0},{1,9},{9... | collective-permute-start | bytes 1032200 | tf_op jit(solution)/shard_map/ppermute | solution.py:37
  7.1 2.0 collective-permute-start.16
  11.9 1.5 collective-permute-done.16
  13.5 1.6 collective-permute-done.refs_1_
  15.1 1.5 collective-permute-done.3.refs_2_
  17.7 1.6 collective-permute-start.12
  19.3 1.6 collective-permute-start.1
  21.3 1.9 multiply_cosine_fusion
  23.2 4.4 %collective-permute-done.1.refs_3_ = bf16[224,768]{1,0:T(8,128)(2,1)S(1)} collective-permute-done((bf16[224,768]{1,0:T(8,128)(2,1)S(1)}, bf16[224,768]{1,0:T(8,128)(2,1)S(1)}, u32[]{:S(2)}, u32[]{:S(2)}) %collective-permute-start.1) | collective-permute-done | bytes 344096 | tf_op jit(solution)/shard_map/ppermute | solution.py:37
  27.6 1.6 collective-permute-start.2
  30.4 5.3 %collective-permute-done.2.refs_5_ = bf16[224,768]{1,0:T(8,128)(2,1)S(1)} collective-permute-done((bf16[224,768]{1,0:T(8,128)(2,1)S(1)}, bf16[224,768]{1,0:T(8,128)(2,1)S(1)}, u32[]{:S(2)}, u32[]{:S(2)}) %collective-permute-start.2) | collective-permute-done | bytes 344096 | tf_op jit(solution)/shard_map/ppermute | solution.py:37
  35.8 1.6 collective-permute-start.10
  37.9 1.6 collective-permute-start.6
  40.8 2.3 %collective-permute-done.10.refs_7_ = bf16[112,768]{1,0:T(8,128)(2,1)S(1)} collective-permute-done((bf16[112,768]{1,0:T(8,128)(2,1)S(1)}, bf16[112,768]{1,0:T(8,128)(2,1)S(1)}, u32[]{:S(2)}, u32[]{:S(2)}) %collective-permute-start.10) | collective-permute-done | bytes 172064 | tf_op jit(solution)/shard_map/ppermute | solution.py:37
  43.1 1.7 collective-permute-done.11.refs_8_
  46.8 1.9 attend.5
  49.7 3.4 %attend.6 = (bf16[3,80,4096]{2,1,0:T(8,128)(2,1)S(1)}, bf16[3,80,4096]{2,1,0:T(8,128)(2,1)S(1)}, bf16[3,80,4096]{2,1,0:T(8,128)(2,1)S(1)}, f32[3,512]{1,0:T(4,12...) custom-call(s32[1]{0:T(128)} %constant.63.clone.1.slot, ...), custom_call_target="tpu_custom_call", output_to_operand_aliasing={{0}: (10, {}), {1}: (11, {}), {2}: (12, {})} | custom-call | flops 16106127 | bytes 335052 | tf_op jit(solution)/shard_map/attend/pallas_call | solution.py:147
  54.2 6.3 %collective-permute-done.15 = bf16[128,768]{1,0:T(8,128)(2,1)S(1)} collective-permute-done((bf16[128,768]{1,0:T(8,128)(2,1)S(1)}, bf16[128,768]{1,0:T(8,128)(2,1)S(1)}, u32[]{:S(2)}, u32[]{:S(2)}) %collective-permute-start.15) | collective-permute-done | bytes 196640 | tf_op jit(solution)/shard_map/ppermute | solution.py:47
  60.6 3.4 %attend.7 = (bf16[3,80,4096]{2,1,0:T(8,128)(2,1)S(1)}, bf16[3,80,4096]{2,1,0:T(8,128)(2,1)S(1)}, bf16[3,80,4096]{2,1,0:T(8,128)(2,1)S(1)}, f32[3,512]{1,0:T(4,12...) custom-call(s32[1]{0:T(128)} %constant.48.clone.1.slot, ...), custom_call_target="tpu_custom_call", output_to_operand_aliasing={{0}: (10, {}), {1}: (11, {}), {2}: (12, {})} | custom-call | flops 16106127 | bytes 335052 | tf_op jit(solution)/shard_map/attend/pallas_call | solution.py:147
  64.0 1.6 collective-permute-start.8
  66.3 3.4 %attend.8 = (bf16[3,80,4096]{2,1,0:T(8,128)(2,1)S(1)}, bf16[3,80,4096]{2,1,0:T(8,128)(2,1)S(1)}, bf16[3,80,4096]{2,1,0:T(8,128)(2,1)S(1)}, f32[3,512]{1,0:T(4,12...) custom-call(s32[1]{0:T(128)} %constant.64.clone.1.slot, ...), custom_call_target="tpu_custom_call", output_to_operand_aliasing={{0}: (10, {}), {1}: (11, {}), {2}: (12, {})} | custom-call | flops 16106127 | bytes 335052 | tf_op jit(solution)/shard_map/attend/pallas_call | solution.py:147
  69.7 2.5 %attend.9 = (bf16[3,80,4096]{2,1,0:T(8,128)(2,1)S(1)}, bf16[3,80,4096]{2,1,0:T(8,128)(2,1)S(1)}, bf16[3,80,4096]{2,1,0:T(8,128)(2,1)S(1)}, bf16[256,768]{1,0:T(8...) custom-call(s32[1]{0:T(128)} %constant.47.clone.1.slot, ...), custom_call_target="tpu_custom_call", output_to_operand_aliasing={{0}: (10, {}), {1}: (11, {}), {2}: (12, {})} | custom-call | flops 8053063 | bytes 344760 | tf_op jit(solution)/shard_map/attend/pallas_call | solution.py:147
  72.3 4.4 %collective-permute-done.8.refs_3_ = bf16[96,2304]{1,0:T(8,128)(2,1)S(1)} collective-permute-done((bf16[96,2304]{1,0:T(8,128)(2,1)S(1)}, bf16[96,2304]{1,0:T(8,128)(2,1)S(1)}, u32[]{:S(2)}, u32[]{:S(2)}) %collective-permute-start.8) | collective-permute-done | bytes 442400 | tf_op jit(solution)/shard_map/ppermute | solution.py:37
  76.6 1.5 collective-permute-done.9.refs_4_
  78.1 1.5 collective-permute-start.22
  80.8 5.1 %collective-permute-done.27.last = bf16[128,768]{1,0:T(8,128)(2,1)S(1)} collective-permute-done((bf16[128,768]{1,0:T(8,128)(2,1)S(1)}, bf16[128,768]{1,0:T(8,128)(2,1)S(1)}, u32[]{:S(2)}, u32[]{:S(2)}) %collective-permute-start.27) | collective-permute-done | bytes 196640 | tf_op jit(solution)/shard_map/ppermute | solution.py:47
  86.8 2.7 %collective-permute-done.22.refs_5_ = bf16[96,2304]{1,0:T(8,128)(2,1)S(1)} collective-permute-done((bf16[96,2304]{1,0:T(8,128)(2,1)S(1)}, bf16[96,2304]{1,0:T(8,128)(2,1)S(1)}, u32[]{:S(2)}, u32[]{:S(2)}) %collective-permute-start.22) | collective-permute-done | bytes 442400 | tf_op jit(solution)/shard_map/ppermute | solution.py:37
  89.5 1.6 collective-permute-start.24
  92.6 2.9 %collective-permute-done.24.refs_7_ = bf16[48,2304]{1,0:T(8,128)(2,1)S(1)} collective-permute-done((bf16[48,2304]{1,0:T(8,128)(2,1)S(1)}, bf16[48,2304]{1,0:T(8,128)(2,1)S(1)}, u32[]{:S(2)}, u32[]{:S(2)}) %collective-permute-start.24) | collective-permute-done | bytes 221216 | tf_op jit(solution)/shard_map/ppermute | solution.py:37
  95.5 2.0 collective-permute-done.25.refs_8_
  97.5 2.9 %ffn_forward.1 = (bf16[768,1536]{1,0:T(8,128)(2,1)S(1)}, bf16[768,768]{1,0:T(8,128)(2,1)S(1)}, f32[512,1536]{1,0:T(8,128)S(1)}, bf16[512,768]{1,0:T(8,128)(2,1)S...) custom-call(s32[9]{0:T(128)S(1)} %fusion.23.starts, bf16[96,2304]{1,0:T(8,128)(2,1)S(1)} %pad_maximum_fusion.1.refs_0_, ...), custom_call_target="tpu_custom_call" | custom-call | flops 36238784 | bytes 251658 | tf_op jit(solution)/shard_map/ffn_forward/pallas_call | solution.py:147
  100.5 1.7 collective-permute-done.31.other
  102.9 6.4 %collective-permute-done.32.last = bf16[128,768]{1,0:T(8,128)(2,1)S(1)} collective-permute-done((bf16[128,768]{1,0:T(8,128)(2,1)S(1)}, bf16[128,768]{1,0:T(8,128)(2,1)S(1)}, u32[]{:S(2)}, u32[]{:S(2)}) %collective-permute-start.32) | collective-permute-done | bytes 196640 | tf_op jit(solution)/shard_map/ppermute | solution.py:47
  111.0 5.6 %collective-permute-done.33.refs_1_.refs_5_ = bf16[128,768]{1,0:T(8,128)(2,1)S(1)} collective-permute-done((bf16[128,768]{1,0:T(8,128)(2,1)S(1)}, bf16[128,768]{1,0:T(8,128)(2,1)S(1)}, u32[]{:S(2)}, u32[]{:S(2)}) %collective-permute-start.33) | collective-permute-done | bytes 196640 | tf_op jit(solution)/shard_map/ppermute | solution.py:47
  116.6 1.4 collective-permute-done.35.refs_3_.refs_7_
  118.0 2.6 %ffn_backward.1 = (bf16[512,1536]{1,0:T(8,128)(2,1)S(1)}, bf16[256,768]{1,0:T(8,128)(2,1)S(1)}, bf16[256,768]{1,0:T(8,128)(2,1)S(1)}) custom-call(bf16[128,768]{1,0:T(8,128)(2,1)S(1)} %get-tuple-element.187.refs_0_.refs_4_, bf16[128,768]{1,0:T(8,128)(2,1)S(1)} %collective-permute-done.33.refs_1_.refs_5_, ...), custom_call_target="tpu_custom_call" | custom-call | flops 36238784 | bytes 196608 | tf_op jit(solution)/shard_map/ffn_backward/pallas_call | solution.py:147
  120.9 1.6 collective-permute-done.36.other
  123.0 2.8 %ffn_grad.1 = (bf16[96,2304]{1,0:T(8,128)(2,1)S(1)}, bf16[96,2304]{1,0:T(8,128)(2,1)S(1)}, bf16[96,2304]{1,0:T(8,128)(2,1)S(1)}, bf16[96,2304]{1,0:T(8,128)(2,1)...) custom-call(s32[9]{0:T(128)S(1)} %fusion.39.starts, ...), custom_call_target="tpu_custom_call" | custom-call | flops 36238784 | bytes 149422 | tf_op jit(solution)/shard_map/ffn_grad/pallas_call | solution.py:147
  126.5 1.5 collective-permute-start.41
  128.0 1.4 collective-permute-done.37.last
  130.5 2.7 %collective-permute-done.42 = bf16[48,2304]{1,0:T(8,128)(2,1)S(1)} collective-permute-done((bf16[48,2304]{1,0:T(8,128)(2,1)S(1)}, bf16[48,2304]{1,0:T(8,128)(2,1)S(1)}, u32[]{:S(2)}, u32[]{:S(2)}) %collective-permute-start.42) | collective-permute-done | bytes 221216 | tf_op jit(solution)/shard_map/ppermute | solution.py:42
  133.8 2.8 %collective-permute-done.38.refs_1_.refs_3_ = bf16[144,768]{1,0:T(8,128)(2,1)S(1)} collective-permute-done((bf16[144,768]{1,0:T(8,128)(2,1)S(1)}, bf16[144,768]{1,0:T(8,128)(2,1)S(1)}, u32[]{:S(2)}, u32[]{:S(2)}) %collective-permute-start.38) | collective-permute-done | bytes 221216 | tf_op jit(solution)/shard_map/ppermute | solution.py:47
  136.7 1.4 collective-permute-done.40.refs_3_.refs_5_
  139.2 1.4 collective-permute-start.44
  140.7 10.1 %query_grad.1.refs_6_ = f32[3,64,512]{2,1,0:T(8,128)S(1)} custom-call(bf16[3,80,512]{2,1,0:T(8,128)(2,1)S(1)} %get-tuple-element.148.refs_5_.q, bf16[272,512]{1,0:T(8,128)(2,1)S(1)} %prepare.1.g.refs_0_, bf16[3,80,4096]{2,1,0:T(8,128)(2,1)S(1)} %get-tuple-element.212.k.refs_2_.refs_3_, bf16[3,80,4096]{2,1,0:T(8,128)(2,1)S(1)} %get-tuple-element.213.v.refs_3_.refs_4_, ...), custom_call_target="tpu_custom_call" | custom-call | flops 96636768 | bytes 104857 | tf_op jit(solution)/shard_map/query_grad/pallas_call | solution.py:147
  152.4 1.4 collective-permute-start.46
  154.5 2.1 key_grad.5
  156.6 3.6 %key_grad.6 = (f32[3,64,512]{2,1,0:T(8,128)S(1)}, f32[3,64,512]{2,1,0:T(8,128)S(1)}, f32[2,24,256]{2,1,0:T(8,128)S(1)}) custom-call(s32[2]{0:T(128)S(1)} %fusion.48.slots, bf16[272,512]{1,0:T(8,128)(2,1)S(1)} %collective-permute-done.43.refs_0_, bf16[272,512]{1,0:T(8,128)(2,1)S(1)} %collective-permute-done.44.refs_1_, ...), custom_call_target="tpu_custom_call" | custom-call | flops 32212254 | bytes 161546 | tf_op jit(solution)/shard_map/key_grad/pallas_call | solution.py:147
  162.0 1.4 collective-permute-start.48
  163.5 3.6 %key_grad.7 = (f32[3,64,512]{2,1,0:T(8,128)S(1)}, f32[3,64,512]{2,1,0:T(8,128)S(1)}, f32[2,24,256]{2,1,0:T(8,128)S(1)}) custom-call(s32[2]{0:T(128)S(1)} %fusion.47.slots, bf16[272,512]{1,0:T(8,128)(2,1)S(1)} %collective-permute-done.45.refs_0_, bf16[272,512]{1,0:T(8,128)(2,1)S(1)} %collective-permute-done.46.refs_1_, ...), custom_call_target="tpu_custom_call" | custom-call | flops 32212254 | bytes 161546 | tf_op jit(solution)/shard_map/key_grad/pallas_call | solution.py:147
  167.1 8.3 %collective-permute-done.47.refs_0_ = bf16[272,512]{1,0:T(8,128)(2,1)S(1)} collective-permute-done((bf16[272,512]{1,0:T(8,128)(2,1)S(1)}, bf16[272,512]{1,0:T(8,128)(2,1)S(1)}, u32[]{:S(2)}, u32[]{:S(2)}) %collective-permute-start.47) | collective-permute-done | bytes 278560 | tf_op jit(solution)/shard_map/ppermute | solution.py:37
  176.1 1.5 collective-permute-start.50
  177.7 3.6 %key_grad.8 = (f32[3,64,512]{2,1,0:T(8,128)S(1)}, f32[3,64,512]{2,1,0:T(8,128)S(1)}, f32[2,24,256]{2,1,0:T(8,128)S(1)}) custom-call(s32[2]{0:T(128)S(1)} %fusion.46.slots, bf16[272,512]{1,0:T(8,128)(2,1)S(1)} %collective-permute-done.47.refs_0_, bf16[272,512]{1,0:T(8,128)(2,1)S(1)} %collective-permute-done.48.refs_1_, ...), custom_call_target="tpu_custom_call" | custom-call | flops 32212254 | bytes 161546 | tf_op jit(solution)/shard_map/key_grad/pallas_call | solution.py:147
  182.0 1.6 collective-permute-start.65
  183.6 2.1 key_grad.9
  185.7 1.9 late_grad.1
  188.3 1.4 collective-permute-start.57
  190.9 2.2 collective-permute-done.53
  193.9 1.5 collective-permute-start.58
  195.3 3.1 %collective-permute-done.54 = bf16[96,768]{1,0:T(8,128)(2,1)S(1)} collective-permute-done((bf16[96,768]{1,0:T(8,128)(2,1)S(1)}, bf16[96,768]{1,0:T(8,128)(2,1)S(1)}, u32[]{:S(2)}, u32[]{:S(2)}) %collective-permute-start.54) | collective-permute-done | bytes 147488 | tf_op jit(solution)/shard_map/ppermute | solution.py:37
  203.0 2.3 %collective-permute-done.55 = bf16[96,768]{1,0:T(8,128)(2,1)S(1)} collective-permute-done((bf16[96,768]{1,0:T(8,128)(2,1)S(1)}, bf16[96,768]{1,0:T(8,128)(2,1)S(1)}, u32[]{:S(2)}, u32[]{:S(2)}) %collective-permute-start.55) | collective-permute-done | bytes 147488 | tf_op jit(solution)/shard_map/ppermute | solution.py:37
  208.9 5.5 %collective-permute-done.56 = bf16[96,768]{1,0:T(8,128)(2,1)S(1)} collective-permute-done((bf16[96,768]{1,0:T(8,128)(2,1)S(1)}, bf16[96,768]{1,0:T(8,128)(2,1)S(1)}, u32[]{:S(2)}, u32[]{:S(2)}) %collective-permute-start.56) | collective-permute-done | bytes 147488 | tf_op jit(solution)/shard_map/ppermute | solution.py:37
  216.8 1.6 copy.56
  218.5 1.8 add_add_fusion
  (227 shorter events, 44.9 us)
Async XLA Ops:
  4.1 11.0 %collective-permute-start = (bf16[224,768]{1,0:T(8,128)(2,1)S(1)}, bf16[224,768]{1,0:T(8,128)(2,1)S(1)}, u32[]{:S(2)}, u32[]{:S(2)}) collective-permute-start(bf16[224,768]{1,0:T(8,128)(2,1)S(1)} %fusion.6.refs_0_), channel_id=1, source_target_pairs={{0,8},{8,16},{16,24},{24,28},{28,20},{20,12},{12,4},{4,0},{1,9},{9... | collective-permute-start | bytes 1032200 | tf_op jit(solution)/shard_map/ppermute | solution.py:37
  7.1 9.5 %collective-permute-start.3 = (bf16[224,768]{1,0:T(8,128)(2,1)S(1)}, bf16[224,768]{1,0:T(8,128)(2,1)S(1)}, u32[]{:S(2)}, u32[]{:S(2)}) collective-permute-start(bf16[224,768]{1,0:T(8,128)(2,1)S(1)} %fusion.6.refs_0_), channel_id=1, source_target_pairs={{8,0},{16,8},{24,16},{28,24},{20,28},{12,20},{4,12},{0,4},{9,1},{1... | collective-permute-start | bytes 1032200 | tf_op jit(solution)/shard_map/ppermute | solution.py:42
  7.1 6.4 %collective-permute-start.16 = (bf16[128,768]{1,0:T(8,128)(2,1)S(1)}, bf16[128,768]{1,0:T(8,128)(2,1)S(1)}, u32[]{:S(2)}, u32[]{:S(2)}) collective-permute-start(bf16[128,768]{1,0:T(8,128)(2,1)S(1)} %copy-done), channel_id=1, source_target_pairs={{0,2},{1,3},{2,0},{3,1},{4,6},{5,7},{6,4},{7,5},{8,10},{9,11},{10,... | collective-permute-start | bytes 589832 | tf_op jit(solution)/shard_map/ppermute | solution.py:47
  17.7 12.0 %collective-permute-start.12 = (bf16[256,768]{1,0:T(8,128)(2,1)S(1)}, bf16[256,768]{1,0:T(8,128)(2,1)S(1)}, u32[]{:S(2)}, u32[]{:S(2)}) collective-permute-start(bf16[256,768]{1,0:T(8,128)(2,1)S(1)} %pad_maximum_fusion.4), channel_id=1, source_target_pairs={{0,2},{1,3},{2,0},{3,1},{4,6},{5,7},{6,4},{7,5},{8,10},{9,11},{10,... | collective-permute-start | bytes 1179656 | tf_op jit(solution)/shard_map/ppermute | solution.py:47
  19.3 8.3 %collective-permute-start.1 = (bf16[224,768]{1,0:T(8,128)(2,1)S(1)}, bf16[224,768]{1,0:T(8,128)(2,1)S(1)}, u32[]{:S(2)}, u32[]{:S(2)}) collective-permute-start(bf16[224,768]{1,0:T(8,128)(2,1)S(1)} %collective-permute-done.refs_1_), channel_id=1, source_target_pairs={{0,8},{8,16},{16,24},{24,28},{28,20},{20,12},{12,4},{4,0},{1,9},{9... | collective-permute-start | bytes 1032200 | tf_op jit(solution)/shard_map/ppermute | solution.py:37
  20.8 8.3 %collective-permute-start.4 = (bf16[224,768]{1,0:T(8,128)(2,1)S(1)}, bf16[224,768]{1,0:T(8,128)(2,1)S(1)}, u32[]{:S(2)}, u32[]{:S(2)}) collective-permute-start(bf16[224,768]{1,0:T(8,128)(2,1)S(1)} %collective-permute-done.3.refs_2_), channel_id=1, source_target_pairs={{8,0},{16,8},{24,16},{28,24},{20,28},{12,20},{4,12},{0,4},{9,1},{1... | collective-permute-start | bytes 1032200 | tf_op jit(solution)/shard_map/ppermute | solution.py:42
  27.6 8.2 %collective-permute-start.2 = (bf16[224,768]{1,0:T(8,128)(2,1)S(1)}, bf16[224,768]{1,0:T(8,128)(2,1)S(1)}, u32[]{:S(2)}, u32[]{:S(2)}) collective-permute-start(bf16[224,768]{1,0:T(8,128)(2,1)S(1)} %collective-permute-done.1.refs_3_), channel_id=1, source_target_pairs={{0,8},{8,16},{16,24},{24,28},{28,20},{20,12},{12,4},{4,0},{1,9},{9... | collective-permute-start | bytes 1032200 | tf_op jit(solution)/shard_map/ppermute | solution.py:37
  29.2 8.2 %collective-permute-start.5 = (bf16[224,768]{1,0:T(8,128)(2,1)S(1)}, bf16[224,768]{1,0:T(8,128)(2,1)S(1)}, u32[]{:S(2)}, u32[]{:S(2)}) collective-permute-start(bf16[224,768]{1,0:T(8,128)(2,1)S(1)} %collective-permute-done.4.refs_4_), channel_id=1, source_target_pairs={{8,0},{16,8},{24,16},{28,24},{20,28},{12,20},{4,12},{0,4},{9,1},{1... | collective-permute-start | bytes 1032200 | tf_op jit(solution)/shard_map/ppermute | solution.py:42
  29.8 10.3 %collective-permute-start.13 = (bf16[256,768]{1,0:T(8,128)(2,1)S(1)}, bf16[256,768]{1,0:T(8,128)(2,1)S(1)}, u32[]{:S(2)}, u32[]{:S(2)}) collective-permute-start(bf16[256,768]{1,0:T(8,128)(2,1)S(1)} %pad_maximum_fusion.5), channel_id=1, source_target_pairs={{0,2},{1,3},{2,0},{3,1},{4,6},{5,7},{6,4},{7,5},{8,10},{9,11},{10,... | collective-permute-start | bytes 1179656 | tf_op jit(solution)/shard_map/ppermute | solution.py:47
  35.8 7.4 %collective-permute-start.10 = (bf16[112,768]{1,0:T(8,128)(2,1)S(1)}, bf16[112,768]{1,0:T(8,128)(2,1)S(1)}, u32[]{:S(2)}, u32[]{:S(2)}) collective-permute-start(bf16[112,768]{1,0:T(8,128)(2,1)S(1)} %slice.218), channel_id=1, source_target_pairs={{0,8},{8,16},{16,24},{24,28},{28,20},{20,12},{12,4},{4,0},{1,9},{9... | collective-permute-start | bytes 516104 | tf_op jit(solution)/shard_map/ppermute | solution.py:37
  37.4 7.4 %collective-permute-start.11 = (bf16[112,768]{1,0:T(8,128)(2,1)S(1)}, bf16[112,768]{1,0:T(8,128)(2,1)S(1)}, u32[]{:S(2)}, u32[]{:S(2)}) collective-permute-start(bf16[112,768]{1,0:T(8,128)(2,1)S(1)} %slice.219), channel_id=1, source_target_pairs={{8,0},{16,8},{24,16},{28,24},{20,28},{12,20},{4,12},{0,4},{9,1},{1... | collective-permute-start | bytes 516104 | tf_op jit(solution)/shard_map/ppermute | solution.py:42
  37.9 10.8 %collective-permute-start.6 = (bf16[96,2304]{1,0:T(8,128)(2,1)S(1)}, bf16[96,2304]{1,0:T(8,128)(2,1)S(1)}, u32[]{:S(2)}, u32[]{:S(2)}) collective-permute-start(bf16[96,2304]{1,0:T(8,128)(2,1)S(1)} %pad_maximum_fusion.1.refs_0_), channel_id=1, source_target_pairs={{0,8},{8,16},{16,24},{24,28},{28,20},{20,12},{12,4},{4,0},{1,9},{9... | collective-permute-start | bytes 1327112 | tf_op jit(solution)/shard_map/ppermute | solution.py:37
  39.5 10.1 %collective-permute-start.7 = (bf16[96,2304]{1,0:T(8,128)(2,1)S(1)}, bf16[96,2304]{1,0:T(8,128)(2,1)S(1)}, u32[]{:S(2)}, u32[]{:S(2)}) collective-permute-start(bf16[96,2304]{1,0:T(8,128)(2,1)S(1)} %pad_maximum_fusion.1.refs_0_), channel_id=1, source_target_pairs={{8,0},{16,8},{24,16},{28,24},{20,28},{12,20},{4,12},{0,4},{9,1},{1... | collective-permute-start | bytes 1327112 | tf_op jit(solution)/shard_map/ppermute | solution.py:42
  40.2 9.4 %collective-permute-start.14 = (bf16[256,768]{1,0:T(8,128)(2,1)S(1)}, bf16[256,768]{1,0:T(8,128)(2,1)S(1)}, u32[]{:S(2)}, u32[]{:S(2)}) collective-permute-start(bf16[256,768]{1,0:T(8,128)(2,1)S(1)} %pad_maximum_fusion.6), channel_id=1, source_target_pairs={{0,2},{1,3},{2,0},{3,1},{4,6},{5,7},{6,4},{7,5},{8,10},{9,11},{10,... | collective-permute-start | bytes 1179656 | tf_op jit(solution)/shard_map/ppermute | solution.py:47
  44.8 2.0 collective-permute-start.17
  44.8 4.9 %collective-permute-start.19 = (bf16[512,768]{1,0:T(8,128)(2,1)S(1)}, bf16[512,768]{1,0:T(8,128)(2,1)S(1)}, u32[]{:S(2)}, u32[]{:S(2)}) collective-permute-start(bf16[512,768]{1,0:T(8,128)(2,1)S(1)} %constant_dynamic-update-slice_fusion.refs_0_), channel_id=1, source_target_pairs={{0,1},{1,0},{2,3},{3,2},{4,5},{5,4},{6,7},{7,6},{8,9},{9,8},{10,11... | collective-permute-start | bytes 2359304 | tf_op jit(solution)/shard_map/ppermute | solution.py:47
  49.6 11.0 %collective-permute-start.18 = (bf16[512,768]{1,0:T(8,128)(2,1)S(1)}, bf16[512,768]{1,0:T(8,128)(2,1)S(1)}, u32[]{:S(2)}, u32[]{:S(2)}) collective-permute-start(bf16[512,768]{1,0:T(8,128)(2,1)S(1)} %constant_dynamic-update-slice_fusion.5.refs_0_), channel_id=1, source_target_pairs={{0,1},{1,0},{2,3},{3,2},{4,5},{5,4},{6,7},{7,6},{8,9},{9,8},{10,11... | collective-permute-start | bytes 2359304 | tf_op jit(solution)/shard_map/ppermute | solution.py:47
  53.1 13.2 %collective-permute-start.21 = (bf16[512,768]{1,0:T(8,128)(2,1)S(1)}, bf16[512,768]{1,0:T(8,128)(2,1)S(1)}, u32[]{:S(2)}, u32[]{:S(2)}) collective-permute-start(bf16[512,768]{1,0:T(8,128)(2,1)S(1)} %constant_dynamic-update-slice_fusion.10.refs_0_), channel_id=1, source_target_pairs={{0,1},{1,0},{2,3},{3,2},{4,5},{5,4},{6,7},{7,6},{8,9},{9,8},{10,11... | collective-permute-start | bytes 2359304 | tf_op jit(solution)/shard_map/ppermute | solution.py:47
  53.7 6.9 %collective-permute-start.15 = (bf16[128,768]{1,0:T(8,128)(2,1)S(1)}, bf16[128,768]{1,0:T(8,128)(2,1)S(1)}, u32[]{:S(2)}, u32[]{:S(2)}) collective-permute-start(bf16[128,768]{1,0:T(8,128)(2,1)S(1)} %pad_maximum_fusion.10), channel_id=1, source_target_pairs={{0,2},{1,3},{2,0},{3,1},{4,6},{5,7},{6,4},{7,5},{8,10},{9,11},{10,... | collective-permute-start | bytes 589832 | tf_op jit(solution)/shard_map/ppermute | solution.py:47
  64.0 5.7 %collective-permute-start.20 = (bf16[256,768]{1,0:T(8,128)(2,1)S(1)}, bf16[256,768]{1,0:T(8,128)(2,1)S(1)}, u32[]{:S(2)}, u32[]{:S(2)}) collective-permute-start(bf16[256,768]{1,0:T(8,128)(2,1)S(1)} %pad_maximum_fusion.7.refs_0_), channel_id=1, source_target_pairs={{0,1},{1,0},{2,3},{3,2},{4,5},{5,4},{6,7},{7,6},{8,9},{9,8},{10,11... | collective-permute-start | bytes 1179656 | tf_op jit(solution)/shard_map/ppermute | solution.py:47
  64.0 12.6 %collective-permute-start.8 = (bf16[96,2304]{1,0:T(8,128)(2,1)S(1)}, bf16[96,2304]{1,0:T(8,128)(2,1)S(1)}, u32[]{:S(2)}, u32[]{:S(2)}) collective-permute-start(bf16[96,2304]{1,0:T(8,128)(2,1)S(1)} %collective-permute-done.6.refs_1_), channel_id=1, source_target_pairs={{0,8},{8,16},{16,24},{24,28},{28,20},{20,12},{12,4},{4,0},{1,9},{9... | collective-permute-start | bytes 1327112 | tf_op jit(solution)/shard_map/ppermute | solution.py:37
  65.7 12.4 %collective-permute-start.9 = (bf16[96,2304]{1,0:T(8,128)(2,1)S(1)}, bf16[96,2304]{1,0:T(8,128)(2,1)S(1)}, u32[]{:S(2)}, u32[]{:S(2)}) collective-permute-start(bf16[96,2304]{1,0:T(8,128)(2,1)S(1)} %collective-permute-done.7.refs_2_), channel_id=1, source_target_pairs={{8,0},{16,8},{24,16},{28,24},{20,28},{12,20},{4,12},{0,4},{9,1},{1... | collective-permute-start | bytes 1327112 | tf_op jit(solution)/shard_map/ppermute | solution.py:42
  72.2 7.9 %collective-permute-start.26 = (bf16[256,768]{1,0:T(8,128)(2,1)S(1)}, bf16[256,768]{1,0:T(8,128)(2,1)S(1)}, u32[]{:S(2)}, u32[]{:S(2)}) collective-permute-start(bf16[256,768]{1,0:T(8,128)(2,1)S(1)} %get-tuple-element.180), channel_id=1, source_target_pairs={{0,1},{1,0},{2,3},{3,2},{4,5},{5,4},{6,7},{7,6},{8,9},{9,8},{10,11... | collective-permute-start | bytes 1179656 | tf_op jit(solution)/shard_map/ppermute | solution.py:47
  78.1 11.4 %collective-permute-start.22 = (bf16[96,2304]{1,0:T(8,128)(2,1)S(1)}, bf16[96,2304]{1,0:T(8,128)(2,1)S(1)}, u32[]{:S(2)}, u32[]{:S(2)}) collective-permute-start(bf16[96,2304]{1,0:T(8,128)(2,1)S(1)} %collective-permute-done.8.refs_3_), channel_id=1, source_target_pairs={{0,8},{8,16},{16,24},{24,28},{28,20},{20,12},{12,4},{4,0},{1,9},{9... | collective-permute-start | bytes 1327112 | tf_op jit(solution)/shard_map/ppermute | solution.py:37
  79.6 11.5 %collective-permute-start.23 = (bf16[96,2304]{1,0:T(8,128)(2,1)S(1)}, bf16[96,2304]{1,0:T(8,128)(2,1)S(1)}, u32[]{:S(2)}, u32[]{:S(2)}) collective-permute-start(bf16[96,2304]{1,0:T(8,128)(2,1)S(1)} %collective-permute-done.9.refs_4_), channel_id=1, source_target_pairs={{8,0},{16,8},{24,16},{28,24},{20,28},{12,20},{4,12},{0,4},{9,1},{1... | collective-permute-start | bytes 1327112 | tf_op jit(solution)/shard_map/ppermute | solution.py:42
  80.2 5.7 %collective-permute-start.27 = (bf16[128,768]{1,0:T(8,128)(2,1)S(1)}, bf16[128,768]{1,0:T(8,128)(2,1)S(1)}, u32[]{:S(2)}, u32[]{:S(2)}) collective-permute-start(bf16[128,768]{1,0:T(8,128)(2,1)S(1)} %add_convert_fusion.9), channel_id=1, source_target_pairs={{0,2},{1,3},{2,0},{3,1},{4,6},{5,7},{6,4},{7,5},{8,10},{9,11},{10,... | collective-permute-start | bytes 589832 | tf_op jit(solution)/shard_map/ppermute | solution.py:47
  86.2 5.9 %collective-permute-start.28 = (bf16[128,768]{1,0:T(8,128)(2,1)S(1)}, bf16[128,768]{1,0:T(8,128)(2,1)S(1)}, u32[]{:S(2)}, u32[]{:S(2)}) collective-permute-start(bf16[128,768]{1,0:T(8,128)(2,1)S(1)} %get-tuple-element.181.refs_9_.refs_0_), channel_id=1, source_target_pairs={{0,2},{1,3},{2,0},{3,1},{4,6},{5,7},{6,4},{7,5},{8,10},{9,11},{10,... | collective-permute-start | bytes 589832 | tf_op jit(solution)/shard_map/ppermute | solution.py:47
  89.5 6.0 %collective-permute-start.24 = (bf16[48,2304]{1,0:T(8,128)(2,1)S(1)}, bf16[48,2304]{1,0:T(8,128)(2,1)S(1)}, u32[]{:S(2)}, u32[]{:S(2)}) collective-permute-start(bf16[48,2304]{1,0:T(8,128)(2,1)S(1)} %slice.224), channel_id=1, source_target_pairs={{0,8},{8,16},{16,24},{24,28},{28,20},{20,12},{12,4},{4,0},{1,9},{9... | collective-permute-start | bytes 663560 | tf_op jit(solution)/shard_map/ppermute | solution.py:37
  91.1 6.4 %collective-permute-start.25 = (bf16[48,2304]{1,0:T(8,128)(2,1)S(1)}, bf16[48,2304]{1,0:T(8,128)(2,1)S(1)}, u32[]{:S(2)}, u32[]{:S(2)}) collective-permute-start(bf16[48,2304]{1,0:T(8,128)(2,1)S(1)} %slice.225), channel_id=1, source_target_pairs={{8,0},{16,8},{24,16},{28,24},{20,28},{12,20},{4,12},{0,4},{9,1},{1... | collective-permute-start | bytes 663560 | tf_op jit(solution)/shard_map/ppermute | solution.py:42
  92.1 5.4 %collective-permute-start.29 = (bf16[128,768]{1,0:T(8,128)(2,1)S(1)}, bf16[128,768]{1,0:T(8,128)(2,1)S(1)}, u32[]{:S(2)}, u32[]{:S(2)}) collective-permute-start(bf16[128,768]{1,0:T(8,128)(2,1)S(1)} %get-tuple-element.181.refs_9_.refs_0_), channel_id=1, source_target_pairs={{0,1},{1,0},{2,3},{3,2},{4,5},{5,4},{6,7},{7,6},{8,9},{9,8},{10,11... | collective-permute-start | bytes 589832 | tf_op jit(solution)/shard_map/ppermute | solution.py:47
  92.1 5.4 %collective-permute-start.30 = (bf16[128,768]{1,0:T(8,128)(2,1)S(1)}, bf16[128,768]{1,0:T(8,128)(2,1)S(1)}, u32[]{:S(2)}, u32[]{:S(2)}) collective-permute-start(bf16[128,768]{1,0:T(8,128)(2,1)S(1)} %collective-permute-done.28.refs_10_.refs_1_), channel_id=1, source_target_pairs={{0,1},{1,0},{2,3},{3,2},{4,5},{5,4},{6,7},{7,6},{8,9},{9,8},{10,11... | collective-permute-start | bytes 589832 | tf_op jit(solution)/shard_map/ppermute | solution.py:47
  100.5 1.8 collective-permute-start.31
  102.3 7.0 %collective-permute-start.32 = (bf16[128,768]{1,0:T(8,128)(2,1)S(1)}, bf16[128,768]{1,0:T(8,128)(2,1)S(1)}, u32[]{:S(2)}, u32[]{:S(2)}) collective-permute-start(bf16[128,768]{1,0:T(8,128)(2,1)S(1)} %add_convert_fusion.8), channel_id=1, source_target_pairs={{0,2},{1,3},{2,0},{3,1},{4,6},{5,7},{6,4},{7,5},{8,10},{9,11},{10,... | collective-permute-start | bytes 589832 | tf_op jit(solution)/shard_map/ppermute | solution.py:47
  110.5 6.1 %collective-permute-start.33 = (bf16[128,768]{1,0:T(8,128)(2,1)S(1)}, bf16[128,768]{1,0:T(8,128)(2,1)S(1)}, u32[]{:S(2)}, u32[]{:S(2)}) collective-permute-start(bf16[128,768]{1,0:T(8,128)(2,1)S(1)} %get-tuple-element.187.refs_0_.refs_4_), channel_id=1, source_target_pairs={{0,2},{1,3},{2,0},{3,1},{4,6},{5,7},{6,4},{7,5},{8,10},{9,11},{10,... | collective-permute-start | bytes 589832 | tf_op jit(solution)/shard_map/ppermute | solution.py:47
  111.0 5.6 %collective-permute-start.34 = (bf16[128,768]{1,0:T(8,128)(2,1)S(1)}, bf16[128,768]{1,0:T(8,128)(2,1)S(1)}, u32[]{:S(2)}, u32[]{:S(2)}) collective-permute-start(bf16[128,768]{1,0:T(8,128)(2,1)S(1)} %get-tuple-element.187.refs_0_.refs_4_), channel_id=1, source_target_pairs={{0,1},{1,0},{2,3},{3,2},{4,5},{5,4},{6,7},{7,6},{8,9},{9,8},{10,11... | collective-permute-start | bytes 589832 | tf_op jit(solution)/shard_map/ppermute | solution.py:47
  122.5 7.0 %collective-permute-start.37 = (bf16[128,768]{1,0:T(8,128)(2,1)S(1)}, bf16[128,768]{1,0:T(8,128)(2,1)S(1)}, u32[]{:S(2)}, u32[]{:S(2)}) collective-permute-start(bf16[128,768]{1,0:T(8,128)(2,1)S(1)} %add_convert_fusion.7), channel_id=1, source_target_pairs={{0,2},{1,3},{2,0},{3,1},{4,6},{5,7},{6,4},{7,5},{8,10},{9,11},{10,... | collective-permute-start | bytes 589832 | tf_op jit(solution)/shard_map/ppermute | solution.py:47
  125.9 7.2 %collective-permute-start.42 = (bf16[48,2304]{1,0:T(8,128)(2,1)S(1)}, bf16[48,2304]{1,0:T(8,128)(2,1)S(1)}, u32[]{:S(2)}, u32[]{:S(2)}) collective-permute-start(bf16[48,2304]{1,0:T(8,128)(2,1)S(1)} %get-tuple-element.201), channel_id=1, source_target_pairs={{8,0},{16,8},{24,16},{28,24},{20,28},{12,20},{4,12},{0,4},{9,1},{1... | collective-permute-start | bytes 663560 | tf_op jit(solution)/shard_map/ppermute | solution.py:42
  126.5 10.1 %collective-permute-start.41 = (bf16[48,2304]{1,0:T(8,128)(2,1)S(1)}, bf16[48,2304]{1,0:T(8,128)(2,1)S(1)}, u32[]{:S(2)}, u32[]{:S(2)}) collective-permute-start(bf16[48,2304]{1,0:T(8,128)(2,1)S(1)} %get-tuple-element.200), channel_id=1, source_target_pairs={{0,8},{8,16},{16,24},{24,28},{28,20},{20,12},{12,4},{4,0},{1,9},{9... | collective-permute-start | bytes 663560 | tf_op jit(solution)/shard_map/ppermute | solution.py:37
  129.9 6.7 %collective-permute-start.38 = (bf16[144,768]{1,0:T(8,128)(2,1)S(1)}, bf16[144,768]{1,0:T(8,128)(2,1)S(1)}, u32[]{:S(2)}, u32[]{:S(2)}) collective-permute-start(bf16[144,768]{1,0:T(8,128)(2,1)S(1)} %get-tuple-element.209.refs_0_.refs_2_), channel_id=1, source_target_pairs={{0,2},{1,3},{2,0},{3,1},{4,6},{5,7},{6,4},{7,5},{8,10},{9,11},{10,... | collective-permute-start | bytes 663560 | tf_op jit(solution)/shard_map/ppermute | solution.py:47
  130.4 6.2 %collective-permute-start.39 = (bf16[144,768]{1,0:T(8,128)(2,1)S(1)}, bf16[144,768]{1,0:T(8,128)(2,1)S(1)}, u32[]{:S(2)}, u32[]{:S(2)}) collective-permute-start(bf16[144,768]{1,0:T(8,128)(2,1)S(1)} %get-tuple-element.209.refs_0_.refs_2_), channel_id=1, source_target_pairs={{0,1},{1,0},{2,3},{3,2},{4,5},{5,4},{6,7},{7,6},{8,9},{9,8},{10,11... | collective-permute-start | bytes 663560 | tf_op jit(solution)/shard_map/ppermute | solution.py:47
  133.2 30.2 %collective-permute-start.62 = (bf16[96,2304]{1,0:T(8,128)(2,1)S(1)}, bf16[96,2304]{1,0:T(8,128)(2,1)S(1)}, u32[]{:S(2)}, u32[]{:S(2)}) collective-permute-start(bf16[96,2304]{1,0:T(8,128)(2,1)S(1)} %pad_maximum_fusion.3), channel_id=1, source_target_pairs={{8,0},{16,8},{24,16},{28,24},{20,28},{12,20},{4,12},{0,4},{9,1},{1... | collective-permute-start | bytes 1327112 | tf_op jit(solution)/shard_map/ppermute | solution.py:42
  138.5 13.0 %collective-permute-start.43 = (bf16[272,512]{1,0:T(8,128)(2,1)S(1)}, bf16[272,512]{1,0:T(8,128)(2,1)S(1)}, u32[]{:S(2)}, u32[]{:S(2)}) collective-permute-start(bf16[272,512]{1,0:T(8,128)(2,1)S(1)} %prepare.1.g.refs_0_), channel_id=1, source_target_pairs={{0,8},{8,16},{16,24},{24,28},{28,20},{20,12},{12,4},{4,0},{1,9},{9... | collective-permute-start | bytes 835592 | tf_op jit(solution)/shard_map/ppermute | solution.py:37
  139.2 12.3 %collective-permute-start.44 = (bf16[272,512]{1,0:T(8,128)(2,1)S(1)}, bf16[272,512]{1,0:T(8,128)(2,1)S(1)}, u32[]{:S(2)}, u32[]{:S(2)}) collective-permute-start(bf16[272,512]{1,0:T(8,128)(2,1)S(1)} %prepare.1.g.refs_0_), channel_id=1, source_target_pairs={{8,0},{16,8},{24,16},{28,24},{20,28},{12,20},{4,12},{0,4},{9,1},{1... | collective-permute-start | bytes 835592 | tf_op jit(solution)/shard_map/ppermute | solution.py:42
  151.6 9.8 %collective-permute-start.45 = (bf16[272,512]{1,0:T(8,128)(2,1)S(1)}, bf16[272,512]{1,0:T(8,128)(2,1)S(1)}, u32[]{:S(2)}, u32[]{:S(2)}) collective-permute-start(bf16[272,512]{1,0:T(8,128)(2,1)S(1)} %collective-permute-done.43.refs_0_), channel_id=1, source_target_pairs={{0,8},{8,16},{16,24},{24,28},{28,20},{20,12},{12,4},{4,0},{1,9},{9... | collective-permute-start | bytes 835592 | tf_op jit(solution)/shard_map/ppermute | solution.py:37
  152.4 9.0 %collective-permute-start.46 = (bf16[272,512]{1,0:T(8,128)(2,1)S(1)}, bf16[272,512]{1,0:T(8,128)(2,1)S(1)}, u32[]{:S(2)}, u32[]{:S(2)}) collective-permute-start(bf16[272,512]{1,0:T(8,128)(2,1)S(1)} %collective-permute-done.44.refs_1_), channel_id=1, source_target_pairs={{8,0},{16,8},{24,16},{28,24},{20,28},{12,20},{4,12},{0,4},{9,1},{1... | collective-permute-start | bytes 835592 | tf_op jit(solution)/shard_map/ppermute | solution.py:42
  153.8 23.7 %collective-permute-start.61 = (bf16[96,2304]{1,0:T(8,128)(2,1)S(1)}, bf16[96,2304]{1,0:T(8,128)(2,1)S(1)}, u32[]{:S(2)}, u32[]{:S(2)}) collective-permute-start(bf16[96,2304]{1,0:T(8,128)(2,1)S(1)} %pad_maximum_fusion.2), channel_id=1, source_target_pairs={{0,8},{8,16},{16,24},{24,28},{28,20},{20,12},{12,4},{4,0},{1,9},{9... | collective-permute-start | bytes 1327112 | tf_op jit(solution)/shard_map/ppermute | solution.py:37
  161.4 14.0 %collective-permute-start.47 = (bf16[272,512]{1,0:T(8,128)(2,1)S(1)}, bf16[272,512]{1,0:T(8,128)(2,1)S(1)}, u32[]{:S(2)}, u32[]{:S(2)}) collective-permute-start(bf16[272,512]{1,0:T(8,128)(2,1)S(1)} %collective-permute-done.45.refs_0_), channel_id=1, source_target_pairs={{0,8},{8,16},{16,24},{24,28},{28,20},{20,12},{12,4},{4,0},{1,9},{9... | collective-permute-start | bytes 835592 | tf_op jit(solution)/shard_map/ppermute | solution.py:37
  162.0 13.4 %collective-permute-start.48 = (bf16[272,512]{1,0:T(8,128)(2,1)S(1)}, bf16[272,512]{1,0:T(8,128)(2,1)S(1)}, u32[]{:S(2)}, u32[]{:S(2)}) collective-permute-start(bf16[272,512]{1,0:T(8,128)(2,1)S(1)} %collective-permute-done.46.refs_1_), channel_id=1, source_target_pairs={{8,0},{16,8},{24,16},{28,24},{20,28},{12,20},{4,12},{0,4},{9,1},{1... | collective-permute-start | bytes 835592 | tf_op jit(solution)/shard_map/ppermute | solution.py:42
  175.4 8.1 %collective-permute-start.49 = (bf16[272,256]{1,0:T(8,128)(2,1)S(1)}, bf16[272,256]{1,0:T(8,128)(2,1)S(1)}, u32[]{:S(2)}, u32[]{:S(2)}) collective-permute-start(bf16[272,256]{1,0:T(8,128)(2,1)S(1)} %slice.197), channel_id=1, source_target_pairs={{0,8},{8,16},{16,24},{24,28},{28,20},{20,12},{12,4},{4,0},{1,9},{9... | collective-permute-start | bytes 417800 | tf_op jit(solution)/shard_map/ppermute | solution.py:37
  176.1 7.4 %collective-permute-start.50 = (bf16[272,256]{1,0:T(8,128)(2,1)S(1)}, bf16[272,256]{1,0:T(8,128)(2,1)S(1)}, u32[]{:S(2)}, u32[]{:S(2)}) collective-permute-start(bf16[272,256]{1,0:T(8,128)(2,1)S(1)} %slice.198), channel_id=1, source_target_pairs={{8,0},{16,8},{24,16},{28,24},{20,28},{12,20},{4,12},{0,4},{9,1},{1... | collective-permute-start | bytes 417800 | tf_op jit(solution)/shard_map/ppermute | solution.py:42
  181.3 19.4 %collective-permute-start.63 = (bf16[96,2304]{1,0:T(8,128)(2,1)S(1)}, bf16[96,2304]{1,0:T(8,128)(2,1)S(1)}, u32[]{:S(2)}, u32[]{:S(2)}) collective-permute-start(bf16[96,2304]{1,0:T(8,128)(2,1)S(1)} %add_convert_fusion.3), channel_id=1, source_target_pairs={{0,8},{8,16},{16,24},{24,28},{28,20},{20,12},{12,4},{4,0},{1,9},{9... | collective-permute-start | bytes 1327112 | tf_op jit(solution)/shard_map/ppermute | solution.py:37
  182.0 19.8 %collective-permute-start.65 = (bf16[96,2304]{1,0:T(8,128)(2,1)S(1)}, bf16[96,2304]{1,0:T(8,128)(2,1)S(1)}, u32[]{:S(2)}, u32[]{:S(2)}) collective-permute-start(bf16[96,2304]{1,0:T(8,128)(2,1)S(1)} %add_convert_fusion.2), channel_id=1, source_target_pairs={{8,0},{16,8},{24,16},{28,24},{20,28},{12,20},{4,12},{0,4},{9,1},{1... | collective-permute-start | bytes 1327112 | tf_op jit(solution)/shard_map/ppermute | solution.py:42
  187.6 5.5 %collective-permute-start.53 = (bf16[48,768]{1,0:T(8,128)(2,1)S(1)}, bf16[48,768]{1,0:T(8,128)(2,1)S(1)}, u32[]{:S(2)}, u32[]{:S(2)}) collective-permute-start(bf16[48,768]{1,0:T(8,128)(2,1)S(1)} %get-tuple-element.241), channel_id=1, source_target_pairs={{0,8},{8,16},{16,24},{24,28},{28,20},{20,12},{12,4},{4,0},{1,9},{9... | collective-permute-start | bytes 221192 | tf_op jit(solution)/shard_map/ppermute | solution.py:37
  188.3 5.6 %collective-permute-start.57 = (bf16[48,768]{1,0:T(8,128)(2,1)S(1)}, bf16[48,768]{1,0:T(8,128)(2,1)S(1)}, u32[]{:S(2)}, u32[]{:S(2)}) collective-permute-start(bf16[48,768]{1,0:T(8,128)(2,1)S(1)} %get-tuple-element.246), channel_id=1, source_target_pairs={{8,0},{16,8},{24,16},{28,24},{20,28},{12,20},{4,12},{0,4},{9,1},{1... | collective-permute-start | bytes 221192 | tf_op jit(solution)/shard_map/ppermute | solution.py:42
  189.7 17.9 %collective-permute-start.51 = (bf16[256,768]{1,0:T(8,128)(2,1)S(1)}, bf16[256,768]{1,0:T(8,128)(2,1)S(1)}, u32[]{:S(2)}, u32[]{:S(2)}) collective-permute-start(bf16[256,768]{1,0:T(8,128)(2,1)S(1)} %get-tuple-element.239), channel_id=1, source_target_pairs={{0,1},{1,0},{2,3},{3,2},{4,5},{5,4},{6,7},{7,6},{8,9},{9,8},{10,11... | collective-permute-start | bytes 1179656 | tf_op jit(solution)/shard_map/ppermute | solution.py:47
  193.1 5.3 %collective-permute-start.54 = (bf16[96,768]{1,0:T(8,128)(2,1)S(1)}, bf16[96,768]{1,0:T(8,128)(2,1)S(1)}, u32[]{:S(2)}, u32[]{:S(2)}) collective-permute-start(bf16[96,768]{1,0:T(8,128)(2,1)S(1)} %pad_maximum_fusion.11), channel_id=1, source_target_pairs={{0,8},{8,16},{16,24},{24,28},{28,20},{20,12},{12,4},{4,0},{1,9},{9... | collective-permute-start | bytes 442376 | tf_op jit(solution)/shard_map/ppermute | solution.py:37
  193.9 5.6 %collective-permute-start.58 = (bf16[96,768]{1,0:T(8,128)(2,1)S(1)}, bf16[96,768]{1,0:T(8,128)(2,1)S(1)}, u32[]{:S(2)}, u32[]{:S(2)}) collective-permute-start(bf16[96,768]{1,0:T(8,128)(2,1)S(1)} %pad_maximum_fusion.12), channel_id=1, source_target_pairs={{8,0},{16,8},{24,16},{28,24},{20,28},{12,20},{4,12},{0,4},{9,1},{1... | collective-permute-start | bytes 442376 | tf_op jit(solution)/shard_map/ppermute | solution.py:42
  198.5 6.8 %collective-permute-start.55 = (bf16[96,768]{1,0:T(8,128)(2,1)S(1)}, bf16[96,768]{1,0:T(8,128)(2,1)S(1)}, u32[]{:S(2)}, u32[]{:S(2)}) collective-permute-start(bf16[96,768]{1,0:T(8,128)(2,1)S(1)} %add_convert_fusion.13), channel_id=1, source_target_pairs={{0,8},{8,16},{16,24},{24,28},{28,20},{20,12},{12,4},{4,0},{1,9},{9... | collective-permute-start | bytes 442376 | tf_op jit(solution)/shard_map/ppermute | solution.py:37
  199.6 6.8 %collective-permute-start.59 = (bf16[96,768]{1,0:T(8,128)(2,1)S(1)}, bf16[96,768]{1,0:T(8,128)(2,1)S(1)}, u32[]{:S(2)}, u32[]{:S(2)}) collective-permute-start(bf16[96,768]{1,0:T(8,128)(2,1)S(1)} %add_convert_fusion.11), channel_id=1, source_target_pairs={{8,0},{16,8},{24,16},{28,24},{20,28},{12,20},{4,12},{0,4},{9,1},{1... | collective-permute-start | bytes 442376 | tf_op jit(solution)/shard_map/ppermute | solution.py:42
  200.8 19.5 %collective-permute-start.64 = (bf16[96,2304]{1,0:T(8,128)(2,1)S(1)}, bf16[96,2304]{1,0:T(8,128)(2,1)S(1)}, u32[]{:S(2)}, u32[]{:S(2)}) collective-permute-start(bf16[96,2304]{1,0:T(8,128)(2,1)S(1)} %add_convert_fusion.1), channel_id=1, source_target_pairs={{0,8},{8,16},{16,24},{24,28},{28,20},{20,12},{12,4},{4,0},{1,9},{9... | collective-permute-start | bytes 1327112 | tf_op jit(solution)/shard_map/ppermute | solution.py:37
  201.9 18.4 %collective-permute-start.66 = (bf16[96,2304]{1,0:T(8,128)(2,1)S(1)}, bf16[96,2304]{1,0:T(8,128)(2,1)S(1)}, u32[]{:S(2)}, u32[]{:S(2)}) collective-permute-start(bf16[96,2304]{1,0:T(8,128)(2,1)S(1)} %add_convert_fusion), channel_id=1, source_target_pairs={{8,0},{16,8},{24,16},{28,24},{20,28},{12,20},{4,12},{0,4},{9,1},{1... | collective-permute-start | bytes 1327112 | tf_op jit(solution)/shard_map/ppermute | solution.py:42
  205.4 9.0 %collective-permute-start.56 = (bf16[96,768]{1,0:T(8,128)(2,1)S(1)}, bf16[96,768]{1,0:T(8,128)(2,1)S(1)}, u32[]{:S(2)}, u32[]{:S(2)}) collective-permute-start(bf16[96,768]{1,0:T(8,128)(2,1)S(1)} %add_convert_fusion.12), channel_id=1, source_target_pairs={{0,8},{8,16},{16,24},{24,28},{28,20},{20,12},{12,4},{4,0},{1,9},{9... | collective-permute-start | bytes 442376 | tf_op jit(solution)/shard_map/ppermute | solution.py:37
  206.4 8.4 %collective-permute-start.60 = (bf16[96,768]{1,0:T(8,128)(2,1)S(1)}, bf16[96,768]{1,0:T(8,128)(2,1)S(1)}, u32[]{:S(2)}, u32[]{:S(2)}) collective-permute-start(bf16[96,768]{1,0:T(8,128)(2,1)S(1)} %add_convert_fusion.10), channel_id=1, source_target_pairs={{8,0},{16,8},{24,16},{28,24},{20,28},{12,20},{4,12},{0,4},{9,1},{1... | collective-permute-start | bytes 442376 | tf_op jit(solution)/shard_map/ppermute | solution.py:42
  208.4 10.1 %collective-permute-start.52 = (bf16[128,768]{1,0:T(8,128)(2,1)}, bf16[128,768]{1,0:T(8,128)(2,1)}, u32[]{:S(2)}, u32[]{:S(2)}) collective-permute-start(bf16[128,768]{1,0:T(8,128)(2,1)} %add_convert_fusion.6), channel_id=1, source_target_pairs={{0,2},{1,3},{2,0},{3,1},{4,6},{5,7},{6,4},{7,5},{8,10},{9,11},{10,... | collective-permute-start | bytes 589832 | tf_op jit(solution)/shard_map/ppermute | solution.py:47
  (21 other events, 173.9 us)
where the time goes:
time: 227 us; the launch traced here: 223 us
  waiting for transfers between devices  93 us (41%)
  Pallas kernels  54.6 us (24%)
  starting transfers between devices  53.4 us (24%)
  local copies, waits for them, and re-layouts  10.4 us (5%)
  other arithmetic  7.63 us (3%)
  between operations  3.69 us (2%)
    pallas_call x22, Pallas kernels, call(): pl.pallas_call(kernel, grid_spec=pltpu.PrefetchScalarGridSpec(num_scalar_...  54.6 us
    ppermute x20, waiting for transfers between devices, forward_hop(): lax.ppermute(v, 'row', [(CYCLE[i], CYCLE[(i + 1) % n]) for i in range(n)])  46.2 us
    ppermute x27, waiting for transfers between devices, col_swap(): return lax.ppermute(v, 'col', [(i, i ^ mask) for i in range(count)])  35.4 us
    ppermute x20, starting transfers between devices, forward_hop(): lax.ppermute(v, 'row', [(CYCLE[i], CYCLE[(i + 1) % n]) for i in range(n)])  23.5 us
    ppermute x20, starting transfers between devices, backward_hop(): lax.ppermute(v, 'row', [(CYCLE[(i + 1) % n], CYCLE[i]) for i in range(n)])  18.8 us
    ppermute x20, waiting for transfers between devices, backward_hop(): lax.ppermute(v, 'row', [(CYCLE[(i + 1) % n], CYCLE[i]) for i in range(n)])  11.4 us
    ppermute x27, starting transfers between devices, col_swap(): return lax.ppermute(v, 'col', [(i, i ^ mask) for i in range(count)])  11.1 us
    unnamed x47, local copies, waits for them, and re-layouts  4.74 us
  transfers between devices with their start and end apart: 67, of which 33 were waited for; matrix products, arithmetic and copies ran while one was open for 5% of the time, Pallas kernels for 22%

commit v1 on v0

--- a/solution.py
+++ b/solution.py
@@ -111,13 +111,13 @@
         self.moving = ahead, back
         return self.moving
 
-    def result(self):
+    def terms(self):
         if len(self.blocks) == 1:
-            return lax.psum_scatter(self.blocks[0].astype(F32), "row", scatter_dimension=0, tiled=True)
+            full = lax.psum_scatter(self.blocks[0].astype(F32), "row", scatter_dimension=0, tiled=True)
+            return [full, jnp.zeros_like(full), jnp.zeros_like(full)]
         while self.hops < 4:
             self.step()
-        ahead, back = self.moving
-        return self.blocks[0].astype(F32) + ahead.astype(F32) + back.astype(F32)
+        return [self.blocks[0], *self.moving]
 
 
 def col_pieces(v, *first):
@@ -139,7 +139,7 @@
 ANY = pl.BlockSpec(memory_space=pl.ANY)
 
 
-def call(kernel, name, args, outs, prefetch=(), scratch=(), specs=None, out_specs=None, aliases=None, grid=(1,), flops=0, exps=0, limit=20):
+def call(kernel, name, args, outs, prefetch=(), scratch=(), specs=None, out_specs=None, aliases=None, grid=(1,), flops=0, exps=0, limit=20, cost=COST):
     args, outs = list(args), list(outs)
     moved = sum(a.size * a.dtype.itemsize for a in args) + sum(
         math.prod(o.shape) * o.dtype.itemsize for o in outs
@@ -155,7 +155,7 @@
         ),
         out_shape=outs,
         input_output_aliases=aliases or {},
-        cost_estimate=pl.CostEstimate(flops=int(flops * COST), bytes_accessed=int(moved * COST), transcendentals=int(exps * COST)),
+        cost_estimate=pl.CostEstimate(flops=int(flops * cost), bytes_accessed=int(moved * cost), transcendentals=int(exps * cost)),
         compiler_params=pltpu.CompilerParams(vmem_limit_bytes=limit << 20),
         name=name,
     )(*prefetch, *args)
@@ -167,6 +167,15 @@
 
 def rows_at(start, count):
     return pl.ds(pl.multiple_of(start, 4), count)
+
+
+def pack_kernel(parts, weights, w_out, tokens, out):
+    early = jnp.concatenate([*(weights[c] for c in range(3)), w_out[...].T], axis=1)
+    half, token_half = early.shape[0] // parts, tokens.shape[0] // parts
+    for i in range(parts):
+        at = i * (half + token_half)
+        out[at : at + half] = early[i * half : (i + 1) * half]
+        out[at + half : at + half + token_half] = tokens[i * token_half : (i + 1) * token_half]
 
 
 def assemble_kernel(split, cuts, starts, *refs):
@@ -235,36 +244,41 @@
     if mode == "first":
         q_own, refs = refs[0], refs[1:]
         q_own[...] = q[...]
-    each = range(heads)
-    scores = [dot(k[h], q_own[h], TN) for h in each]
-    news = [jnp.max(s, axis=0, keepdims=True) for s in scores]
-    if mode != "first":
-        olds = [top_in[h : h + 1] for h in each]
-        news = [jnp.maximum(o, n) for o, n in zip(olds, news)]
-        keeps = [jnp.exp(o - n) for o, n in zip(olds, news)]
-    weights = [jnp.exp(s - n) for s, n in zip(scores, news)]
-    sums = [jnp.sum(w, axis=0, keepdims=True) for w in weights]
-    values = [dot(v[h, :HEAD, :], w.astype(BF), NN) for h, w in enumerate(weights)]
-    if mode != "first":
-        sums = [sum_in[h : h + 1] * keeps[h] + sums[h] for h in each]
-        values = [acc_in[h] * keeps[h] + values[h] for h in each]
-    if mode != "last":
+    if mode == "last":
+        near, far, context_bf, context, log_total = refs
+    else:
         top, total, acc = refs
-        for h in each:
-            top[h : h + 1] = news[h]
-            total[h : h + 1] = sums[h]
-            acc[h] = values[h]
-        return
-    near, far, context_bf, context, log_total = refs
-    for h in each:
-        value = values[h] / sums[h]
-        context[h] = value
-        context_bf[h * HEAD : (h + 1) * HEAD] = value.astype(BF)
-        log_total[h : h + 1] = news[h] + jnp.log(sums[h])
-    attn = dot(context_bf[...], w_out[...], TN)
-    half = near.shape[0]
-    near[...] = attn[:half].astype(BF)
-    far[...] = attn[half:].astype(BF)
+
+    @pl.loop(0, heads)
+    def _(h):
+        one = pl.ds(h, 1)
+        scores = dot(k[h], q_own[h], TN)
+        new = jnp.max(scores, axis=0, keepdims=True)
+        if mode != "first":
+            old = top_in[one, :]
+            new = jnp.maximum(old, new)
+            keep = jnp.exp(old - new)
+        weights = jnp.exp(scores - new)
+        count = jnp.sum(weights, axis=0, keepdims=True)
+        value = dot(v[h, :HEAD, :], weights.astype(BF), NN)
+        if mode != "first":
+            count = sum_in[one, :] * keep + count
+            value = acc_in[h] * keep + value
+        if mode == "last":
+            value = value / count
+            context[h] = value
+            context_bf[pl.ds(pl.multiple_of(h * HEAD, HEAD), HEAD), :] = value.astype(BF)
+            log_total[one, :] = new + jnp.log(count)
+        else:
+            top[one, :] = new
+            total[one, :] = count
+            acc[h] = value
+
+    if mode == "last":
+        attn = dot(context_bf[...], w_out[...], TN)
+        half = near.shape[0]
+        near[...] = attn[:half].astype(BF)
+        far[...] = attn[half:].astype(BF)
 
 
 def attend(mode, pieces, slot, weight, turn, marks, heads, total, group, carried=(), w_out=None):
@@ -330,12 +344,13 @@
         out[...] = out_in[...]
 
     rows = HEAD + AUX
-    each = range(heads)
-    terms = [g[h * rows : (h + 1) * rows] for h in each]
-    probs = [jnp.exp(dot(k[h], with_terms(q[h], terms[h]), TN)) for h in each]
-    grads = [(probs[h] * dot(v[h], terms[h], TN)).astype(BF) for h in each]
-    for h in each:
-        out[h] += dot(k[h, :HEAD, :], grads[h], NN)
+
+    @pl.loop(0, heads)
+    def _(h):
+        terms = g[pl.ds(pl.multiple_of(h * rows, 16), rows), :]
+        probs = jnp.exp(dot(k[h], with_terms(q[h], terms), TN))
+        grads = (probs * dot(v[h], terms, TN)).astype(BF)
+        out[h] += dot(k[h, :HEAD, :], grads, NN)
 
 
 def query_grad(q, g, keys, values, heads, width, begin, steps, carried):
@@ -358,26 +373,24 @@
 def key_grad_kernel(heads, count, step, carried, slots, *refs):
     pieces, (q, k, v), refs = refs[:count], refs[count : count + 3], refs[count + 3 :]
     rows = HEAD + AUX
-    each = range(heads)
     if carried:
         dk_in, dv_in = refs[:2]
         refs = refs[2:]
     dk, dv, norms = refs
 
-    def of(h):
-        if count == 1:
-            return pieces[0][h * rows : (h + 1) * rows]
+    @pl.loop(0, heads)
+    def _(h):
+        mine = pl.ds(pl.multiple_of(h * rows, 16), rows)
         lanes = [slice(i, i + step) for i in range(0, pieces[0].shape[1], step)]
-        return jnp.concatenate([p[h * rows : (h + 1) * rows, n] for n in lanes for p in pieces], axis=1)
-
-    terms = [of(h) for h in each]
-    probs = [jnp.exp(dot(with_terms(q[h], terms[h]), k[h], TN)) for h in each]
-    grads = [(probs[h] * dot(terms[h], v[h], TN)).astype(BF) for h in each]
-    for h in each:
-        value = dot(terms[h][:HEAD], probs[h].astype(BF), NN)
-        key = dot(q[h, :HEAD, :], grads[h], NN)
+        parts = [p[mine, n] for n in lanes for p in pieces]
+        terms = parts[0] if len(parts) == 1 else jnp.concatenate(parts, axis=1)
+        probs = jnp.exp(dot(with_terms(q[h], terms), k[h], TN))
+        grads = (probs * dot(terms, v[h], TN)).astype(BF)
+        value = dot(terms[:HEAD], probs.astype(BF), NN)
+        key = dot(q[h, :HEAD, :], grads, NN)
         dv[h] = dv_in[h] + value if carried else value
         dk[h] = dk_in[h] + key if carried else key
+
     for i in range(norms.shape[0]):
         norms[i] = pieces[i][heads * rows : heads * rows + NORM_ROWS, :NORM_LANES].astype(F32)
 
@@ -464,40 +477,49 @@
 
 
 def forward_kernel(count, units, starts, *refs):
-    pieces, hidden, (gu, dn, gate_up, inner, near, far) = refs[:count], refs[count:-6], refs[-6:]
+    pieces, hidden, (gu, dn, gate_up, inner, near, far, held) = refs[:count], refs[count:-7], refs[-7:]
     for i, piece in enumerate(pieces):
         rows = pl.ds(pl.multiple_of(starts[i], 16), piece.shape[0])
         gu[rows, :] = piece[:, : 2 * units]
         dn[rows, :] = piece[:, 2 * units :]
-    pairs = len(hidden) // 2
-    for out, part in ((near, hidden[:pairs]), (far, hidden[pairs:])):
-        x = stacked(part, part[0].shape[0])
-        size = x.shape[0]
-        begin = 0 if out is near else size
-        both = dot(x, gu[...], NN)
-        gate_up[begin : begin + size] = both
+    held[...] = stacked(hidden, hidden[0].shape[0])
+    size = held.shape[0] // 2
+
+    @pl.loop(0, 2)
+    def _(i):
+        rows = pl.ds(pl.multiple_of(i * size, 128), size)
+        both = dot(held[rows, :], gu[...], NN)
+        gate_up[rows, :] = both
         up, gate = both[:, :units], both[:, units:]
         value = (gate * jax.nn.sigmoid(gate) * up).astype(BF)
-        inner[begin : begin + size] = value
-        out[...] = dot(value, dn[...], NT).astype(BF)
+        inner[rows, :] = value
+        part = dot(value, dn[...], NT).astype(BF)
+        for j, out in enumerate((near, far)):
+
+            @pl.when(i == j)
+            def _():
+                out[...] = part
 
 
 def backward_kernel(units, *refs):
-    pieces, (gu, dn, gate_up, grads, near, far) = refs[:-6], refs[-6:]
-    pairs = len(pieces) // 2
-    for out, part in ((near, pieces[:pairs]), (far, pieces[pairs:])):
-        g = stacked(part, part[0].shape[0])
-        size = g.shape[0]
-        begin = 0 if out is near else size
-        grad_inner = dot(g, dn[...], NN)
-        up = gate_up[begin : begin + size, :units]
-        gate = gate_up[begin : begin + size, units:]
+    pieces, (gu, dn, gate_up, grads, near, far, held) = refs[:-7], refs[-7:]
+    held[...] = stacked(pieces, pieces[0].shape[0])
+    size = held.shape[0] // 2
+
+    @pl.loop(0, 2)
+    def _(i):
+        rows = pl.ds(pl.multiple_of(i * size, 128), size)
+        grad_inner = dot(held[rows, :], dn[...], NN)
+        up, gate = gate_up[rows, :units], gate_up[rows, units:]
         sigma = jax.nn.sigmoid(gate)
-        grads[begin : begin + size, :units] = (grad_inner * gate * sigma).astype(BF)
-        grads[begin : begin + size, units:] = (
-            grad_inner * up * sigma * (1.0 + gate * (1.0 - sigma))
-        ).astype(BF)
-        out[...] = dot(grads[begin : begin + size], gu[...], NT).astype(BF)
+        grads[rows, :units] = (grad_inner * gate * sigma).astype(BF)
+        grads[rows, units:] = (grad_inner * up * sigma * (1.0 + gate * (1.0 - sigma))).astype(BF)
+        part = dot(grads[rows, :], gu[...], NT).astype(BF)
+        for j, out in enumerate((near, far)):
+
+            @pl.when(i == j)
+            def _():
+                out[...] = part
 
 
 def write_blocks(held, starts, outs):
@@ -595,6 +617,21 @@
     held[:, : 2 * width] = early[...]
     held[:, 2 * width :] = dot(mixed[width:], x, NN).T.astype(BF)
     write_blocks(held, starts, outs)
+
+
+def finish_ffn_kernel(units, block, ahead, back, gu, dn):
+    total = block[...].astype(F32) + ahead[...].astype(F32) + back[...].astype(F32)
+    gu[:, 0, :] = total[:, :units]
+    gu[:, 1, :] = total[:, units : 2 * units]
+    dn[...] = total[:, 2 * units :].T
+
+
+def finish_mix_kernel(width, block, ahead, back, mix, out):
+    total = block[...].astype(F32) + ahead[...].astype(F32) + back[...].astype(F32)
+    mix[0] = total[:, :width]
+    mix[1] = total[:, 2 * width : 3 * width]
+    mix[2] = total[:, 3 * width :]
+    out[...] = total[:, width : 2 * width].T
 
 
 NORM_ROWS = 24
@@ -684,12 +721,13 @@
         wanted = cycle_rows(place, [step for step, _ in layout]) * len(OFFSETS)
         wanted = wanted + (col ^ jnp.array([o for _, o in layout], jnp.int32))
         token_half = own // 2
-        ring_early = Rounds(
-            jnp.concatenate(
-                [early[:half], tokens[:token_half], early[half:], tokens[token_half:]], axis=0
-            ),
-            0,
+        (packed,) = call(
+            functools.partial(pack_kernel, 2),
+            "pack",
+            [w_qkv.transpose(1, 0, 2), w_out, tokens],
+            [struct((share + own, features), BF)],
         )
+        ring_early = Rounds(packed, 0)
         waits = [ring_early.step(), ring_early.step()]
         ring_early.step()
         ring_early.step()
@@ -750,6 +788,7 @@
         late_ring.step()
         far = after(far, state[0])
         keys, values, queries, *state = middle(2, three)
+        far = after(far, late_ring.done[1])
         keys, values, queries, *finished = attend(
             "last",
             [far, col_swap(far, 1)],
@@ -779,7 +818,6 @@
     near, far, context_bf, context, log_total = finished
 
     if ring:
-        near = after(near, late_ring.done[1])
         late_ring.step(near)
     else:
         late_pieces = [lax.all_gather(late, "row", axis=0, tiled=True)]
@@ -810,6 +848,7 @@
             part,
         ],
         prefetch=[starts],
+        scratch=[pltpu.VMEM((group, features), BF)],
         flops=6 * group * features * units,
     )
     result, grad_res2, grad_bf, sums2 = call(
@@ -824,6 +863,7 @@
         "ffn_backward",
         [*grad_pieces, w_gu, w_dn, gate_up],
         [struct((group, 2 * units), BF), part, part],
+        scratch=[pltpu.VMEM((group, features), BF)],
         flops=6 * group * features * units,
     )
     exchanged, passed = col_exchange(near, far)
@@ -847,7 +887,7 @@
         [*exchanged, residual1, gains[0], grad_res2, sums2],
         [flat, struct((own + 16, features), BF)],
     )
-    attn_pieces = col_pieces(package)
+    attn_pieces = after(col_pieces(package), sent)
     (package,) = call(
         functools.partial(prepare_kernel, heads, own),
         "prepare",
@@ -861,8 +901,7 @@
     if ring:
         package_ring = Rounds(package, 1)
         package_ring.step()
-        grad_query = after(grad_query, sent)
-        ffn_sum.step()
+        sent = ffn_sum.step()
     grad_query = query_grad(own_q, package, keys, values, heads, span, 0, steps_all, grad_query)
     own_turn = pl.BlockSpec((HEAD, group), lambda i, s, *_: (0, s[0]))
     args = [*x_pieces, *attn_pieces, grad_query, turn, context_bf]
@@ -889,7 +928,7 @@
     norm_out = struct((4, features), F32)
     if ring:
         package_ring.step(early_grad)
-        sums, norms = key_step([after(package, early_grad, package_ring.done[0])], 1, 6, ())
+        sums, norms = key_step([after(package, early_grad, package_ring.done[0], sent)], 1, 6, ())
         norm_pieces = [norms]
         for i in range(3):
             sums, norms = key_step(package_ring.done[i], 2, i, sums)
@@ -942,20 +981,33 @@
         specs=specs,
         flops=10 * width * features * group,
     )
-    late_grad = RowSum(blocks).result()
+    late_sum = RowSum(blocks)
+    late_sum = late_sum.terms()
     near, other, last = col_exchange(near, far)[0]
-    ffn_grad = ffn_sum.result()
+    grad_gu, grad_dn = call(
+        functools.partial(finish_ffn_kernel, units),
+        "finish_ffn",
+        ffn_sum.terms(),
+        [struct((share, 2, units), F32), struct((units, share), F32)],
+        cost=20.0,
+    )
     grad_tokens = grad_res1 + (
         near[:own].astype(F32) + other[:own].astype(F32) + last.astype(F32)
     )
-    grad_mix = jnp.concatenate([late_grad[:, :width], late_grad[:, 2 * width :]], axis=1)
+    grad_mix, grad_out = call(
+        functools.partial(finish_mix_kernel, width),
+        "finish_mix",
+        late_sum,
+        [struct((3, share, width), F32), struct((width, share), F32)],
+        cost=20.0,
+    )
     return (
         result,
         grad_tokens,
-        grad_mix.reshape(share, 3, width),
-        late_grad[:, width : 2 * width].T,
-        ffn_grad[:, : 2 * units].reshape(share, 2, units),
-        ffn_grad[:, 2 * units :].T,
+        grad_mix.transpose(1, 0, 2),
+        grad_out,
+        grad_gu,
+        grad_dn,
         norm_sums[0],
         norm_sums[1],
         norm_sums[2],

time: 227 us -> 222 us (0.978); the launches traced: 223 us -> 222 us
  Pallas kernels: 54.6 us -> 67.2 us
  waiting for transfers between devices: 93 us -> 83.8 us
  local copies, waits for them, and re-layouts: 10.4 us -> 6.06 us
    pallas_call x22 -> x25, Pallas kernels: 54.6 us -> 67.2 us  [call(): pl.pallas_call(kernel, grid_spec=pltpu.PrefetchScalarGridSpec(num_scalar_...]
    ppermute x20, waiting for transfers between devices: 46.2 us -> 34.1 us  [forward_hop(): lax.ppermute(v, 'row', [(CYCLE[i], CYCLE[(i + 1) % n]) for i in range(n)])]
    ppermute x20, starting transfers between devices: 23.5 us -> 32.4 us  [forward_hop(): lax.ppermute(v, 'row', [(CYCLE[i], CYCLE[(i + 1) % n]) for i in range(n)])]
    ppermute x20, starting transfers between devices: 18.8 us -> 10.7 us  [backward_hop(): lax.ppermute(v, 'row', [(CYCLE[(i + 1) % n], CYCLE[i]) for i in range(n)])]
    ppermute x27, waiting for transfers between devices: 35.4 us -> 40.5 us  [col_swap(): return lax.ppermute(v, 'col', [(i, i ^ mask) for i in range(count)])]
    ppermute x20, waiting for transfers between devices: 11.4 us -> 9.14 us  [backward_hop(): lax.ppermute(v, 'row', [(CYCLE[(i + 1) % n], CYCLE[i]) for i in range(n)])]
    unnamed x47 -> x34, local copies, waits for them, and re-layouts: 4.74 us -> 3.69 us
  transfers between devices with their start and end apart: 67 -> 67, of which waited for: 33 -> 31; matrix products, arithmetic and copies ran while one was open for 5% -> 5% of each run, Pallas kernels for 22% -> 21%
where the time goes in v1:
time: 222 us
  waiting for transfers between devices  83.8 us (38%)
  Pallas kernels  67.2 us (30%)
  starting transfers between devices  53.4 us (24%)
  other arithmetic  7.94 us (4%)
  local copies, waits for them, and re-layouts  6.06 us (3%)
  between operations  3.45 us (2%)
    pallas_call x25, Pallas kernels, call(): pl.pallas_call(kernel, grid_spec=pltpu.PrefetchScalarGridSpec(num_scalar_...  67.2 us
    ppermute x27, waiting for transfers between devices, col_swap(): return lax.ppermute(v, 'col', [(i, i ^ mask) for i in range(count)])  40.5 us
    ppermute x20, waiting for transfers between devices, forward_hop(): lax.ppermute(v, 'row', [(CYCLE[i], CYCLE[(i + 1) % n]) for i in range(n)])  34.1 us
    ppermute x20, starting transfers between devices, forward_hop(): lax.ppermute(v, 'row', [(CYCLE[i], CYCLE[(i + 1) % n]) for i in range(n)])  32.4 us
    ppermute x20, starting transfers between devices, backward_hop(): lax.ppermute(v, 'row', [(CYCLE[(i + 1) % n], CYCLE[i]) for i in range(n)])  10.7 us
    ppermute x27, starting transfers between devices, col_swap(): return lax.ppermute(v, 'col', [(i, i ^ mask) for i in range(count)])  10.3 us
    ppermute x20, waiting for transfers between devices, backward_hop(): lax.ppermute(v, 'row', [(CYCLE[(i + 1) % n], CYCLE[i]) for i in range(n)])  9.14 us
  transfers between devices with their start and end apart: 67, of which 31 were waited for; matrix products, arithmetic and copies ran while one was open for 5% of the time, Pallas kernels for 21%

profile of v1, /device:TPU:0, one launch (start us, length us, event | category | flops | bytes accessed | tf_op | source)
XLA Modules:
  0.0 221.8 jit_solution(1106970819114967593)
XLA Ops:
  3.5 3.1 %collective-permute-start = (bf16[224,768]{1,0:T(8,128)(2,1)S(1)}, bf16[224,768]{1,0:T(8,128)(2,1)S(1)}, u32[]{:S(2)}, u32[]{:S(2)}) collective-permute-start(bf16[224,768]{1,0:T(8,128)(2,1)S(1)} %pack.1.refs_0_), channel_id=1, source_target_pairs={{0,8},{8,16},{16,24},{24,28},{28,20},{20,12},{12,4},{4,0},{1,9},{9... | collective-permute-start | bytes 1032200 | tf_op jit(solution)/shard_map/ppermute | solution.py:37
  6.6 2.0 collective-permute-start.16
  9.4 1.4 fusion.49
  17.1 1.6 collective-permute-start.12
  18.7 1.6 collective-permute-start.1
  20.7 1.9 multiply_cosine_fusion
  22.6 4.4 %collective-permute-done.1.refs_3_ = bf16[224,768]{1,0:T(8,128)(2,1)S(1)} collective-permute-done((bf16[224,768]{1,0:T(8,128)(2,1)S(1)}, bf16[224,768]{1,0:T(8,128)(2,1)S(1)}, u32[]{:S(2)}, u32[]{:S(2)}) %collective-permute-start.1) | collective-permute-done | bytes 344096 | tf_op jit(solution)/shard_map/ppermute | solution.py:37
  27.0 1.6 collective-permute-start.2
  29.9 5.3 %collective-permute-done.2.refs_5_ = bf16[224,768]{1,0:T(8,128)(2,1)S(1)} collective-permute-done((bf16[224,768]{1,0:T(8,128)(2,1)S(1)}, bf16[224,768]{1,0:T(8,128)(2,1)S(1)}, u32[]{:S(2)}, u32[]{:S(2)}) %collective-permute-start.2) | collective-permute-done | bytes 344096 | tf_op jit(solution)/shard_map/ppermute | solution.py:37
  35.2 1.6 collective-permute-start.10
  37.4 1.6 collective-permute-start.6
  39.8 2.8 %collective-permute-done.10.refs_7_ = bf16[112,768]{1,0:T(8,128)(2,1)S(1)} collective-permute-done((bf16[112,768]{1,0:T(8,128)(2,1)S(1)}, bf16[112,768]{1,0:T(8,128)(2,1)S(1)}, u32[]{:S(2)}, u32[]{:S(2)}) %collective-permute-start.10) | collective-permute-done | bytes 172064 | tf_op jit(solution)/shard_map/ppermute | solution.py:37
  42.6 1.7 collective-permute-done.11.refs_8_
  46.2 2.7 %attend.5 = (bf16[3,80,4096]{2,1,0:T(8,128)(2,1)S(1)}, bf16[3,80,4096]{2,1,0:T(8,128)(2,1)S(1)}, bf16[3,80,4096]{2,1,0:T(8,128)(2,1)S(1)}, bf16[3,80,512]{2,1,0:...) custom-call(s32[1]{0:T(128)} %constant.49.clone.1.slot.slots, ...), custom_call_target="tpu_custom_call" | custom-call | flops 8053063 | bytes 193249 | tf_op jit(solution)/shard_map/attend/pallas_call | solution.py:147
  49.1 1.6 collective-permute-start.8
  51.2 4.4 %attend.6 = (bf16[3,80,4096]{2,1,0:T(8,128)(2,1)S(1)}, bf16[3,80,4096]{2,1,0:T(8,128)(2,1)S(1)}, bf16[3,80,4096]{2,1,0:T(8,128)(2,1)S(1)}, f32[3,512]{1,0:T(4,12...) custom-call(s32[1]{0:T(128)} %constant.63.clone.1.slot, ...), custom_call_target="tpu_custom_call", output_to_operand_aliasing={{0}: (10, {}), {1}: (11, {}), {2}: (12, {})} | custom-call | flops 16106127 | bytes 335052 | tf_op jit(solution)/shard_map/attend/pallas_call | solution.py:147
  56.3 6.8 %collective-permute-done.15 = bf16[128,768]{1,0:T(8,128)(2,1)S(1)} collective-permute-done((bf16[128,768]{1,0:T(8,128)(2,1)S(1)}, bf16[128,768]{1,0:T(8,128)(2,1)S(1)}, u32[]{:S(2)}, u32[]{:S(2)}) %collective-permute-start.15) | collective-permute-done | bytes 196640 | tf_op jit(solution)/shard_map/ppermute | solution.py:47
  63.1 4.4 %attend.7 = (bf16[3,80,4096]{2,1,0:T(8,128)(2,1)S(1)}, bf16[3,80,4096]{2,1,0:T(8,128)(2,1)S(1)}, bf16[3,80,4096]{2,1,0:T(8,128)(2,1)S(1)}, f32[3,512]{1,0:T(4,12...) custom-call(s32[1]{0:T(128)} %constant.48.clone.1.slot, ...), custom_call_target="tpu_custom_call", output_to_operand_aliasing={{0}: (10, {}), {1}: (11, {}), {2}: (12, {})} | custom-call | flops 16106127 | bytes 335052 | tf_op jit(solution)/shard_map/attend/pallas_call | solution.py:147
  67.6 4.3 %attend.8 = (bf16[3,80,4096]{2,1,0:T(8,128)(2,1)S(1)}, bf16[3,80,4096]{2,1,0:T(8,128)(2,1)S(1)}, bf16[3,80,4096]{2,1,0:T(8,128)(2,1)S(1)}, f32[3,512]{1,0:T(4,12...) custom-call(s32[1]{0:T(128)} %constant.64.clone.1.slot, ...), custom_call_target="tpu_custom_call", output_to_operand_aliasing={{0}: (10, {}), {1}: (11, {}), {2}: (12, {})} | custom-call | flops 16106127 | bytes 335052 | tf_op jit(solution)/shard_map/attend/pallas_call | solution.py:147
  72.0 3.1 %attend.9 = (bf16[3,80,4096]{2,1,0:T(8,128)(2,1)S(1)}, bf16[3,80,4096]{2,1,0:T(8,128)(2,1)S(1)}, bf16[3,80,4096]{2,1,0:T(8,128)(2,1)S(1)}, bf16[256,768]{1,0:T(8...) custom-call(s32[1]{0:T(128)} %constant.47.clone.1.slot, ...), custom_call_target="tpu_custom_call", output_to_operand_aliasing={{0}: (10, {}), {1}: (11, {}), {2}: (12, {})} | custom-call | flops 8053063 | bytes 344760 | tf_op jit(solution)/shard_map/attend/pallas_call | solution.py:147
  75.6 1.6 collective-permute-start.22
  78.3 6.0 %collective-permute-done.27.last = bf16[128,768]{1,0:T(8,128)(2,1)S(1)} collective-permute-done((bf16[128,768]{1,0:T(8,128)(2,1)S(1)}, bf16[128,768]{1,0:T(8,128)(2,1)S(1)}, u32[]{:S(2)}, u32[]{:S(2)}) %collective-permute-start.27) | collective-permute-done | bytes 196640 | tf_op jit(solution)/shard_map/ppermute | solution.py:47
  84.2 1.2 first_norm.1
  86.0 1.7 collective-permute-done.22.refs_5_
  87.8 1.6 collective-permute-start.24
  91.2 3.2 %collective-permute-done.24.refs_7_ = bf16[48,2304]{1,0:T(8,128)(2,1)S(1)} collective-permute-done((bf16[48,2304]{1,0:T(8,128)(2,1)S(1)}, bf16[48,2304]{1,0:T(8,128)(2,1)S(1)}, u32[]{:S(2)}, u32[]{:S(2)}) %collective-permute-start.24) | collective-permute-done | bytes 221216 | tf_op jit(solution)/shard_map/ppermute | solution.py:37
  94.4 1.6 collective-permute-done.25.refs_8_
  96.0 3.4 %ffn_forward.1 = (bf16[768,1536]{1,0:T(8,128)(2,1)S(1)}, bf16[768,768]{1,0:T(8,128)(2,1)S(1)}, f32[512,1536]{1,0:T(8,128)S(1)}, bf16[512,768]{1,0:T(8,128)(2,1)S...) custom-call(s32[9]{0:T(128)S(1)} %fusion.16.starts, bf16[96,2304]{1,0:T(8,128)(2,1)S(1)} %pad_maximum_fusion.1.refs_0_, ...), custom_call_target="tpu_custom_call" | custom-call | flops 36238784 | bytes 251658 | tf_op jit(solution)/shard_map/ffn_forward/pallas_call | solution.py:147
  99.5 1.7 collective-permute-done.31.other
  101.8 6.4 %collective-permute-done.32.last = bf16[128,768]{1,0:T(8,128)(2,1)S(1)} collective-permute-done((bf16[128,768]{1,0:T(8,128)(2,1)S(1)}, bf16[128,768]{1,0:T(8,128)(2,1)S(1)}, u32[]{:S(2)}, u32[]{:S(2)}) %collective-permute-start.32) | collective-permute-done | bytes 196640 | tf_op jit(solution)/shard_map/ppermute | solution.py:47
  109.9 5.6 %collective-permute-done.33.refs_1_.refs_5_ = bf16[128,768]{1,0:T(8,128)(2,1)S(1)} collective-permute-done((bf16[128,768]{1,0:T(8,128)(2,1)S(1)}, bf16[128,768]{1,0:T(8,128)(2,1)S(1)}, u32[]{:S(2)}, u32[]{:S(2)}) %collective-permute-start.33) | collective-permute-done | bytes 196640 | tf_op jit(solution)/shard_map/ppermute | solution.py:47
  115.5 1.4 collective-permute-done.35.refs_3_.refs_7_
  117.0 3.2 %ffn_backward.1 = (bf16[512,1536]{1,0:T(8,128)(2,1)S(1)}, bf16[256,768]{1,0:T(8,128)(2,1)S(1)}, bf16[256,768]{1,0:T(8,128)(2,1)S(1)}) custom-call(bf16[128,768]{1,0:T(8,128)(2,1)S(1)} %get-tuple-element.194.refs_0_.refs_4_, bf16[128,768]{1,0:T(8,128)(2,1)S(1)} %collective-permute-done.33.refs_1_.refs_5_, ...), custom_call_target="tpu_custom_call" | custom-call | flops 36238784 | bytes 196608 | tf_op jit(solution)/shard_map/ffn_backward/pallas_call | solution.py:147
  120.4 1.6 collective-permute-done.36.other
  122.0 2.8 %ffn_grad.1 = (bf16[96,2304]{1,0:T(8,128)(2,1)S(1)}, bf16[96,2304]{1,0:T(8,128)(2,1)S(1)}, bf16[96,2304]{1,0:T(8,128)(2,1)S(1)}, bf16[96,2304]{1,0:T(8,128)(2,1)...) custom-call(s32[9]{0:T(128)S(1)} %fusion.32.starts, ...), custom_call_target="tpu_custom_call" | custom-call | flops 36238784 | bytes 149422 | tf_op jit(solution)/shard_map/ffn_grad/pallas_call | solution.py:147
  125.9 1.6 collective-permute-start.41
  127.5 4.5 %collective-permute-done.37.last = bf16[128,768]{1,0:T(8,128)(2,1)S(1)} collective-permute-done((bf16[128,768]{1,0:T(8,128)(2,1)S(1)}, bf16[128,768]{1,0:T(8,128)(2,1)S(1)}, u32[]{:S(2)}, u32[]{:S(2)}) %collective-permute-start.37) | collective-permute-done | bytes 196640 | tf_op jit(solution)/shard_map/ppermute | solution.py:47
  133.6 5.2 %collective-permute-done.38.refs_1_.refs_3_ = bf16[144,768]{1,0:T(8,128)(2,1)S(1)} collective-permute-done((bf16[144,768]{1,0:T(8,128)(2,1)S(1)}, bf16[144,768]{1,0:T(8,128)(2,1)S(1)}, u32[]{:S(2)}, u32[]{:S(2)}) %collective-permute-start.38) | collective-permute-done | bytes 221216 | tf_op jit(solution)/shard_map/ppermute | solution.py:47
  138.9 1.6 collective-permute-start.47
  141.0 1.5 collective-permute-start.43
  143.1 11.5 %query_grad.1.refs_6_ = f32[3,64,512]{2,1,0:T(8,128)S(1)} custom-call(bf16[3,80,512]{2,1,0:T(8,128)(2,1)S(1)} %get-tuple-element.155.refs_5_.q, bf16[272,512]{1,0:T(8,128)(2,1)S(1)} %prepare.1.g.refs_0_, bf16[3,80,4096]{2,1,0:T(8,128)(2,1)S(1)} %get-tuple-element.223.k.refs_2_.refs_3_, bf16[3,80,4096]{2,1,0:T(8,128)(2,1)S(1)} %get-tuple-element.224.v.refs_3_.refs_4_, ...), custom_call_target="tpu_custom_call" | custom-call | flops 96636768 | bytes 104857 | tf_op jit(solution)/shard_map/query_grad/pallas_call | solution.py:147
  155.4 2.0 collective-permute-done.43.refs_0_
  157.5 1.6 collective-permute-start.45
  159.6 2.4 %key_grad.5 = (f32[3,64,512]{2,1,0:T(8,128)S(1)}, f32[3,64,512]{2,1,0:T(8,128)S(1)}, f32[1,24,256]{2,1,0:T(8,128)S(1)}) custom-call(s32[2]{0:T(128)S(1)} %broadcast_in_dim.210.slots, bf16[272,512]{1,0:T(8,128)(2,1)S(1)} %prepare.1.g.refs_0_, bf16[3,80,4096]{2,1,0:T(8,128)(2,1)S(1)} %get-tuple-element.230.refs_1_.refs_2_, ...), custom_call_target="tpu_custom_call" | custom-call | flops 16106127 | bytes 139755 | tf_op jit(solution)/shard_map/key_grad/pallas_call | solution.py:147
  162.1 3.9 %key_grad.6 = (f32[3,64,512]{2,1,0:T(8,128)S(1)}, f32[3,64,512]{2,1,0:T(8,128)S(1)}, f32[2,24,256]{2,1,0:T(8,128)S(1)}) custom-call(s32[2]{0:T(128)S(1)} %fusion.41.slots, bf16[272,512]{1,0:T(8,128)(2,1)S(1)} %collective-permute-done.43.refs_0_, bf16[272,512]{1,0:T(8,128)(2,1)S(1)} %collective-permute-done.44.refs_1_, ...), custom_call_target="tpu_custom_call" | custom-call | flops 32212254 | bytes 161546 | tf_op jit(solution)/shard_map/key_grad/pallas_call | solution.py:147
  167.0 1.5 collective-permute-start.49
  169.1 3.9 %key_grad.7 = (f32[3,64,512]{2,1,0:T(8,128)S(1)}, f32[3,64,512]{2,1,0:T(8,128)S(1)}, f32[2,24,256]{2,1,0:T(8,128)S(1)}) custom-call(s32[2]{0:T(128)S(1)} %fusion.40.slots, bf16[272,512]{1,0:T(8,128)(2,1)S(1)} %collective-permute-done.45.refs_0_, bf16[272,512]{1,0:T(8,128)(2,1)S(1)} %collective-permute-done.46.refs_1_, ...), custom_call_target="tpu_custom_call" | custom-call | flops 32212254 | bytes 161546 | tf_op jit(solution)/shard_map/key_grad/pallas_call | solution.py:147
  174.1 1.2 collective-permute-done.50.refs_1_
  175.3 1.3 collective-permute-start.51
  177.5 3.9 %key_grad.8 = (f32[3,64,512]{2,1,0:T(8,128)S(1)}, f32[3,64,512]{2,1,0:T(8,128)S(1)}, f32[2,24,256]{2,1,0:T(8,128)S(1)}) custom-call(s32[2]{0:T(128)S(1)} %fusion.39.slots, bf16[272,512]{1,0:T(8,128)(2,1)S(1)} %collective-permute-done.49.refs_0_, bf16[272,512]{1,0:T(8,128)(2,1)S(1)} %collective-permute-done.50.refs_1_, ...), custom_call_target="tpu_custom_call" | custom-call | flops 32212254 | bytes 161546 | tf_op jit(solution)/shard_map/key_grad/pallas_call | solution.py:147
  181.7 2.5 %key_grad.9 = (f32[3,64,512]{2,1,0:T(8,128)S(1)}, f32[3,64,512]{2,1,0:T(8,128)S(1)}, f32[1,24,256]{2,1,0:T(8,128)S(1)}) custom-call(s32[2]{0:T(128)S(1)} %fusion.42.slots, bf16[272,256]{1,0:T(8,128)(2,1)S(1)} %collective-permute-done.51.refs_0_, bf16[272,256]{1,0:T(8,128)(2,1)S(1)} %collective-permute-done.52.refs_1_, ...), custom_call_target="tpu_custom_call" | custom-call | flops 16106127 | bytes 155484 | tf_op jit(solution)/shard_map/key_grad/pallas_call | solution.py:147
  184.2 1.9 late_grad.1
  187.5 1.5 collective-permute-start.63
  189.0 1.2 collective-permute-start.55
  192.2 6.1 %collective-permute-done.55 = bf16[48,768]{1,0:T(8,128)(2,1)S(1)} collective-permute-done((bf16[48,768]{1,0:T(8,128)(2,1)S(1)}, bf16[48,768]{1,0:T(8,128)(2,1)S(1)}, u32[]{:S(2)}, u32[]{:S(2)}) %collective-permute-start.55) | collective-permute-done | bytes 73760 | tf_op jit(solution)/shard_map/ppermute | solution.py:37
  198.3 1.6 collective-permute-start.56
  200.5 4.4 %collective-permute-done.56 = bf16[96,768]{1,0:T(8,128)(2,1)S(1)} collective-permute-done((bf16[96,768]{1,0:T(8,128)(2,1)S(1)}, bf16[96,768]{1,0:T(8,128)(2,1)S(1)}, u32[]{:S(2)}, u32[]{:S(2)}) %collective-permute-start.56) | collective-permute-done | bytes 147488 | tf_op jit(solution)/shard_map/ppermute | solution.py:37
  204.9 1.6 collective-permute-start.57
  207.3 1.6 collective-permute-start.64
  209.5 2.0 collective-permute-done.57
  211.5 1.6 collective-permute-start.58
  214.9 1.6 collective-permute-done.62.back
  216.6 1.2 collective-permute-done.58.ahead
  219.7 1.2 finish_ffn.1
  (204 shorter events, 40.2 us)
Async XLA Ops:
  3.5 12.1 %collective-permute-start = (bf16[224,768]{1,0:T(8,128)(2,1)S(1)}, bf16[224,768]{1,0:T(8,128)(2,1)S(1)}, u32[]{:S(2)}, u32[]{:S(2)}) collective-permute-start(bf16[224,768]{1,0:T(8,128)(2,1)S(1)} %pack.1.refs_0_), channel_id=1, source_target_pairs={{0,8},{8,16},{16,24},{24,28},{28,20},{20,12},{12,4},{4,0},{1,9},{9... | collective-permute-start | bytes 1032200 | tf_op jit(solution)/shard_map/ppermute | solution.py:37
  6.6 9.5 %collective-permute-start.3 = (bf16[224,768]{1,0:T(8,128)(2,1)S(1)}, bf16[224,768]{1,0:T(8,128)(2,1)S(1)}, u32[]{:S(2)}, u32[]{:S(2)}) collective-permute-start(bf16[224,768]{1,0:T(8,128)(2,1)S(1)} %pack.1.refs_0_), channel_id=1, source_target_pairs={{8,0},{16,8},{24,16},{28,24},{20,28},{12,20},{4,12},{0,4},{9,1},{1... | collective-permute-start | bytes 1032200 | tf_op jit(solution)/shard_map/ppermute | solution.py:42
  6.6 8.1 %collective-permute-start.16 = (bf16[128,768]{1,0:T(8,128)(2,1)}, bf16[128,768]{1,0:T(8,128)(2,1)S(1)}, u32[]{:S(2)}, u32[]{:S(2)}) collective-permute-start(bf16[128,768]{1,0:T(8,128)(2,1)} %tokens.3), channel_id=1, source_target_pairs={{0,2},{1,3},{2,0},{3,1},{4,6},{5,7},{6,4},{7,5},{8,10},{9,11},{10,... | collective-permute-start | bytes 589832 | tf_op jit(solution)/shard_map/ppermute | solution.py:47
  17.1 12.0 %collective-permute-start.12 = (bf16[256,768]{1,0:T(8,128)(2,1)S(1)}, bf16[256,768]{1,0:T(8,128)(2,1)S(1)}, u32[]{:S(2)}, u32[]{:S(2)}) collective-permute-start(bf16[256,768]{1,0:T(8,128)(2,1)S(1)} %pad_maximum_fusion.4), channel_id=1, source_target_pairs={{0,2},{1,3},{2,0},{3,1},{4,6},{5,7},{6,4},{7,5},{8,10},{9,11},{10,... | collective-permute-start | bytes 1179656 | tf_op jit(solution)/shard_map/ppermute | solution.py:47
  18.7 8.3 %collective-permute-start.1 = (bf16[224,768]{1,0:T(8,128)(2,1)S(1)}, bf16[224,768]{1,0:T(8,128)(2,1)S(1)}, u32[]{:S(2)}, u32[]{:S(2)}) collective-permute-start(bf16[224,768]{1,0:T(8,128)(2,1)S(1)} %collective-permute-done.refs_1_), channel_id=1, source_target_pairs={{0,8},{8,16},{16,24},{24,28},{28,20},{20,12},{12,4},{4,0},{1,9},{9... | collective-permute-start | bytes 1032200 | tf_op jit(solution)/shard_map/ppermute | solution.py:37
  20.3 8.3 %collective-permute-start.4 = (bf16[224,768]{1,0:T(8,128)(2,1)S(1)}, bf16[224,768]{1,0:T(8,128)(2,1)S(1)}, u32[]{:S(2)}, u32[]{:S(2)}) collective-permute-start(bf16[224,768]{1,0:T(8,128)(2,1)S(1)} %collective-permute-done.3.refs_2_), channel_id=1, source_target_pairs={{8,0},{16,8},{24,16},{28,24},{20,28},{12,20},{4,12},{0,4},{9,1},{1... | collective-permute-start | bytes 1032200 | tf_op jit(solution)/shard_map/ppermute | solution.py:42
  27.0 8.2 %collective-permute-start.2 = (bf16[224,768]{1,0:T(8,128)(2,1)S(1)}, bf16[224,768]{1,0:T(8,128)(2,1)S(1)}, u32[]{:S(2)}, u32[]{:S(2)}) collective-permute-start(bf16[224,768]{1,0:T(8,128)(2,1)S(1)} %collective-permute-done.1.refs_3_), channel_id=1, source_target_pairs={{0,8},{8,16},{16,24},{24,28},{28,20},{20,12},{12,4},{4,0},{1,9},{9... | collective-permute-start | bytes 1032200 | tf_op jit(solution)/shard_map/ppermute | solution.py:37
  28.6 8.2 %collective-permute-start.5 = (bf16[224,768]{1,0:T(8,128)(2,1)S(1)}, bf16[224,768]{1,0:T(8,128)(2,1)S(1)}, u32[]{:S(2)}, u32[]{:S(2)}) collective-permute-start(bf16[224,768]{1,0:T(8,128)(2,1)S(1)} %collective-permute-done.4.refs_4_), channel_id=1, source_target_pairs={{8,0},{16,8},{24,16},{28,24},{20,28},{12,20},{4,12},{0,4},{9,1},{1... | collective-permute-start | bytes 1032200 | tf_op jit(solution)/shard_map/ppermute | solution.py:42
  29.2 10.2 %collective-permute-start.13 = (bf16[256,768]{1,0:T(8,128)(2,1)S(1)}, bf16[256,768]{1,0:T(8,128)(2,1)S(1)}, u32[]{:S(2)}, u32[]{:S(2)}) collective-permute-start(bf16[256,768]{1,0:T(8,128)(2,1)S(1)} %pad_maximum_fusion.5), channel_id=1, source_target_pairs={{0,2},{1,3},{2,0},{3,1},{4,6},{5,7},{6,4},{7,5},{8,10},{9,11},{10,... | collective-permute-start | bytes 1179656 | tf_op jit(solution)/shard_map/ppermute | solution.py:47
  35.2 7.4 %collective-permute-start.10 = (bf16[112,768]{1,0:T(8,128)(2,1)S(1)}, bf16[112,768]{1,0:T(8,128)(2,1)S(1)}, u32[]{:S(2)}, u32[]{:S(2)}) collective-permute-start(bf16[112,768]{1,0:T(8,128)(2,1)S(1)} %slice.180), channel_id=1, source_target_pairs={{0,8},{8,16},{16,24},{24,28},{28,20},{20,12},{12,4},{4,0},{1,9},{9... | collective-permute-start | bytes 516104 | tf_op jit(solution)/shard_map/ppermute | solution.py:37
  36.9 7.4 %collective-permute-start.11 = (bf16[112,768]{1,0:T(8,128)(2,1)S(1)}, bf16[112,768]{1,0:T(8,128)(2,1)S(1)}, u32[]{:S(2)}, u32[]{:S(2)}) collective-permute-start(bf16[112,768]{1,0:T(8,128)(2,1)S(1)} %slice.181), channel_id=1, source_target_pairs={{8,0},{16,8},{24,16},{28,24},{20,28},{12,20},{4,12},{0,4},{9,1},{1... | collective-permute-start | bytes 516104 | tf_op jit(solution)/shard_map/ppermute | solution.py:42
  37.4 11.6 %collective-permute-start.6 = (bf16[96,2304]{1,0:T(8,128)(2,1)S(1)}, bf16[96,2304]{1,0:T(8,128)(2,1)S(1)}, u32[]{:S(2)}, u32[]{:S(2)}) collective-permute-start(bf16[96,2304]{1,0:T(8,128)(2,1)S(1)} %pad_maximum_fusion.1.refs_0_), channel_id=1, source_target_pairs={{0,8},{8,16},{16,24},{24,28},{28,20},{20,12},{12,4},{4,0},{1,9},{9... | collective-permute-start | bytes 1327112 | tf_op jit(solution)/shard_map/ppermute | solution.py:37
  38.9 10.1 %collective-permute-start.7 = (bf16[96,2304]{1,0:T(8,128)(2,1)S(1)}, bf16[96,2304]{1,0:T(8,128)(2,1)S(1)}, u32[]{:S(2)}, u32[]{:S(2)}) collective-permute-start(bf16[96,2304]{1,0:T(8,128)(2,1)S(1)} %pad_maximum_fusion.1.refs_0_), channel_id=1, source_target_pairs={{8,0},{16,8},{24,16},{28,24},{20,28},{12,20},{4,12},{0,4},{9,1},{1... | collective-permute-start | bytes 1327112 | tf_op jit(solution)/shard_map/ppermute | solution.py:42
  39.5 11.6 %collective-permute-start.14 = (bf16[256,768]{1,0:T(8,128)(2,1)S(1)}, bf16[256,768]{1,0:T(8,128)(2,1)S(1)}, u32[]{:S(2)}, u32[]{:S(2)}) collective-permute-start(bf16[256,768]{1,0:T(8,128)(2,1)S(1)} %pad_maximum_fusion.6), channel_id=1, source_target_pairs={{0,2},{1,3},{2,0},{3,1},{4,6},{5,7},{6,4},{7,5},{8,10},{9,11},{10,... | collective-permute-start | bytes 1179656 | tf_op jit(solution)/shard_map/ppermute | solution.py:47
  44.2 2.0 collective-permute-start.17
  44.2 7.0 %collective-permute-start.19 = (bf16[512,768]{1,0:T(8,128)(2,1)S(1)}, bf16[512,768]{1,0:T(8,128)(2,1)S(1)}, u32[]{:S(2)}, u32[]{:S(2)}) collective-permute-start(bf16[512,768]{1,0:T(8,128)(2,1)S(1)} %constant_dynamic-update-slice_fusion.refs_0_), channel_id=1, source_target_pairs={{0,1},{1,0},{2,3},{3,2},{4,5},{5,4},{6,7},{7,6},{8,9},{9,8},{10,11... | collective-permute-start | bytes 2359304 | tf_op jit(solution)/shard_map/ppermute | solution.py:47
  49.0 14.1 %collective-permute-start.18 = (bf16[512,768]{1,0:T(8,128)(2,1)S(1)}, bf16[512,768]{1,0:T(8,128)(2,1)S(1)}, u32[]{:S(2)}, u32[]{:S(2)}) collective-permute-start(bf16[512,768]{1,0:T(8,128)(2,1)S(1)} %constant_dynamic-update-slice_fusion.5.refs_0_), channel_id=1, source_target_pairs={{0,1},{1,0},{2,3},{3,2},{4,5},{5,4},{6,7},{7,6},{8,9},{9,8},{10,11... | collective-permute-start | bytes 2359304 | tf_op jit(solution)/shard_map/ppermute | solution.py:47
  49.1 18.4 %collective-permute-start.8 = (bf16[96,2304]{1,0:T(8,128)(2,1)S(1)}, bf16[96,2304]{1,0:T(8,128)(2,1)S(1)}, u32[]{:S(2)}, u32[]{:S(2)}) collective-permute-start(bf16[96,2304]{1,0:T(8,128)(2,1)S(1)} %collective-permute-done.6.refs_1_), channel_id=1, source_target_pairs={{0,8},{8,16},{16,24},{24,28},{28,20},{20,12},{12,4},{4,0},{1,9},{9... | collective-permute-start | bytes 1327112 | tf_op jit(solution)/shard_map/ppermute | solution.py:37
  50.7 16.8 %collective-permute-start.9 = (bf16[96,2304]{1,0:T(8,128)(2,1)S(1)}, bf16[96,2304]{1,0:T(8,128)(2,1)S(1)}, u32[]{:S(2)}, u32[]{:S(2)}) collective-permute-start(bf16[96,2304]{1,0:T(8,128)(2,1)S(1)} %collective-permute-done.7.refs_2_), channel_id=1, source_target_pairs={{8,0},{16,8},{24,16},{28,24},{20,28},{12,20},{4,12},{0,4},{9,1},{1... | collective-permute-start | bytes 1327112 | tf_op jit(solution)/shard_map/ppermute | solution.py:42
  55.6 12.0 %collective-permute-start.21 = (bf16[512,768]{1,0:T(8,128)(2,1)S(1)}, bf16[512,768]{1,0:T(8,128)(2,1)S(1)}, u32[]{:S(2)}, u32[]{:S(2)}) collective-permute-start(bf16[512,768]{1,0:T(8,128)(2,1)S(1)} %constant_dynamic-update-slice_fusion.10.refs_0_), channel_id=1, source_target_pairs={{0,1},{1,0},{2,3},{3,2},{4,5},{5,4},{6,7},{7,6},{8,9},{9,8},{10,11... | collective-permute-start | bytes 2359304 | tf_op jit(solution)/shard_map/ppermute | solution.py:47
  55.7 7.4 %collective-permute-start.15 = (bf16[128,768]{1,0:T(8,128)(2,1)S(1)}, bf16[128,768]{1,0:T(8,128)(2,1)S(1)}, u32[]{:S(2)}, u32[]{:S(2)}) collective-permute-start(bf16[128,768]{1,0:T(8,128)(2,1)S(1)} %pad_maximum_fusion.9), channel_id=1, source_target_pairs={{0,2},{1,3},{2,0},{3,1},{4,6},{5,7},{6,4},{7,5},{8,10},{9,11},{10,... | collective-permute-start | bytes 589832 | tf_op jit(solution)/shard_map/ppermute | solution.py:47
  67.5 4.4 %collective-permute-start.20 = (bf16[256,768]{1,0:T(8,128)(2,1)S(1)}, bf16[256,768]{1,0:T(8,128)(2,1)S(1)}, u32[]{:S(2)}, u32[]{:S(2)}) collective-permute-start(bf16[256,768]{1,0:T(8,128)(2,1)S(1)} %pad_maximum_fusion.7.refs_0_), channel_id=1, source_target_pairs={{0,1},{1,0},{2,3},{3,2},{4,5},{5,4},{6,7},{7,6},{8,9},{9,8},{10,11... | collective-permute-start | bytes 1179656 | tf_op jit(solution)/shard_map/ppermute | solution.py:47
  75.1 2.6 %collective-permute-start.26 = (bf16[256,768]{1,0:T(8,128)(2,1)S(1)}, bf16[256,768]{1,0:T(8,128)(2,1)S(1)}, u32[]{:S(2)}, u32[]{:S(2)}) collective-permute-start(bf16[256,768]{1,0:T(8,128)(2,1)S(1)} %get-tuple-element.187), channel_id=1, source_target_pairs={{0,1},{1,0},{2,3},{3,2},{4,5},{5,4},{6,7},{7,6},{8,9},{9,8},{10,11... | collective-permute-start | bytes 1179656 | tf_op jit(solution)/shard_map/ppermute | solution.py:47
  75.6 12.1 %collective-permute-start.22 = (bf16[96,2304]{1,0:T(8,128)(2,1)S(1)}, bf16[96,2304]{1,0:T(8,128)(2,1)S(1)}, u32[]{:S(2)}, u32[]{:S(2)}) collective-permute-start(bf16[96,2304]{1,0:T(8,128)(2,1)S(1)} %collective-permute-done.8.refs_3_), channel_id=1, source_target_pairs={{0,8},{8,16},{16,24},{24,28},{28,20},{20,12},{12,4},{4,0},{1,9},{9... | collective-permute-start | bytes 1327112 | tf_op jit(solution)/shard_map/ppermute | solution.py:37
  77.2 12.2 %collective-permute-start.23 = (bf16[96,2304]{1,0:T(8,128)(2,1)S(1)}, bf16[96,2304]{1,0:T(8,128)(2,1)S(1)}, u32[]{:S(2)}, u32[]{:S(2)}) collective-permute-start(bf16[96,2304]{1,0:T(8,128)(2,1)S(1)} %collective-permute-done.9.refs_4_), channel_id=1, source_target_pairs={{8,0},{16,8},{24,16},{28,24},{20,28},{12,20},{4,12},{0,4},{9,1},{1... | collective-permute-start | bytes 1327112 | tf_op jit(solution)/shard_map/ppermute | solution.py:42
  77.7 6.6 %collective-permute-start.27 = (bf16[128,768]{1,0:T(8,128)(2,1)S(1)}, bf16[128,768]{1,0:T(8,128)(2,1)S(1)}, u32[]{:S(2)}, u32[]{:S(2)}) collective-permute-start(bf16[128,768]{1,0:T(8,128)(2,1)S(1)} %add_convert_fusion.9), channel_id=1, source_target_pairs={{0,2},{1,3},{2,0},{3,1},{4,6},{5,7},{6,4},{7,5},{8,10},{9,11},{10,... | collective-permute-start | bytes 589832 | tf_op jit(solution)/shard_map/ppermute | solution.py:47
  85.5 5.7 %collective-permute-start.28 = (bf16[128,768]{1,0:T(8,128)(2,1)S(1)}, bf16[128,768]{1,0:T(8,128)(2,1)S(1)}, u32[]{:S(2)}, u32[]{:S(2)}) collective-permute-start(bf16[128,768]{1,0:T(8,128)(2,1)S(1)} %get-tuple-element.188.refs_9_.refs_0_), channel_id=1, source_target_pairs={{0,2},{1,3},{2,0},{3,1},{4,6},{5,7},{6,4},{7,5},{8,10},{9,11},{10,... | collective-permute-start | bytes 589832 | tf_op jit(solution)/shard_map/ppermute | solution.py:47
  87.8 6.6 %collective-permute-start.24 = (bf16[48,2304]{1,0:T(8,128)(2,1)S(1)}, bf16[48,2304]{1,0:T(8,128)(2,1)S(1)}, u32[]{:S(2)}, u32[]{:S(2)}) collective-permute-start(bf16[48,2304]{1,0:T(8,128)(2,1)S(1)} %slice.186), channel_id=1, source_target_pairs={{0,8},{8,16},{16,24},{24,28},{28,20},{20,12},{12,4},{4,0},{1,9},{9... | collective-permute-start | bytes 663560 | tf_op jit(solution)/shard_map/ppermute | solution.py:37
  89.4 6.6 %collective-permute-start.25 = (bf16[48,2304]{1,0:T(8,128)(2,1)S(1)}, bf16[48,2304]{1,0:T(8,128)(2,1)S(1)}, u32[]{:S(2)}, u32[]{:S(2)}) collective-permute-start(bf16[48,2304]{1,0:T(8,128)(2,1)S(1)} %slice.187), channel_id=1, source_target_pairs={{8,0},{16,8},{24,16},{28,24},{20,28},{12,20},{4,12},{0,4},{9,1},{1... | collective-permute-start | bytes 663560 | tf_op jit(solution)/shard_map/ppermute | solution.py:42
  90.2 5.8 %collective-permute-start.29 = (bf16[128,768]{1,0:T(8,128)(2,1)S(1)}, bf16[128,768]{1,0:T(8,128)(2,1)S(1)}, u32[]{:S(2)}, u32[]{:S(2)}) collective-permute-start(bf16[128,768]{1,0:T(8,128)(2,1)S(1)} %get-tuple-element.188.refs_9_.refs_0_), channel_id=1, source_target_pairs={{0,1},{1,0},{2,3},{3,2},{4,5},{5,4},{6,7},{7,6},{8,9},{9,8},{10,11... | collective-permute-start | bytes 589832 | tf_op jit(solution)/shard_map/ppermute | solution.py:47
  91.2 4.8 %collective-permute-start.30 = (bf16[128,768]{1,0:T(8,128)(2,1)S(1)}, bf16[128,768]{1,0:T(8,128)(2,1)S(1)}, u32[]{:S(2)}, u32[]{:S(2)}) collective-permute-start(bf16[128,768]{1,0:T(8,128)(2,1)S(1)} %collective-permute-done.28.refs_10_.refs_1_), channel_id=1, source_target_pairs={{0,1},{1,0},{2,3},{3,2},{4,5},{5,4},{6,7},{7,6},{8,9},{9,8},{10,11... | collective-permute-start | bytes 589832 | tf_op jit(solution)/shard_map/ppermute | solution.py:47
  99.4 1.8 collective-permute-start.31
  101.2 7.0 %collective-permute-start.32 = (bf16[128,768]{1,0:T(8,128)(2,1)S(1)}, bf16[128,768]{1,0:T(8,128)(2,1)S(1)}, u32[]{:S(2)}, u32[]{:S(2)}) collective-permute-start(bf16[128,768]{1,0:T(8,128)(2,1)S(1)} %add_convert_fusion.8), channel_id=1, source_target_pairs={{0,2},{1,3},{2,0},{3,1},{4,6},{5,7},{6,4},{7,5},{8,10},{9,11},{10,... | collective-permute-start | bytes 589832 | tf_op jit(solution)/shard_map/ppermute | solution.py:47
  109.4 6.1 %collective-permute-start.33 = (bf16[128,768]{1,0:T(8,128)(2,1)S(1)}, bf16[128,768]{1,0:T(8,128)(2,1)S(1)}, u32[]{:S(2)}, u32[]{:S(2)}) collective-permute-start(bf16[128,768]{1,0:T(8,128)(2,1)S(1)} %get-tuple-element.194.refs_0_.refs_4_), channel_id=1, source_target_pairs={{0,2},{1,3},{2,0},{3,1},{4,6},{5,7},{6,4},{7,5},{8,10},{9,11},{10,... | collective-permute-start | bytes 589832 | tf_op jit(solution)/shard_map/ppermute | solution.py:47
  109.9 5.6 %collective-permute-start.34 = (bf16[128,768]{1,0:T(8,128)(2,1)S(1)}, bf16[128,768]{1,0:T(8,128)(2,1)S(1)}, u32[]{:S(2)}, u32[]{:S(2)}) collective-permute-start(bf16[128,768]{1,0:T(8,128)(2,1)S(1)} %get-tuple-element.194.refs_0_.refs_4_), channel_id=1, source_target_pairs={{0,1},{1,0},{2,3},{3,2},{4,5},{5,4},{6,7},{7,6},{8,9},{9,8},{10,11... | collective-permute-start | bytes 589832 | tf_op jit(solution)/shard_map/ppermute | solution.py:47
  124.8 8.2 %collective-permute-start.42 = (bf16[48,2304]{1,0:T(8,128)(2,1)S(1)}, bf16[48,2304]{1,0:T(8,128)(2,1)S(1)}, u32[]{:S(2)}, u32[]{:S(2)}) collective-permute-start(bf16[48,2304]{1,0:T(8,128)(2,1)S(1)} %get-tuple-element.208), channel_id=1, source_target_pairs={{8,0},{16,8},{24,16},{28,24},{20,28},{12,20},{4,12},{0,4},{9,1},{1... | collective-permute-start | bytes 663560 | tf_op jit(solution)/shard_map/ppermute | solution.py:42
  125.4 6.7 %collective-permute-start.37 = (bf16[128,768]{1,0:T(8,128)(2,1)S(1)}, bf16[128,768]{1,0:T(8,128)(2,1)S(1)}, u32[]{:S(2)}, u32[]{:S(2)}) collective-permute-start(bf16[128,768]{1,0:T(8,128)(2,1)S(1)} %add_convert_fusion.7), channel_id=1, source_target_pairs={{0,2},{1,3},{2,0},{3,1},{4,6},{5,7},{6,4},{7,5},{8,10},{9,11},{10,... | collective-permute-start | bytes 589832 | tf_op jit(solution)/shard_map/ppermute | solution.py:47
  125.9 7.7 %collective-permute-start.41 = (bf16[48,2304]{1,0:T(8,128)(2,1)S(1)}, bf16[48,2304]{1,0:T(8,128)(2,1)S(1)}, u32[]{:S(2)}, u32[]{:S(2)}) collective-permute-start(bf16[48,2304]{1,0:T(8,128)(2,1)S(1)} %get-tuple-element.207), channel_id=1, source_target_pairs={{0,8},{8,16},{16,24},{24,28},{28,20},{20,12},{12,4},{4,0},{1,9},{9... | collective-permute-start | bytes 663560 | tf_op jit(solution)/shard_map/ppermute | solution.py:37
  132.4 6.4 %collective-permute-start.38 = (bf16[144,768]{1,0:T(8,128)(2,1)S(1)}, bf16[144,768]{1,0:T(8,128)(2,1)S(1)}, u32[]{:S(2)}, u32[]{:S(2)}) collective-permute-start(bf16[144,768]{1,0:T(8,128)(2,1)S(1)} %get-tuple-element.217.refs_0_.refs_2_), channel_id=1, source_target_pairs={{0,2},{1,3},{2,0},{3,1},{4,6},{5,7},{6,4},{7,5},{8,10},{9,11},{10,... | collective-permute-start | bytes 663560 | tf_op jit(solution)/shard_map/ppermute | solution.py:47
  133.0 7.5 %collective-permute-start.39 = (bf16[144,768]{1,0:T(8,128)(2,1)S(1)}, bf16[144,768]{1,0:T(8,128)(2,1)S(1)}, u32[]{:S(2)}, u32[]{:S(2)}) collective-permute-start(bf16[144,768]{1,0:T(8,128)(2,1)S(1)} %get-tuple-element.217.refs_0_.refs_2_), channel_id=1, source_target_pairs={{0,1},{1,0},{2,3},{3,2},{4,5},{5,4},{6,7},{7,6},{8,9},{9,8},{10,11... | collective-permute-start | bytes 663560 | tf_op jit(solution)/shard_map/ppermute | solution.py:47
  133.1 22.2 %collective-permute-start.48 = (bf16[96,2304]{1,0:T(8,128)(2,1)S(1)}, bf16[96,2304]{1,0:T(8,128)(2,1)S(1)}, u32[]{:S(2)}, u32[]{:S(2)}) collective-permute-start(bf16[96,2304]{1,0:T(8,128)(2,1)S(1)} %pad_maximum_fusion.3), channel_id=1, source_target_pairs={{8,0},{16,8},{24,16},{28,24},{20,28},{12,20},{4,12},{0,4},{9,1},{1... | collective-permute-start | bytes 1327112 | tf_op jit(solution)/shard_map/ppermute | solution.py:42
  138.9 20.6 %collective-permute-start.47 = (bf16[96,2304]{1,0:T(8,128)(2,1)S(1)}, bf16[96,2304]{1,0:T(8,128)(2,1)S(1)}, u32[]{:S(2)}, u32[]{:S(2)}) collective-permute-start(bf16[96,2304]{1,0:T(8,128)(2,1)S(1)} %pad_maximum_fusion.2), channel_id=1, source_target_pairs={{0,8},{8,16},{16,24},{24,28},{28,20},{20,12},{12,4},{4,0},{1,9},{9... | collective-permute-start | bytes 1327112 | tf_op jit(solution)/shard_map/ppermute | solution.py:37
  141.0 16.5 %collective-permute-start.43 = (bf16[272,512]{1,0:T(8,128)(2,1)S(1)}, bf16[272,512]{1,0:T(8,128)(2,1)S(1)}, u32[]{:S(2)}, u32[]{:S(2)}) collective-permute-start(bf16[272,512]{1,0:T(8,128)(2,1)S(1)} %prepare.1.g.refs_0_), channel_id=1, source_target_pairs={{0,8},{8,16},{16,24},{24,28},{28,20},{20,12},{12,4},{4,0},{1,9},{9... | collective-permute-start | bytes 835592 | tf_op jit(solution)/shard_map/ppermute | solution.py:37
  142.5 15.0 %collective-permute-start.44 = (bf16[272,512]{1,0:T(8,128)(2,1)S(1)}, bf16[272,512]{1,0:T(8,128)(2,1)S(1)}, u32[]{:S(2)}, u32[]{:S(2)}) collective-permute-start(bf16[272,512]{1,0:T(8,128)(2,1)S(1)} %prepare.1.g.refs_0_), channel_id=1, source_target_pairs={{8,0},{16,8},{24,16},{28,24},{20,28},{12,20},{4,12},{0,4},{9,1},{1... | collective-permute-start | bytes 835592 | tf_op jit(solution)/shard_map/ppermute | solution.py:42
  157.5 8.5 %collective-permute-start.45 = (bf16[272,512]{1,0:T(8,128)(2,1)S(1)}, bf16[272,512]{1,0:T(8,128)(2,1)S(1)}, u32[]{:S(2)}, u32[]{:S(2)}) collective-permute-start(bf16[272,512]{1,0:T(8,128)(2,1)S(1)} %collective-permute-done.43.refs_0_), channel_id=1, source_target_pairs={{0,8},{8,16},{16,24},{24,28},{28,20},{20,12},{12,4},{4,0},{1,9},{9... | collective-permute-start | bytes 835592 | tf_op jit(solution)/shard_map/ppermute | solution.py:37
  159.0 8.0 %collective-permute-start.46 = (bf16[272,512]{1,0:T(8,128)(2,1)S(1)}, bf16[272,512]{1,0:T(8,128)(2,1)S(1)}, u32[]{:S(2)}, u32[]{:S(2)}) collective-permute-start(bf16[272,512]{1,0:T(8,128)(2,1)S(1)} %collective-permute-done.44.refs_1_), channel_id=1, source_target_pairs={{8,0},{16,8},{24,16},{28,24},{20,28},{12,20},{4,12},{0,4},{9,1},{1... | collective-permute-start | bytes 835592 | tf_op jit(solution)/shard_map/ppermute | solution.py:42
  167.0 7.1 %collective-permute-start.49 = (bf16[272,512]{1,0:T(8,128)(2,1)S(1)}, bf16[272,512]{1,0:T(8,128)(2,1)S(1)}, u32[]{:S(2)}, u32[]{:S(2)}) collective-permute-start(bf16[272,512]{1,0:T(8,128)(2,1)S(1)} %collective-permute-done.45.refs_0_), channel_id=1, source_target_pairs={{0,8},{8,16},{16,24},{24,28},{28,20},{20,12},{12,4},{4,0},{1,9},{9... | collective-permute-start | bytes 835592 | tf_op jit(solution)/shard_map/ppermute | solution.py:37
  168.5 6.8 %collective-permute-start.50 = (bf16[272,512]{1,0:T(8,128)(2,1)S(1)}, bf16[272,512]{1,0:T(8,128)(2,1)S(1)}, u32[]{:S(2)}, u32[]{:S(2)}) collective-permute-start(bf16[272,512]{1,0:T(8,128)(2,1)S(1)} %collective-permute-done.46.refs_1_), channel_id=1, source_target_pairs={{8,0},{16,8},{24,16},{28,24},{20,28},{12,20},{4,12},{0,4},{9,1},{1... | collective-permute-start | bytes 835592 | tf_op jit(solution)/shard_map/ppermute | solution.py:42
  175.3 6.1 %collective-permute-start.51 = (bf16[272,256]{1,0:T(8,128)(2,1)S(1)}, bf16[272,256]{1,0:T(8,128)(2,1)S(1)}, u32[]{:S(2)}, u32[]{:S(2)}) collective-permute-start(bf16[272,256]{1,0:T(8,128)(2,1)S(1)} %slice.166), channel_id=1, source_target_pairs={{0,8},{8,16},{16,24},{24,28},{28,20},{20,12},{12,4},{4,0},{1,9},{9... | collective-permute-start | bytes 417800 | tf_op jit(solution)/shard_map/ppermute | solution.py:37
  176.6 5.1 %collective-permute-start.52 = (bf16[272,256]{1,0:T(8,128)(2,1)S(1)}, bf16[272,256]{1,0:T(8,128)(2,1)S(1)}, u32[]{:S(2)}, u32[]{:S(2)}) collective-permute-start(bf16[272,256]{1,0:T(8,128)(2,1)S(1)} %slice.167), channel_id=1, source_target_pairs={{8,0},{16,8},{24,16},{28,24},{20,28},{12,20},{4,12},{0,4},{9,1},{1... | collective-permute-start | bytes 417800 | tf_op jit(solution)/shard_map/ppermute | solution.py:42
  186.1 5.3 %collective-permute-start.59 = (bf16[48,768]{1,0:T(8,128)(2,1)S(1)}, bf16[48,768]{1,0:T(8,128)(2,1)S(1)}, u32[]{:S(2)}, u32[]{:S(2)}) collective-permute-start(bf16[48,768]{1,0:T(8,128)(2,1)S(1)} %get-tuple-element.256), channel_id=1, source_target_pairs={{8,0},{16,8},{24,16},{28,24},{20,28},{12,20},{4,12},{0,4},{9,1},{1... | collective-permute-start | bytes 221192 | tf_op jit(solution)/shard_map/ppermute | solution.py:42
  186.9 19.6 %collective-permute-start.65 = (bf16[96,2304]{1,0:T(8,128)(2,1)S(1)}, bf16[96,2304]{1,0:T(8,128)(2,1)S(1)}, u32[]{:S(2)}, u32[]{:S(2)}) collective-permute-start(bf16[96,2304]{1,0:T(8,128)(2,1)S(1)} %add_convert_fusion.2), channel_id=1, source_target_pairs={{8,0},{16,8},{24,16},{28,24},{20,28},{12,20},{4,12},{0,4},{9,1},{1... | collective-permute-start | bytes 1327112 | tf_op jit(solution)/shard_map/ppermute | solution.py:42
  187.5 19.7 %collective-permute-start.63 = (bf16[96,2304]{1,0:T(8,128)(2,1)S(1)}, bf16[96,2304]{1,0:T(8,128)(2,1)S(1)}, u32[]{:S(2)}, u32[]{:S(2)}) collective-permute-start(bf16[96,2304]{1,0:T(8,128)(2,1)S(1)} %add_convert_fusion.3), channel_id=1, source_target_pairs={{0,8},{8,16},{16,24},{24,28},{28,20},{20,12},{12,4},{4,0},{1,9},{9... | collective-permute-start | bytes 1327112 | tf_op jit(solution)/shard_map/ppermute | solution.py:37
  189.0 9.3 %collective-permute-start.55 = (bf16[48,768]{1,0:T(8,128)(2,1)S(1)}, bf16[48,768]{1,0:T(8,128)(2,1)S(1)}, u32[]{:S(2)}, u32[]{:S(2)}) collective-permute-start(bf16[48,768]{1,0:T(8,128)(2,1)S(1)} %get-tuple-element.251), channel_id=1, source_target_pairs={{0,8},{8,16},{16,24},{24,28},{28,20},{20,12},{12,4},{4,0},{1,9},{9... | collective-permute-start | bytes 221192 | tf_op jit(solution)/shard_map/ppermute | solution.py:37
  190.2 22.9 %collective-permute-start.53 = (bf16[256,768]{1,0:T(8,128)(2,1)S(1)}, bf16[256,768]{1,0:T(8,128)(2,1)S(1)}, u32[]{:S(2)}, u32[]{:S(2)}) collective-permute-start(bf16[256,768]{1,0:T(8,128)(2,1)S(1)} %get-tuple-element.249), channel_id=1, source_target_pairs={{0,1},{1,0},{2,3},{3,2},{4,5},{5,4},{6,7},{7,6},{8,9},{9,8},{10,11... | collective-permute-start | bytes 1179656 | tf_op jit(solution)/shard_map/ppermute | solution.py:47
  191.4 8.6 %collective-permute-start.60 = (bf16[96,768]{1,0:T(8,128)(2,1)S(1)}, bf16[96,768]{1,0:T(8,128)(2,1)S(1)}, u32[]{:S(2)}, u32[]{:S(2)}) collective-permute-start(bf16[96,768]{1,0:T(8,128)(2,1)S(1)} %pad_maximum_fusion.11), channel_id=1, source_target_pairs={{8,0},{16,8},{24,16},{28,24},{20,28},{12,20},{4,12},{0,4},{9,1},{1... | collective-permute-start | bytes 442376 | tf_op jit(solution)/shard_map/ppermute | solution.py:42
  198.3 6.5 %collective-permute-start.56 = (bf16[96,768]{1,0:T(8,128)(2,1)S(1)}, bf16[96,768]{1,0:T(8,128)(2,1)S(1)}, u32[]{:S(2)}, u32[]{:S(2)}) collective-permute-start(bf16[96,768]{1,0:T(8,128)(2,1)S(1)} %pad_maximum_fusion.10), channel_id=1, source_target_pairs={{0,8},{8,16},{16,24},{24,28},{28,20},{20,12},{12,4},{4,0},{1,9},{9... | collective-permute-start | bytes 442376 | tf_op jit(solution)/shard_map/ppermute | solution.py:37
  200.0 8.9 %collective-permute-start.61 = (bf16[96,768]{1,0:T(8,128)(2,1)S(1)}, bf16[96,768]{1,0:T(8,128)(2,1)S(1)}, u32[]{:S(2)}, u32[]{:S(2)}) collective-permute-start(bf16[96,768]{1,0:T(8,128)(2,1)S(1)} %add_convert_fusion.11), channel_id=1, source_target_pairs={{8,0},{16,8},{24,16},{28,24},{20,28},{12,20},{4,12},{0,4},{9,1},{1... | collective-permute-start | bytes 442376 | tf_op jit(solution)/shard_map/ppermute | solution.py:42
  204.9 6.5 %collective-permute-start.57 = (bf16[96,768]{1,0:T(8,128)(2,1)S(1)}, bf16[96,768]{1,0:T(8,128)(2,1)S(1)}, u32[]{:S(2)}, u32[]{:S(2)}) collective-permute-start(bf16[96,768]{1,0:T(8,128)(2,1)S(1)} %add_convert_fusion.13), channel_id=1, source_target_pairs={{0,8},{8,16},{16,24},{24,28},{28,20},{20,12},{12,4},{4,0},{1,9},{9... | collective-permute-start | bytes 442376 | tf_op jit(solution)/shard_map/ppermute | solution.py:37
  206.6 13.1 %collective-permute-start.66 = (bf16[96,2304]{1,0:T(8,128)(2,1)S(1)}, bf16[96,2304]{1,0:T(8,128)(2,1)S(1)}, u32[]{:S(2)}, u32[]{:S(2)}) collective-permute-start(bf16[96,2304]{1,0:T(8,128)(2,1)S(1)} %add_convert_fusion), channel_id=1, source_target_pairs={{8,0},{16,8},{24,16},{28,24},{20,28},{12,20},{4,12},{0,4},{9,1},{1... | collective-permute-start | bytes 1327112 | tf_op jit(solution)/shard_map/ppermute | solution.py:42
  207.3 12.4 %collective-permute-start.64 = (bf16[96,2304]{1,0:T(8,128)(2,1)S(1)}, bf16[96,2304]{1,0:T(8,128)(2,1)S(1)}, u32[]{:S(2)}, u32[]{:S(2)}) collective-permute-start(bf16[96,2304]{1,0:T(8,128)(2,1)S(1)} %add_convert_fusion.1), channel_id=1, source_target_pairs={{0,8},{8,16},{16,24},{24,28},{28,20},{20,12},{12,4},{4,0},{1,9},{9... | collective-permute-start | bytes 1327112 | tf_op jit(solution)/shard_map/ppermute | solution.py:37
  208.9 7.7 %collective-permute-start.62 = (bf16[96,768]{1,0:T(8,128)(2,1)S(1)}, bf16[96,768]{1,0:T(8,128)(2,1)S(1)}, u32[]{:S(2)}, u32[]{:S(2)}) collective-permute-start(bf16[96,768]{1,0:T(8,128)(2,1)S(1)} %add_convert_fusion.10), channel_id=1, source_target_pairs={{8,0},{16,8},{24,16},{28,24},{20,28},{12,20},{4,12},{0,4},{9,1},{1... | collective-permute-start | bytes 442376 | tf_op jit(solution)/shard_map/ppermute | solution.py:42
  211.5 6.3 %collective-permute-start.58 = (bf16[96,768]{1,0:T(8,128)(2,1)S(1)}, bf16[96,768]{1,0:T(8,128)(2,1)S(1)}, u32[]{:S(2)}, u32[]{:S(2)}) collective-permute-start(bf16[96,768]{1,0:T(8,128)(2,1)S(1)} %add_convert_fusion.12), channel_id=1, source_target_pairs={{0,8},{8,16},{16,24},{24,28},{28,20},{20,12},{12,4},{4,0},{1,9},{9... | collective-permute-start | bytes 442376 | tf_op jit(solution)/shard_map/ppermute | solution.py:37
  213.1 5.7 %collective-permute-start.54 = (bf16[128,768]{1,0:T(8,128)(2,1)S(1)}, bf16[128,768]{1,0:T(8,128)(2,1)S(1)}, u32[]{:S(2)}, u32[]{:S(2)}) collective-permute-start(bf16[128,768]{1,0:T(8,128)(2,1)S(1)} %add_convert_fusion.6), channel_id=1, source_target_pairs={{0,2},{1,3},{2,0},{3,1},{4,6},{5,7},{6,4},{7,5},{8,10},{9,11},{10,... | collective-permute-start | bytes 589832 | tf_op jit(solution)/shard_map/ppermute | solution.py:47
  (16 other events, 120.1 us)

commit v2 on v1

--- a/solution.py
+++ b/solution.py
@@ -120,16 +120,19 @@
         return [self.blocks[0], *self.moving]
 
 
-def col_pieces(v, *first):
-    side = col_swap(v, 2)
-    return [v, side, col_swap(v, 1), col_swap(after(side, first), 1)]
+def core_sum(near, far):
+    return (near.astype(F32) + col_swap(far, 1).astype(F32)).astype(BF)
 
 
 def col_exchange(near, far):
-    own = near.shape[0] // 2
-    other = col_swap(far, 1)
-    passed = (near[own:].astype(F32) + other[own:].astype(F32)).astype(BF)
-    return (near, other, col_swap(passed, 2)), passed
+    mine = core_sum(near, far)
+    return [mine, col_swap(mine, 2)]
+
+
+def col_sum(near, far):
+    mine = core_sum(near, far)
+    own = mine.shape[0] // 2
+    return mine[:own].astype(F32) + col_swap(mine[own:], 2).astype(F32)
 
 
 def whole(shape):
@@ -431,26 +434,31 @@
         - jnp.mean(scaled, axis=-1, keepdims=True)
         - normed * jnp.mean(scaled * normed, axis=-1, keepdims=True)
     )
-    sums = [jnp.sum(grad_out * normed, axis=0, keepdims=True), jnp.sum(grad_out, axis=0, keepdims=True)]
-    return grad_in, sums
-
-
-def col_total(near, other, last):
-    own = last.shape[0]
-    return near[:own].astype(F32) + other[:own].astype(F32) + last[...].astype(F32)
-
-
-def first_norm_kernel(near, other, last, tokens, gain, bias, residual, hidden):
-    value = tokens[...].astype(F32) + col_total(near, other, last)
+    own = grad_out.shape[0] // 2
+
+    def total(v):
+        return jnp.sum(v[:own], axis=0, keepdims=True) + jnp.sum(v[own:], axis=0, keepdims=True)
+
+    return grad_in, (total(grad_out * normed), total(grad_out))
+
+
+def col_total(mine, other):
+    own = mine.shape[0] // 2
+    return mine[...].astype(F32) + jnp.concatenate([other[own:], other[:own]], axis=0).astype(F32)
+
+
+def first_norm_kernel(mine, other, tokens, gain, bias, residual, hidden):
+    value = tokens[...].astype(F32) + col_total(mine, other)
     residual[...] = value
     normed, _ = norm_parts(value)
     hidden[...] = (normed * gain[...] + bias[...]).astype(BF)
 
 
-def second_norm_kernel(near, other, last, residual, gain1, bias1, gain2, bias2, cotangent, result, grad, grad_bf, sums):
+def second_norm_kernel(mine, other, residual, gain1, bias1, gain2, bias2, cotangent, result, grad, grad_bf, sums):
     hidden = norm_parts(residual[...])[0] * gain1[...] + bias1[...]
-    normed, inverse = norm_parts(hidden + col_total(near, other, last))
-    result[...] = (normed * gain2[...] + bias2[...]).astype(BF)
+    normed, inverse = norm_parts(hidden + col_total(mine, other))
+    own = result.shape[0]
+    result[...] = (normed[:own] * gain2[...] + bias2[...]).astype(BF)
     value, (dgain, dbias) = norm_back(cotangent[...].astype(F32), normed, inverse, gain2[...])
     grad[...] = value
     grad_bf[...] = value.astype(BF)
@@ -458,18 +466,18 @@
     sums[1:2] = dbias
 
 
-def first_norm_back_kernel(near, other, last, residual, gain, grad2, sums2, grad, package):
+def first_norm_back_kernel(mine, other, residual, gain, grad2, sums2, grad, package):
     normed, inverse = norm_parts(residual[...])
-    grad_out = grad2[...] + col_total(near, other, last)
+    grad_out = grad2[...] + col_total(mine, other)
     value, (dgain, dbias) = norm_back(grad_out, normed, inverse, gain[...])
-    grad[...] = value
-    own = value.shape[0]
-    package[:own] = value.astype(BF)
+    grad[...] = value[: grad.shape[0]]
+    rows = value.shape[0]
+    package[:rows] = value.astype(BF)
     sums = jnp.concatenate([dgain, dbias, sums2[0:1], sums2[1:2]], axis=0)
     high = sums.astype(BF)
     low = (sums - high.astype(F32)).astype(BF)
     blank = jnp.zeros((8, sums.shape[1]), F32)
-    package[own:] = jnp.concatenate([high.astype(F32), low.astype(F32), blank], axis=0).astype(BF)
+    package[rows:] = jnp.concatenate([high.astype(F32), low.astype(F32), blank], axis=0).astype(BF)
 
 
 def stacked(refs, rows):
@@ -536,8 +544,8 @@
 
 
 def ffn_grad_kernel(units, n_blocks, starts, *refs):
-    hidden, g, (grads, inner) = refs[:4], refs[4:8], refs[8:10]
-    outs, held = refs[10 : 10 + n_blocks], refs[10 + n_blocks]
+    hidden, g, (grads, inner) = refs[:2], refs[2:4], refs[4:6]
+    outs, held = refs[6 : 6 + n_blocks], refs[6 + n_blocks]
     own = hidden[0].shape[0]
     turned = stacked(hidden, own).T
     for t in range(0, 2 * units, units):
@@ -546,9 +554,9 @@
     write_blocks(held, starts, outs)
 
 
-def prepare_kernel(heads, own, *refs):
-    pieces, (w_out, context, log_total, package) = refs[:4], refs[4:]
-    g = stacked(pieces, own)
+def prepare_kernel(heads, taken, *refs):
+    pieces, (w_out, context, log_total, package) = refs[:2], refs[2:]
+    g = stacked(pieces, taken)
     rows = HEAD + AUX
     grad = dot(w_out[...], g, NT).astype(BF)
     index = lax.broadcasted_iota(jnp.int32, (AUX, g.shape[0]), 0)
@@ -565,10 +573,10 @@
         package[h * rows + HEAD : (h + 1) * rows] = tail.astype(BF)
 
     def sums(piece):
-        both = piece[own : own + 16].astype(F32)
+        both = piece[taken : taken + 16].astype(F32)
         return both[:4] + both[4:8]
 
-    total = (sums(pieces[0]) + sums(pieces[1])) + (sums(pieces[2]) + sums(pieces[3]))
+    total = sums(pieces[0]) + sums(pieces[1])
     high = total.astype(BF).astype(F32)
     both = jnp.concatenate([high, total - high], axis=0)
     base = heads * rows
@@ -582,8 +590,8 @@
     return jnp.concatenate([first * cosine + second * sine, second * cosine - first * sine], axis=0)
 
 
-def early_grad_kernel(heads, own, n_x, slots, *refs):
-    x_refs, g_refs, refs = refs[:n_x], refs[n_x : n_x + 4], refs[n_x + 4 :]
+def early_grad_kernel(heads, taken, n_x, slots, *refs):
+    x_refs, g_refs, refs = refs[:n_x], refs[n_x : n_x + 2], refs[n_x + 2 :]
     grad_query, turn, context, mixed, held = refs
     half = HEAD // 2
     scale = 1.0 / math.sqrt(HEAD)
@@ -593,7 +601,7 @@
     x = stacked(x_refs, x_refs[0].shape[0])
     width = heads * HEAD
     held[:, :width] = dot(mixed[...], x, NN).T.astype(BF)
-    held[:, width:] = dot(context[...], stacked(g_refs, own), NN).T.astype(BF)
+    held[:, width:] = dot(context[...], stacked(g_refs, taken), NN).T.astype(BF)
 
 
 def late_grad_kernel(heads, n_x, n_blocks, slots, starts, *refs):
@@ -710,7 +718,8 @@
     early = jnp.concatenate([w_qkv.reshape(share, 3 * width), w_out.T], axis=1)
     late = jnp.concatenate([w_gate_up.reshape(share, 2 * units), w_down.T], axis=1)
 
-    pair = jnp.concatenate([tokens, col_swap(tokens, 2)], axis=0)
+    pair = tokens_pair = jnp.concatenate([tokens, col_swap(tokens, 2)], axis=0)
+    taken = pair.shape[0]
     if ring:
         place = cycle_place()
         half = share // 2
@@ -782,7 +791,11 @@
         late_ring.step(rounds[2])
         two = after(two, state[0])
         keys, values, queries, *state = middle(0, after(one, rounds[3]))
-        far = side(after(rounds[3], three))
+        both = [rows for v in after(rounds[3], three) for rows in token_rows(v)]
+        both = jnp.concatenate([*both, cotangent], axis=0)
+        swapped = col_swap(both, 2)
+        far = jnp.concatenate([both[:own], swapped[:own]], axis=0)
+        other_cotangent = swapped[own:]
         three = after(three, state[0])
         keys, values, queries, *state = middle(1, after(two, late_ring.done[0]))
         late_ring.step()
@@ -818,23 +831,26 @@
     near, far, context_bf, context, log_total = finished
 
     if ring:
-        late_ring.step(near)
+        late_ring.step()
+        near = after(near, late_ring.done[2])
+        late_ring.step()
     else:
         late_pieces = [lax.all_gather(late, "row", axis=0, tiled=True)]
 
+    if not ring:
+        other_cotangent = col_swap(cotangent, 2)
+    cotangent_pair = jnp.concatenate([cotangent, other_cotangent], axis=0)
     part = struct((group // 2, features), BF)
-    flat = struct((own, features), F32)
+    flat, flat_bf = struct((taken, features), F32), struct((taken, features), BF)
     residual1, hidden = call(
         first_norm_kernel,
         "first_norm",
-        [*col_exchange(near, far)[0], tokens, *gains[:2]],
-        [flat, struct((own, features), BF)],
+        [*col_exchange(near, far), after(tokens_pair, late_ring.done[3]) if ring else tokens_pair, *gains[:2]],
+        [flat, flat_bf],
     )
     if ring:
-        hidden_pieces = col_pieces(hidden, late_ring.done[2])
         late_pieces = [late, *late_ring.pieces()]
-    else:
-        hidden_pieces = col_pieces(hidden)
+    hidden_pieces = [hidden, col_swap(hidden, 1)]
     w_gu, w_dn, gate_up, inner, near, far = call(
         functools.partial(forward_kernel, len(late_pieces), units),
         "ffn_forward",
@@ -854,10 +870,10 @@
     result, grad_res2, grad_bf, sums2 = call(
         second_norm_kernel,
         "second_norm",
-        [*col_exchange(near, far)[0], residual1, *gains, cotangent],
-        [struct((own, features), BF), flat, struct((own, features), BF), struct((8, features), F32)],
-    )
-    grad_pieces = col_pieces(grad_bf)
+        [*col_exchange(near, far), residual1, *gains, cotangent_pair],
+        [struct((own, features), BF), flat, flat_bf, struct((8, features), F32)],
+    )
+    grad_pieces = [grad_bf, col_swap(grad_bf, 1)]
     grad_gate_up, near, far = call(
         functools.partial(backward_kernel, units),
         "ffn_backward",
@@ -866,8 +882,7 @@
         scratch=[pltpu.VMEM((group, features), BF)],
         flops=6 * group * features * units,
     )
-    exchanged, passed = col_exchange(near, far)
-    grad_gate_up = after(grad_gate_up, passed)
+    exchanged = col_exchange(near, far)
     outs = block_structs(features, 3 * units, ring)
     blocks = call(
         functools.partial(ffn_grad_kernel, units, len(outs)),
@@ -885,11 +900,11 @@
         first_norm_back_kernel,
         "first_norm_back",
         [*exchanged, residual1, gains[0], grad_res2, sums2],
-        [flat, struct((own + 16, features), BF)],
-    )
-    attn_pieces = after(col_pieces(package), sent)
+        [struct((own, features), F32), struct((taken + 16, features), BF)],
+    )
+    attn_pieces = after([package, col_swap(package, 1)], sent)
     (package,) = call(
-        functools.partial(prepare_kernel, heads, own),
+        functools.partial(prepare_kernel, heads, taken),
         "prepare",
         [*attn_pieces, full_out, context, log_total],
         [struct((heads * (HEAD + AUX) + 32, group), BF)],
@@ -908,7 +923,7 @@
     specs = [whole(a.shape) for a in args]
     specs[-2] = own_turn
     mixed_q, early_grad = call(
-        functools.partial(early_grad_kernel, heads, own, len(x_pieces)),
+        functools.partial(early_grad_kernel, heads, taken, len(x_pieces)),
         "early_grad",
         args,
         [struct((width, group), BF), struct((features, 2 * width), BF)],
@@ -983,7 +998,6 @@
     )
     late_sum = RowSum(blocks)
     late_sum = late_sum.terms()
-    near, other, last = col_exchange(near, far)[0]
     grad_gu, grad_dn = call(
         functools.partial(finish_ffn_kernel, units),
         "finish_ffn",
@@ -991,9 +1005,7 @@
         [struct((share, 2, units), F32), struct((units, share), F32)],
         cost=20.0,
     )
-    grad_tokens = grad_res1 + (
-        near[:own].astype(F32) + other[:own].astype(F32) + last.astype(F32)
-    )
+    grad_tokens = grad_res1 + col_sum(near, far)
     grad_mix, grad_out = call(
         functools.partial(finish_mix_kernel, width),
         "finish_mix",

time: 222 us -> 216 us (0.973)
  waiting for transfers between devices: 83.8 us -> 80.3 us
  starting transfers between devices: 53.4 us -> 51.1 us
    ppermute x27 -> x21, waiting for transfers between devices: 40.5 us -> 28.7 us  [col_swap(): return lax.ppermute(v, 'col', [(i, i ^ mask) for i in range(count)])]
    ppermute x20, waiting for transfers between devices: 9.14 us -> 16.2 us  [backward_hop(): lax.ppermute(v, 'row', [(CYCLE[(i + 1) % n], CYCLE[i]) for i in range(n)])]
    ppermute x27 -> x21, starting transfers between devices: 10.3 us -> 8.29 us  [col_swap(): return lax.ppermute(v, 'col', [(i, i ^ mask) for i in range(count)])]
    unnamed x34 -> x35, local copies, waits for them, and re-layouts: 3.69 us -> 4.64 us
  transfers between devices with their start and end apart: 67 -> 61, of which waited for: 31 -> 31; matrix products, arithmetic and copies ran while one was open for 5% -> 5% of each run, Pallas kernels for 21% -> 24%
where the time goes in v2:
time: 216 us
  waiting for transfers between devices  80.3 us (37%)
  Pallas kernels  66.8 us (31%)
  starting transfers between devices  51.1 us (24%)
  other arithmetic  7.19 us (3%)
  local copies, waits for them, and re-layouts  7.07 us (3%)
  between operations  3.49 us (2%)
    pallas_call x25, Pallas kernels, call(): pl.pallas_call(kernel, grid_spec=pltpu.PrefetchScalarGridSpec(num_scalar_...  66.8 us
    ppermute x20, waiting for transfers between devices, forward_hop(): lax.ppermute(v, 'row', [(CYCLE[i], CYCLE[(i + 1) % n]) for i in range(n)])  35.3 us
    ppermute x20, starting transfers between devices, forward_hop(): lax.ppermute(v, 'row', [(CYCLE[i], CYCLE[(i + 1) % n]) for i in range(n)])  32.8 us
    ppermute x21, waiting for transfers between devices, col_swap(): return lax.ppermute(v, 'col', [(i, i ^ mask) for i in range(count)])  28.7 us
    ppermute x20, waiting for transfers between devices, backward_hop(): lax.ppermute(v, 'row', [(CYCLE[(i + 1) % n], CYCLE[i]) for i in range(n)])  16.2 us
    ppermute x20, starting transfers between devices, backward_hop(): lax.ppermute(v, 'row', [(CYCLE[(i + 1) % n], CYCLE[i]) for i in range(n)])  10 us
    ppermute x21, starting transfers between devices, col_swap(): return lax.ppermute(v, 'col', [(i, i ^ mask) for i in range(count)])  8.29 us
    unnamed x35, local copies, waits for them, and re-layouts  4.64 us
  transfers between devices with their start and end apart: 61, of which 31 were waited for; matrix products, arithmetic and copies ran while one was open for 5% of the time, Pallas kernels for 24%

profile of v2, /device:TPU:0, one launch (start us, length us, event | category | flops | bytes accessed | tf_op | source)
XLA Modules:
  0.0 215.9 jit_solution(1975557299124165234)
XLA Ops:
  3.5 3.1 %collective-permute-start = (bf16[224,768]{1,0:T(8,128)(2,1)S(1)}, bf16[224,768]{1,0:T(8,128)(2,1)S(1)}, u32[]{:S(2)}, u32[]{:S(2)}) collective-permute-start(bf16[224,768]{1,0:T(8,128)(2,1)S(1)} %pack.1.refs_0_), channel_id=1, source_target_pairs={{0,8},{8,16},{16,24},{24,28},{28,20},{20,12},{12,4},{4,0},{1,9},{9... | collective-permute-start | bytes 1032200 | tf_op jit(solution)/shard_map/ppermute | solution.py:37
  6.6 2.0 collective-permute-start.20
  10.3 1.4 fusion.50
  17.1 1.6 collective-permute-start.16
  18.7 1.6 collective-permute-start.1
  20.7 1.9 multiply_cosine_fusion
  22.6 4.4 %collective-permute-done.1.refs_3_ = bf16[224,768]{1,0:T(8,128)(2,1)S(1)} collective-permute-done((bf16[224,768]{1,0:T(8,128)(2,1)S(1)}, bf16[224,768]{1,0:T(8,128)(2,1)S(1)}, u32[]{:S(2)}, u32[]{:S(2)}) %collective-permute-start.1) | collective-permute-done | bytes 344096 | tf_op jit(solution)/shard_map/ppermute | solution.py:37
  27.0 1.6 collective-permute-start.2
  29.9 5.3 %collective-permute-done.2.refs_5_ = bf16[224,768]{1,0:T(8,128)(2,1)S(1)} collective-permute-done((bf16[224,768]{1,0:T(8,128)(2,1)S(1)}, bf16[224,768]{1,0:T(8,128)(2,1)S(1)}, u32[]{:S(2)}, u32[]{:S(2)}) %collective-permute-start.2) | collective-permute-done | bytes 344096 | tf_op jit(solution)/shard_map/ppermute | solution.py:37
  35.2 1.6 collective-permute-start.14
  37.4 1.6 collective-permute-start.6
  39.8 2.8 %collective-permute-done.14.refs_7_ = bf16[112,768]{1,0:T(8,128)(2,1)S(1)} collective-permute-done((bf16[112,768]{1,0:T(8,128)(2,1)S(1)}, bf16[112,768]{1,0:T(8,128)(2,1)S(1)}, u32[]{:S(2)}, u32[]{:S(2)}) %collective-permute-start.14) | collective-permute-done | bytes 172064 | tf_op jit(solution)/shard_map/ppermute | solution.py:37
  42.6 1.7 collective-permute-done.15.refs_8_
  47.5 2.7 %attend.5 = (bf16[3,80,4096]{2,1,0:T(8,128)(2,1)S(1)}, bf16[3,80,4096]{2,1,0:T(8,128)(2,1)S(1)}, bf16[3,80,4096]{2,1,0:T(8,128)(2,1)S(1)}, bf16[3,80,512]{2,1,0:...) custom-call(s32[1]{0:T(128)} %constant.49.clone.1.slot.slots, ...), custom_call_target="tpu_custom_call" | custom-call | flops 8053063 | bytes 193249 | tf_op jit(solution)/shard_map/attend/pallas_call | solution.py:150
  50.6 1.9 collective-permute-start.8
  52.7 4.3 %attend.6 = (bf16[3,80,4096]{2,1,0:T(8,128)(2,1)S(1)}, bf16[3,80,4096]{2,1,0:T(8,128)(2,1)S(1)}, bf16[3,80,4096]{2,1,0:T(8,128)(2,1)S(1)}, f32[3,512]{1,0:T(4,12...) custom-call(s32[1]{0:T(128)} %constant.63.clone.1.slot, ...), custom_call_target="tpu_custom_call", output_to_operand_aliasing={{0}: (10, {}), {1}: (11, {}), {2}: (12, {})} | custom-call | flops 16106127 | bytes 335052 | tf_op jit(solution)/shard_map/attend/pallas_call | solution.py:150
  57.1 4.8 %collective-permute-done.19 = bf16[256,768]{1,0:T(8,128)(2,1)S(1)} collective-permute-done((bf16[256,768]{1,0:T(8,128)(2,1)S(1)}, bf16[256,768]{1,0:T(8,128)(2,1)S(1)}, u32[]{:S(2)}, u32[]{:S(2)}) %collective-permute-start.19) | collective-permute-done | bytes 393248 | tf_op jit(solution)/shard_map/ppermute | solution.py:47
  62.0 4.3 %attend.7 = (bf16[3,80,4096]{2,1,0:T(8,128)(2,1)S(1)}, bf16[3,80,4096]{2,1,0:T(8,128)(2,1)S(1)}, bf16[3,80,4096]{2,1,0:T(8,128)(2,1)S(1)}, f32[3,512]{1,0:T(4,12...) custom-call(s32[1]{0:T(128)} %constant.48.clone.1.slot, ...), custom_call_target="tpu_custom_call", output_to_operand_aliasing={{0}: (10, {}), {1}: (11, {}), {2}: (12, {})} | custom-call | flops 16106127 | bytes 335052 | tf_op jit(solution)/shard_map/attend/pallas_call | solution.py:150
  66.5 1.6 collective-permute-start.10
  68.5 4.3 %attend.8 = (bf16[3,80,4096]{2,1,0:T(8,128)(2,1)S(1)}, bf16[3,80,4096]{2,1,0:T(8,128)(2,1)S(1)}, bf16[3,80,4096]{2,1,0:T(8,128)(2,1)S(1)}, f32[3,512]{1,0:T(4,12...) custom-call(s32[1]{0:T(128)} %constant.64.clone.1.slot, ...), custom_call_target="tpu_custom_call", output_to_operand_aliasing={{0}: (10, {}), {1}: (11, {}), {2}: (12, {})} | custom-call | flops 16106127 | bytes 335052 | tf_op jit(solution)/shard_map/attend/pallas_call | solution.py:150
  72.9 3.1 %attend.9 = (bf16[3,80,4096]{2,1,0:T(8,128)(2,1)S(1)}, bf16[3,80,4096]{2,1,0:T(8,128)(2,1)S(1)}, bf16[3,80,4096]{2,1,0:T(8,128)(2,1)S(1)}, bf16[256,768]{1,0:T(8...) custom-call(s32[1]{0:T(128)} %constant.47.clone.1.slot, ...), custom_call_target="tpu_custom_call", output_to_operand_aliasing={{0}: (10, {}), {1}: (11, {}), {2}: (12, {})} | custom-call | flops 8053063 | bytes 344760 | tf_op jit(solution)/shard_map/attend/pallas_call | solution.py:150
  76.1 2.9 %collective-permute-done.10.refs_5_ = bf16[96,2304]{1,0:T(8,128)(2,1)S(1)} collective-permute-done((bf16[96,2304]{1,0:T(8,128)(2,1)S(1)}, bf16[96,2304]{1,0:T(8,128)(2,1)S(1)}, u32[]{:S(2)}, u32[]{:S(2)}) %collective-permute-start.10) | collective-permute-done | bytes 442400 | tf_op jit(solution)/shard_map/ppermute | solution.py:37
  79.0 1.3 collective-permute-done.11.refs_6_
  81.0 1.6 collective-permute-start.12
  83.2 4.3 %collective-permute-done.12.refs_7_ = bf16[48,2304]{1,0:T(8,128)(2,1)S(1)} collective-permute-done((bf16[48,2304]{1,0:T(8,128)(2,1)S(1)}, bf16[48,2304]{1,0:T(8,128)(2,1)S(1)}, u32[]{:S(2)}, u32[]{:S(2)}) %collective-permute-start.12) | collective-permute-done | bytes 221216 | tf_op jit(solution)/shard_map/ppermute | solution.py:37
  87.5 1.4 collective-permute-done.13.refs_8_
  88.8 2.0 collective-permute-done.27.other
  91.3 1.7 collective-permute-done.28.refs_10_.refs_1_
  93.0 3.4 %ffn_forward.1 = (bf16[768,1536]{1,0:T(8,128)(2,1)S(1)}, bf16[768,768]{1,0:T(8,128)(2,1)S(1)}, f32[512,1536]{1,0:T(8,128)S(1)}, bf16[512,768]{1,0:T(8,128)(2,1)S...) custom-call(s32[9]{0:T(128)S(1)} %fusion.16.starts, bf16[96,2304]{1,0:T(8,128)(2,1)S(1)} %pad_maximum_fusion.1.refs_0_, ...), custom_call_target="tpu_custom_call" | custom-call | flops 36238784 | bytes 251658 | tf_op jit(solution)/shard_map/ffn_forward/pallas_call | solution.py:150
  96.6 1.6 collective-permute-done.29
  98.9 10.6 %collective-permute-done.30.other = bf16[256,768]{1,0:T(8,128)(2,1)S(1)} collective-permute-done((bf16[256,768]{1,0:T(8,128)(2,1)S(1)}, bf16[256,768]{1,0:T(8,128)(2,1)S(1)}, u32[]{:S(2)}, u32[]{:S(2)}) %collective-permute-start.30) | collective-permute-done | bytes 393248 | tf_op jit(solution)/shard_map/ppermute | solution.py:47
  109.5 1.4 second_norm.1
  110.9 1.7 collective-permute-done.31.refs_1_.refs_3_
  112.7 3.2 %ffn_backward.1 = (bf16[512,1536]{1,0:T(8,128)(2,1)S(1)}, bf16[256,768]{1,0:T(8,128)(2,1)S(1)}, bf16[256,768]{1,0:T(8,128)(2,1)S(1)}) custom-call(bf16[256,768]{1,0:T(8,128)(2,1)S(1)} %get-tuple-element.189.refs_0_.refs_2_, bf16[256,768]{1,0:T(8,128)(2,1)S(1)} %collective-permute-done.31.refs_1_.refs_3_, bf16[768,1536]{1,0:T(8,128)(2,1)S(1)} %get-tuple-element.190.refs_2_, ...), custom_call_target="tpu_custom_call" | custom-call | flops 36238784 | bytes 196608 | tf_op jit(solution)/shard_map/ffn_backward/pallas_call | solution.py:150
  116.1 2.8 %ffn_grad.1 = (bf16[96,2304]{1,0:T(8,128)(2,1)S(1)}, bf16[96,2304]{1,0:T(8,128)(2,1)S(1)}, bf16[96,2304]{1,0:T(8,128)(2,1)S(1)}, bf16[96,2304]{1,0:T(8,128)(2,1)...) custom-call(s32[9]{0:T(128)S(1)} %fusion.32.starts, ...), custom_call_target="tpu_custom_call" | custom-call | flops 36238784 | bytes 149422 | tf_op jit(solution)/shard_map/ffn_grad/pallas_call | solution.py:150
  119.5 1.6 collective-permute-start.35
  121.8 4.9 %collective-permute-done.36 = bf16[48,2304]{1,0:T(8,128)(2,1)S(1)} collective-permute-done((bf16[48,2304]{1,0:T(8,128)(2,1)S(1)}, bf16[48,2304]{1,0:T(8,128)(2,1)S(1)}, u32[]{:S(2)}, u32[]{:S(2)}) %collective-permute-start.36) | collective-permute-done | bytes 221216 | tf_op jit(solution)/shard_map/ppermute | solution.py:42
  127.3 4.8 %collective-permute-done.33.other = bf16[256,768]{1,0:T(8,128)(2,1)S(1)} collective-permute-done((bf16[256,768]{1,0:T(8,128)(2,1)S(1)}, bf16[256,768]{1,0:T(8,128)(2,1)S(1)}, u32[]{:S(2)}, u32[]{:S(2)}) %collective-permute-start.33) | collective-permute-done | bytes 393248 | tf_op jit(solution)/shard_map/ppermute | solution.py:47
  133.0 1.6 collective-permute-start.41
  135.1 1.6 collective-permute-start.37
  137.2 1.3 collective-permute-done.42
  138.6 11.5 %query_grad.1.refs_4_ = f32[3,64,512]{2,1,0:T(8,128)S(1)} custom-call(bf16[3,80,512]{2,1,0:T(8,128)(2,1)S(1)} %get-tuple-element.151.refs_5_.q, bf16[272,512]{1,0:T(8,128)(2,1)S(1)} %prepare.1.g.refs_0_, bf16[3,80,4096]{2,1,0:T(8,128)(2,1)S(1)} %get-tuple-element.215.k.refs_2_.refs_3_, bf16[3,80,4096]{2,1,0:T(8,128)(2,1)S(1)} %get-tuple-element.216.v.refs_3_.refs_4_, ...), custom_call_target="tpu_custom_call" | custom-call | flops 96636768 | bytes 104857 | tf_op jit(solution)/shard_map/query_grad/pallas_call | solution.py:150
  151.6 1.6 collective-permute-start.39
  153.7 2.4 %key_grad.5 = (f32[3,64,512]{2,1,0:T(8,128)S(1)}, f32[3,64,512]{2,1,0:T(8,128)S(1)}, f32[1,24,256]{2,1,0:T(8,128)S(1)}) custom-call(s32[2]{0:T(128)S(1)} %broadcast_in_dim.210.slots, bf16[272,512]{1,0:T(8,128)(2,1)S(1)} %prepare.1.g.refs_0_, bf16[3,80,4096]{2,1,0:T(8,128)(2,1)S(1)} %get-tuple-element.222.refs_1_.refs_2_, ...), custom_call_target="tpu_custom_call" | custom-call | flops 16106127 | bytes 139755 | tf_op jit(solution)/shard_map/key_grad/pallas_call | solution.py:150
  156.1 3.9 %key_grad.6 = (f32[3,64,512]{2,1,0:T(8,128)S(1)}, f32[3,64,512]{2,1,0:T(8,128)S(1)}, f32[2,24,256]{2,1,0:T(8,128)S(1)}) custom-call(s32[2]{0:T(128)S(1)} %fusion.41.slots, bf16[272,512]{1,0:T(8,128)(2,1)S(1)} %collective-permute-done.37.refs_0_, bf16[272,512]{1,0:T(8,128)(2,1)S(1)} %collective-permute-done.38.refs_1_, ...), custom_call_target="tpu_custom_call" | custom-call | flops 32212254 | bytes 161546 | tf_op jit(solution)/shard_map/key_grad/pallas_call | solution.py:150
  161.1 1.5 collective-permute-start.43
  163.1 3.9 %key_grad.7 = (f32[3,64,512]{2,1,0:T(8,128)S(1)}, f32[3,64,512]{2,1,0:T(8,128)S(1)}, f32[2,24,256]{2,1,0:T(8,128)S(1)}) custom-call(s32[2]{0:T(128)S(1)} %fusion.40.slots, bf16[272,512]{1,0:T(8,128)(2,1)S(1)} %collective-permute-done.39.refs_0_, bf16[272,512]{1,0:T(8,128)(2,1)S(1)} %collective-permute-done.40.refs_1_, ...), custom_call_target="tpu_custom_call" | custom-call | flops 32212254 | bytes 161546 | tf_op jit(solution)/shard_map/key_grad/pallas_call | solution.py:150
  168.2 1.2 collective-permute-done.44.refs_1_
  169.4 1.3 collective-permute-start.45
  171.6 3.9 %key_grad.8 = (f32[3,64,512]{2,1,0:T(8,128)S(1)}, f32[3,64,512]{2,1,0:T(8,128)S(1)}, f32[2,24,256]{2,1,0:T(8,128)S(1)}) custom-call(s32[2]{0:T(128)S(1)} %fusion.39.slots, bf16[272,512]{1,0:T(8,128)(2,1)S(1)} %collective-permute-done.43.refs_0_, bf16[272,512]{1,0:T(8,128)(2,1)S(1)} %collective-permute-done.44.refs_1_, ...), custom_call_target="tpu_custom_call" | custom-call | flops 32212254 | bytes 161546 | tf_op jit(solution)/shard_map/key_grad/pallas_call | solution.py:150
  175.8 2.5 %key_grad.9 = (f32[3,64,512]{2,1,0:T(8,128)S(1)}, f32[3,64,512]{2,1,0:T(8,128)S(1)}, f32[1,24,256]{2,1,0:T(8,128)S(1)}) custom-call(s32[2]{0:T(128)S(1)} %fusion.42.slots, bf16[272,256]{1,0:T(8,128)(2,1)S(1)} %collective-permute-done.45.refs_0_, bf16[272,256]{1,0:T(8,128)(2,1)S(1)} %collective-permute-done.46.refs_1_, ...), custom_call_target="tpu_custom_call" | custom-call | flops 16106127 | bytes 155484 | tf_op jit(solution)/shard_map/key_grad/pallas_call | solution.py:150
  178.3 1.9 late_grad.1
  181.5 1.5 collective-permute-start.57
  183.0 1.3 collective-permute-start.49
  186.2 6.1 %collective-permute-done.49 = bf16[48,768]{1,0:T(8,128)(2,1)S(1)} collective-permute-done((bf16[48,768]{1,0:T(8,128)(2,1)S(1)}, bf16[48,768]{1,0:T(8,128)(2,1)S(1)}, u32[]{:S(2)}, u32[]{:S(2)}) %collective-permute-start.49) | collective-permute-done | bytes 73760 | tf_op jit(solution)/shard_map/ppermute | solution.py:37
  192.3 1.7 collective-permute-start.50
  194.5 4.5 %collective-permute-done.50 = bf16[96,768]{1,0:T(8,128)(2,1)S(1)} collective-permute-done((bf16[96,768]{1,0:T(8,128)(2,1)S(1)}, bf16[96,768]{1,0:T(8,128)(2,1)S(1)}, u32[]{:S(2)}, u32[]{:S(2)}) %collective-permute-start.50) | collective-permute-done | bytes 147488 | tf_op jit(solution)/shard_map/ppermute | solution.py:37
  199.0 1.5 collective-permute-start.51
  201.4 1.5 collective-permute-start.58
  203.6 2.0 collective-permute-done.51
  205.6 1.6 collective-permute-start.52
  209.0 1.5 collective-permute-done.56.back
  210.6 1.3 collective-permute-done.52.ahead
  213.8 1.2 finish_ffn.1
  (196 shorter events, 37.8 us)
Async XLA Ops:
  0.6 14.9 %copy-start.10 = (s32[9]{0:T(128)S(1)}, s32[9]{0:T(128)}, u32[]{:S(2)}) copy-start(s32[9]{0:T(128)} %constant.28.clone) | copy-start | bytes 112
  0.7 14.9 %copy-start.11 = (s32[9]{0:T(128)S(1)}, s32[9]{0:T(128)}, u32[]{:S(2)}) copy-start(s32[9]{0:T(128)} %constant.65.clone) | copy-start | bytes 112
  2.4 13.7 %copy-start.3 = (s32[4096]{0:T(1024)S(1)}, s32[4096]{0:T(1024)}, u32[]{:S(2)}) copy-start(s32[4096]{0:T(1024)} %param.30) | copy-start | bytes 49156
  3.5 12.2 %collective-permute-start = (bf16[224,768]{1,0:T(8,128)(2,1)S(1)}, bf16[224,768]{1,0:T(8,128)(2,1)S(1)}, u32[]{:S(2)}, u32[]{:S(2)}) collective-permute-start(bf16[224,768]{1,0:T(8,128)(2,1)S(1)} %pack.1.refs_0_), channel_id=1, source_target_pairs={{0,8},{8,16},{16,24},{24,28},{28,20},{20,12},{12,4},{4,0},{1,9},{9... | collective-permute-start | bytes 1032200 | tf_op jit(solution)/shard_map/ppermute | solution.py:37
  6.6 9.5 %collective-permute-start.3 = (bf16[224,768]{1,0:T(8,128)(2,1)S(1)}, bf16[224,768]{1,0:T(8,128)(2,1)S(1)}, u32[]{:S(2)}, u32[]{:S(2)}) collective-permute-start(bf16[224,768]{1,0:T(8,128)(2,1)S(1)} %pack.1.refs_0_), channel_id=1, source_target_pairs={{8,0},{16,8},{24,16},{28,24},{20,28},{12,20},{4,12},{0,4},{9,1},{1... | collective-permute-start | bytes 1032200 | tf_op jit(solution)/shard_map/ppermute | solution.py:42
  6.6 9.0 %collective-permute-start.20 = (bf16[128,768]{1,0:T(8,128)(2,1)}, bf16[128,768]{1,0:T(8,128)(2,1)S(1)}, u32[]{:S(2)}, u32[]{:S(2)}) collective-permute-start(bf16[128,768]{1,0:T(8,128)(2,1)} %tokens.1), channel_id=1, source_target_pairs={{0,2},{1,3},{2,0},{3,1},{4,6},{5,7},{6,4},{7,5},{8,10},{9,11},{10,... | collective-permute-start | bytes 589832 | tf_op jit(solution)/shard_map/ppermute | solution.py:47
  17.1 12.0 %collective-permute-start.16 = (bf16[256,768]{1,0:T(8,128)(2,1)S(1)}, bf16[256,768]{1,0:T(8,128)(2,1)S(1)}, u32[]{:S(2)}, u32[]{:S(2)}) collective-permute-start(bf16[256,768]{1,0:T(8,128)(2,1)S(1)} %pad_maximum_fusion.4), channel_id=1, source_target_pairs={{0,2},{1,3},{2,0},{3,1},{4,6},{5,7},{6,4},{7,5},{8,10},{9,11},{10,... | collective-permute-start | bytes 1179656 | tf_op jit(solution)/shard_map/ppermute | solution.py:47
  18.7 8.3 %collective-permute-start.1 = (bf16[224,768]{1,0:T(8,128)(2,1)S(1)}, bf16[224,768]{1,0:T(8,128)(2,1)S(1)}, u32[]{:S(2)}, u32[]{:S(2)}) collective-permute-start(bf16[224,768]{1,0:T(8,128)(2,1)S(1)} %collective-permute-done.refs_1_), channel_id=1, source_target_pairs={{0,8},{8,16},{16,24},{24,28},{28,20},{20,12},{12,4},{4,0},{1,9},{9... | collective-permute-start | bytes 1032200 | tf_op jit(solution)/shard_map/ppermute | solution.py:37
  20.3 8.3 %collective-permute-start.4 = (bf16[224,768]{1,0:T(8,128)(2,1)S(1)}, bf16[224,768]{1,0:T(8,128)(2,1)S(1)}, u32[]{:S(2)}, u32[]{:S(2)}) collective-permute-start(bf16[224,768]{1,0:T(8,128)(2,1)S(1)} %collective-permute-done.3.refs_2_), channel_id=1, source_target_pairs={{8,0},{16,8},{24,16},{28,24},{20,28},{12,20},{4,12},{0,4},{9,1},{1... | collective-permute-start | bytes 1032200 | tf_op jit(solution)/shard_map/ppermute | solution.py:42
  27.0 8.2 %collective-permute-start.2 = (bf16[224,768]{1,0:T(8,128)(2,1)S(1)}, bf16[224,768]{1,0:T(8,128)(2,1)S(1)}, u32[]{:S(2)}, u32[]{:S(2)}) collective-permute-start(bf16[224,768]{1,0:T(8,128)(2,1)S(1)} %collective-permute-done.1.refs_3_), channel_id=1, source_target_pairs={{0,8},{8,16},{16,24},{24,28},{28,20},{20,12},{12,4},{4,0},{1,9},{9... | collective-permute-start | bytes 1032200 | tf_op jit(solution)/shard_map/ppermute | solution.py:37
  28.6 8.2 %collective-permute-start.5 = (bf16[224,768]{1,0:T(8,128)(2,1)S(1)}, bf16[224,768]{1,0:T(8,128)(2,1)S(1)}, u32[]{:S(2)}, u32[]{:S(2)}) collective-permute-start(bf16[224,768]{1,0:T(8,128)(2,1)S(1)} %collective-permute-done.4.refs_4_), channel_id=1, source_target_pairs={{8,0},{16,8},{24,16},{28,24},{20,28},{12,20},{4,12},{0,4},{9,1},{1... | collective-permute-start | bytes 1032200 | tf_op jit(solution)/shard_map/ppermute | solution.py:42
  29.2 10.2 %collective-permute-start.17 = (bf16[256,768]{1,0:T(8,128)(2,1)S(1)}, bf16[256,768]{1,0:T(8,128)(2,1)S(1)}, u32[]{:S(2)}, u32[]{:S(2)}) collective-permute-start(bf16[256,768]{1,0:T(8,128)(2,1)S(1)} %pad_maximum_fusion.5), channel_id=1, source_target_pairs={{0,2},{1,3},{2,0},{3,1},{4,6},{5,7},{6,4},{7,5},{8,10},{9,11},{10,... | collective-permute-start | bytes 1179656 | tf_op jit(solution)/shard_map/ppermute | solution.py:47
  35.2 7.4 %collective-permute-start.14 = (bf16[112,768]{1,0:T(8,128)(2,1)S(1)}, bf16[112,768]{1,0:T(8,128)(2,1)S(1)}, u32[]{:S(2)}, u32[]{:S(2)}) collective-permute-start(bf16[112,768]{1,0:T(8,128)(2,1)S(1)} %slice.160), channel_id=1, source_target_pairs={{0,8},{8,16},{16,24},{24,28},{28,20},{20,12},{12,4},{4,0},{1,9},{9... | collective-permute-start | bytes 516104 | tf_op jit(solution)/shard_map/ppermute | solution.py:37
  36.9 7.4 %collective-permute-start.15 = (bf16[112,768]{1,0:T(8,128)(2,1)S(1)}, bf16[112,768]{1,0:T(8,128)(2,1)S(1)}, u32[]{:S(2)}, u32[]{:S(2)}) collective-permute-start(bf16[112,768]{1,0:T(8,128)(2,1)S(1)} %slice.161), channel_id=1, source_target_pairs={{8,0},{16,8},{24,16},{28,24},{20,28},{12,20},{4,12},{0,4},{9,1},{1... | collective-permute-start | bytes 516104 | tf_op jit(solution)/shard_map/ppermute | solution.py:42
  37.4 12.8 %collective-permute-start.6 = (bf16[96,2304]{1,0:T(8,128)(2,1)S(1)}, bf16[96,2304]{1,0:T(8,128)(2,1)S(1)}, u32[]{:S(2)}, u32[]{:S(2)}) collective-permute-start(bf16[96,2304]{1,0:T(8,128)(2,1)S(1)} %pad_maximum_fusion.1.refs_0_), channel_id=1, source_target_pairs={{0,8},{8,16},{16,24},{24,28},{28,20},{20,12},{12,4},{4,0},{1,9},{9... | collective-permute-start | bytes 1327112 | tf_op jit(solution)/shard_map/ppermute | solution.py:37
  38.9 11.3 %collective-permute-start.7 = (bf16[96,2304]{1,0:T(8,128)(2,1)S(1)}, bf16[96,2304]{1,0:T(8,128)(2,1)S(1)}, u32[]{:S(2)}, u32[]{:S(2)}) collective-permute-start(bf16[96,2304]{1,0:T(8,128)(2,1)S(1)} %pad_maximum_fusion.1.refs_0_), channel_id=1, source_target_pairs={{8,0},{16,8},{24,16},{28,24},{20,28},{12,20},{4,12},{0,4},{9,1},{1... | collective-permute-start | bytes 1327112 | tf_op jit(solution)/shard_map/ppermute | solution.py:42
  39.5 7.8 %collective-permute-start.18 = (bf16[256,768]{1,0:T(8,128)(2,1)S(1)}, bf16[256,768]{1,0:T(8,128)(2,1)S(1)}, u32[]{:S(2)}, u32[]{:S(2)}) collective-permute-start(bf16[256,768]{1,0:T(8,128)(2,1)S(1)} %pad_maximum_fusion.6), channel_id=1, source_target_pairs={{0,2},{1,3},{2,0},{3,1},{4,6},{5,7},{6,4},{7,5},{8,10},{9,11},{10,... | collective-permute-start | bytes 1179656 | tf_op jit(solution)/shard_map/ppermute | solution.py:47
  44.2 3.2 %collective-permute-start.21 = (bf16[256,768]{1,0:T(8,128)(2,1)S(1)}, bf16[256,768]{1,0:T(8,128)(2,1)S(1)}, u32[]{:S(2)}, u32[]{:S(2)}) collective-permute-start(bf16[256,768]{1,0:T(8,128)(2,1)S(1)} %constant_dynamic-update-slice_fusion.15.refs_0_.tokens), channel_id=1, source_target_pairs={{0,1},{1,0},{2,3},{3,2},{4,5},{5,4},{6,7},{7,6},{8,9},{9,8},{10,11... | collective-permute-start | bytes 1179656 | tf_op jit(solution)/shard_map/ppermute | solution.py:47
  44.6 8.1 %collective-permute-start.23 = (bf16[512,768]{1,0:T(8,128)(2,1)S(1)}, bf16[512,768]{1,0:T(8,128)(2,1)S(1)}, u32[]{:S(2)}, u32[]{:S(2)}) collective-permute-start(bf16[512,768]{1,0:T(8,128)(2,1)S(1)} %constant_dynamic-update-slice_fusion.refs_0_), channel_id=1, source_target_pairs={{0,1},{1,0},{2,3},{3,2},{4,5},{5,4},{6,7},{7,6},{8,9},{9,8},{10,11... | collective-permute-start | bytes 2359304 | tf_op jit(solution)/shard_map/ppermute | solution.py:47
  50.2 11.8 %collective-permute-start.22 = (bf16[512,768]{1,0:T(8,128)(2,1)S(1)}, bf16[512,768]{1,0:T(8,128)(2,1)S(1)}, u32[]{:S(2)}, u32[]{:S(2)}) collective-permute-start(bf16[512,768]{1,0:T(8,128)(2,1)S(1)} %constant_dynamic-update-slice_fusion.5.refs_0_), channel_id=1, source_target_pairs={{0,1},{1,0},{2,3},{3,2},{4,5},{5,4},{6,7},{7,6},{8,9},{9,8},{10,11... | collective-permute-start | bytes 2359304 | tf_op jit(solution)/shard_map/ppermute | solution.py:47
  50.4 11.6 %collective-permute-start.19 = (bf16[256,768]{1,0:T(8,128)(2,1)S(1)}, bf16[256,768]{1,0:T(8,128)(2,1)S(1)}, u32[]{:S(2)}, u32[]{:S(2)}) collective-permute-start(bf16[256,768]{1,0:T(8,128)(2,1)S(1)} %pad_maximum_fusion.7), channel_id=1, source_target_pairs={{0,2},{1,3},{2,0},{3,1},{4,6},{5,7},{6,4},{7,5},{8,10},{9,11},{10,... | collective-permute-start | bytes 1179656 | tf_op jit(solution)/shard_map/ppermute | solution.py:47
  50.6 15.7 %collective-permute-start.8 = (bf16[96,2304]{1,0:T(8,128)(2,1)S(1)}, bf16[96,2304]{1,0:T(8,128)(2,1)S(1)}, u32[]{:S(2)}, u32[]{:S(2)}) collective-permute-start(bf16[96,2304]{1,0:T(8,128)(2,1)S(1)} %collective-permute-done.6.refs_1_), channel_id=1, source_target_pairs={{0,8},{8,16},{16,24},{24,28},{28,20},{20,12},{12,4},{4,0},{1,9},{9... | collective-permute-start | bytes 1327112 | tf_op jit(solution)/shard_map/ppermute | solution.py:37
  52.5 13.9 %collective-permute-start.9 = (bf16[96,2304]{1,0:T(8,128)(2,1)S(1)}, bf16[96,2304]{1,0:T(8,128)(2,1)S(1)}, u32[]{:S(2)}, u32[]{:S(2)}) collective-permute-start(bf16[96,2304]{1,0:T(8,128)(2,1)S(1)} %collective-permute-done.7.refs_2_), channel_id=1, source_target_pairs={{8,0},{16,8},{24,16},{28,24},{20,28},{12,20},{4,12},{0,4},{9,1},{1... | collective-permute-start | bytes 1327112 | tf_op jit(solution)/shard_map/ppermute | solution.py:42
  57.0 11.5 %collective-permute-start.25 = (bf16[512,768]{1,0:T(8,128)(2,1)S(1)}, bf16[512,768]{1,0:T(8,128)(2,1)S(1)}, u32[]{:S(2)}, u32[]{:S(2)}) collective-permute-start(bf16[512,768]{1,0:T(8,128)(2,1)S(1)} %constant_dynamic-update-slice_fusion.10.refs_0_), channel_id=1, source_target_pairs={{0,1},{1,0},{2,3},{3,2},{4,5},{5,4},{6,7},{7,6},{8,9},{9,8},{10,11... | collective-permute-start | bytes 2359304 | tf_op jit(solution)/shard_map/ppermute | solution.py:47
  66.4 6.5 %collective-permute-start.24 = (bf16[256,768]{1,0:T(8,128)(2,1)S(1)}, bf16[256,768]{1,0:T(8,128)(2,1)S(1)}, u32[]{:S(2)}, u32[]{:S(2)}) collective-permute-start(bf16[256,768]{1,0:T(8,128)(2,1)S(1)} %pad_maximum_fusion.8.refs_0_), channel_id=1, source_target_pairs={{0,1},{1,0},{2,3},{3,2},{4,5},{5,4},{6,7},{7,6},{8,9},{9,8},{10,11... | collective-permute-start | bytes 1179656 | tf_op jit(solution)/shard_map/ppermute | solution.py:47
  66.5 12.6 %collective-permute-start.10 = (bf16[96,2304]{1,0:T(8,128)(2,1)S(1)}, bf16[96,2304]{1,0:T(8,128)(2,1)S(1)}, u32[]{:S(2)}, u32[]{:S(2)}) collective-permute-start(bf16[96,2304]{1,0:T(8,128)(2,1)S(1)} %collective-permute-done.8.refs_3_), channel_id=1, source_target_pairs={{0,8},{8,16},{16,24},{24,28},{28,20},{20,12},{12,4},{4,0},{1,9},{9... | collective-permute-start | bytes 1327112 | tf_op jit(solution)/shard_map/ppermute | solution.py:37
  68.1 12.2 %collective-permute-start.11 = (bf16[96,2304]{1,0:T(8,128)(2,1)S(1)}, bf16[96,2304]{1,0:T(8,128)(2,1)S(1)}, u32[]{:S(2)}, u32[]{:S(2)}) collective-permute-start(bf16[96,2304]{1,0:T(8,128)(2,1)S(1)} %collective-permute-done.9.refs_4_), channel_id=1, source_target_pairs={{8,0},{16,8},{24,16},{28,24},{20,28},{12,20},{4,12},{0,4},{9,1},{1... | collective-permute-start | bytes 1327112 | tf_op jit(solution)/shard_map/ppermute | solution.py:42
  76.0 4.3 %collective-permute-start.26 = (bf16[256,768]{1,0:T(8,128)(2,1)S(1)}, bf16[256,768]{1,0:T(8,128)(2,1)S(1)}, u32[]{:S(2)}, u32[]{:S(2)}) collective-permute-start(bf16[256,768]{1,0:T(8,128)(2,1)S(1)} %get-tuple-element.182), channel_id=1, source_target_pairs={{0,1},{1,0},{2,3},{3,2},{4,5},{5,4},{6,7},{7,6},{8,9},{9,8},{10,11... | collective-permute-start | bytes 1179656 | tf_op jit(solution)/shard_map/ppermute | solution.py:47
  80.4 10.4 %collective-permute-start.27 = (bf16[256,768]{1,0:T(8,128)(2,1)S(1)}, bf16[256,768]{1,0:T(8,128)(2,1)S(1)}, u32[]{:S(2)}, u32[]{:S(2)}) collective-permute-start(bf16[256,768]{1,0:T(8,128)(2,1)S(1)} %add_convert_fusion.7.mine), channel_id=1, source_target_pairs={{0,2},{1,3},{2,0},{3,1},{4,6},{5,7},{6,4},{7,5},{8,10},{9,11},{10,... | collective-permute-start | bytes 1179656 | tf_op jit(solution)/shard_map/ppermute | solution.py:47
  81.0 6.4 %collective-permute-start.12 = (bf16[48,2304]{1,0:T(8,128)(2,1)S(1)}, bf16[48,2304]{1,0:T(8,128)(2,1)S(1)}, u32[]{:S(2)}, u32[]{:S(2)}) collective-permute-start(bf16[48,2304]{1,0:T(8,128)(2,1)S(1)} %slice.158), channel_id=1, source_target_pairs={{0,8},{8,16},{16,24},{24,28},{28,20},{20,12},{12,4},{4,0},{1,9},{9... | collective-permute-start | bytes 663560 | tf_op jit(solution)/shard_map/ppermute | solution.py:37
  82.7 6.2 %collective-permute-start.13 = (bf16[48,2304]{1,0:T(8,128)(2,1)S(1)}, bf16[48,2304]{1,0:T(8,128)(2,1)S(1)}, u32[]{:S(2)}, u32[]{:S(2)}) collective-permute-start(bf16[48,2304]{1,0:T(8,128)(2,1)S(1)} %slice.159), channel_id=1, source_target_pairs={{8,0},{16,8},{24,16},{28,24},{20,28},{12,20},{4,12},{0,4},{9,1},{1... | collective-permute-start | bytes 663560 | tf_op jit(solution)/shard_map/ppermute | solution.py:42
  91.2 1.8 collective-permute-start.28
  96.4 1.8 collective-permute-start.29
  98.3 11.2 %collective-permute-start.30 = (bf16[256,768]{1,0:T(8,128)(2,1)S(1)}, bf16[256,768]{1,0:T(8,128)(2,1)S(1)}, u32[]{:S(2)}, u32[]{:S(2)}) collective-permute-start(bf16[256,768]{1,0:T(8,128)(2,1)S(1)} %add_convert_fusion.6.mine), channel_id=1, source_target_pairs={{0,2},{1,3},{2,0},{3,1},{4,6},{5,7},{6,4},{7,5},{8,10},{9,11},{10,... | collective-permute-start | bytes 1179656 | tf_op jit(solution)/shard_map/ppermute | solution.py:47
  110.9 1.7 collective-permute-start.31
  115.9 5.2 %collective-permute-start.32 = (bf16[256,768]{1,0:T(8,128)(2,1)S(1)}, bf16[256,768]{1,0:T(8,128)(2,1)S(1)}, u32[]{:S(2)}, u32[]{:S(2)}) collective-permute-start(bf16[256,768]{1,0:T(8,128)(2,1)S(1)} %get-tuple-element.194), channel_id=1, source_target_pairs={{0,1},{1,0},{2,3},{3,2},{4,5},{5,4},{6,7},{7,6},{8,9},{9,8},{10,11... | collective-permute-start | bytes 1179656 | tf_op jit(solution)/shard_map/ppermute | solution.py:47
  118.9 7.8 %collective-permute-start.36 = (bf16[48,2304]{1,0:T(8,128)(2,1)S(1)}, bf16[48,2304]{1,0:T(8,128)(2,1)S(1)}, u32[]{:S(2)}, u32[]{:S(2)}) collective-permute-start(bf16[48,2304]{1,0:T(8,128)(2,1)S(1)} %get-tuple-element.202), channel_id=1, source_target_pairs={{8,0},{16,8},{24,16},{28,24},{20,28},{12,20},{4,12},{0,4},{9,1},{1... | collective-permute-start | bytes 663560 | tf_op jit(solution)/shard_map/ppermute | solution.py:42
  119.5 13.4 %collective-permute-start.35 = (bf16[48,2304]{1,0:T(8,128)(2,1)S(1)}, bf16[48,2304]{1,0:T(8,128)(2,1)S(1)}, u32[]{:S(2)}, u32[]{:S(2)}) collective-permute-start(bf16[48,2304]{1,0:T(8,128)(2,1)S(1)} %get-tuple-element.201), channel_id=1, source_target_pairs={{0,8},{8,16},{16,24},{24,28},{28,20},{20,12},{12,4},{4,0},{1,9},{9... | collective-permute-start | bytes 663560 | tf_op jit(solution)/shard_map/ppermute | solution.py:37
  121.2 10.9 %collective-permute-start.33 = (bf16[256,768]{1,0:T(8,128)(2,1)S(1)}, bf16[256,768]{1,0:T(8,128)(2,1)S(1)}, u32[]{:S(2)}, u32[]{:S(2)}) collective-permute-start(bf16[256,768]{1,0:T(8,128)(2,1)S(1)} %add_convert_fusion.5.mine), channel_id=1, source_target_pairs={{0,2},{1,3},{2,0},{3,1},{4,6},{5,7},{6,4},{7,5},{8,10},{9,11},{10,... | collective-permute-start | bytes 1179656 | tf_op jit(solution)/shard_map/ppermute | solution.py:47
  126.8 11.7 %collective-permute-start.42 = (bf16[96,2304]{1,0:T(8,128)(2,1)S(1)}, bf16[96,2304]{1,0:T(8,128)(2,1)S(1)}, u32[]{:S(2)}, u32[]{:S(2)}) collective-permute-start(bf16[96,2304]{1,0:T(8,128)(2,1)S(1)} %pad_maximum_fusion.3), channel_id=1, source_target_pairs={{8,0},{16,8},{24,16},{28,24},{20,28},{12,20},{4,12},{0,4},{9,1},{1... | collective-permute-start | bytes 1327112 | tf_op jit(solution)/shard_map/ppermute | solution.py:42
  132.8 1.8 collective-permute-start.34
  133.0 20.6 %collective-permute-start.41 = (bf16[96,2304]{1,0:T(8,128)(2,1)S(1)}, bf16[96,2304]{1,0:T(8,128)(2,1)S(1)}, u32[]{:S(2)}, u32[]{:S(2)}) collective-permute-start(bf16[96,2304]{1,0:T(8,128)(2,1)S(1)} %pad_maximum_fusion.2), channel_id=1, source_target_pairs={{0,8},{8,16},{16,24},{24,28},{28,20},{20,12},{12,4},{4,0},{1,9},{9... | collective-permute-start | bytes 1327112 | tf_op jit(solution)/shard_map/ppermute | solution.py:37
  135.1 16.5 %collective-permute-start.37 = (bf16[272,512]{1,0:T(8,128)(2,1)S(1)}, bf16[272,512]{1,0:T(8,128)(2,1)S(1)}, u32[]{:S(2)}, u32[]{:S(2)}) collective-permute-start(bf16[272,512]{1,0:T(8,128)(2,1)S(1)} %prepare.1.g.refs_0_), channel_id=1, source_target_pairs={{0,8},{8,16},{16,24},{24,28},{28,20},{20,12},{12,4},{4,0},{1,9},{9... | collective-permute-start | bytes 835592 | tf_op jit(solution)/shard_map/ppermute | solution.py:37
  136.7 14.8 %collective-permute-start.38 = (bf16[272,512]{1,0:T(8,128)(2,1)S(1)}, bf16[272,512]{1,0:T(8,128)(2,1)S(1)}, u32[]{:S(2)}, u32[]{:S(2)}) collective-permute-start(bf16[272,512]{1,0:T(8,128)(2,1)S(1)} %prepare.1.g.refs_0_), channel_id=1, source_target_pairs={{8,0},{16,8},{24,16},{28,24},{20,28},{12,20},{4,12},{0,4},{9,1},{1... | collective-permute-start | bytes 835592 | tf_op jit(solution)/shard_map/ppermute | solution.py:42
  151.6 8.5 %collective-permute-start.39 = (bf16[272,512]{1,0:T(8,128)(2,1)S(1)}, bf16[272,512]{1,0:T(8,128)(2,1)S(1)}, u32[]{:S(2)}, u32[]{:S(2)}) collective-permute-start(bf16[272,512]{1,0:T(8,128)(2,1)S(1)} %collective-permute-done.37.refs_0_), channel_id=1, source_target_pairs={{0,8},{8,16},{16,24},{24,28},{28,20},{20,12},{12,4},{4,0},{1,9},{9... | collective-permute-start | bytes 835592 | tf_op jit(solution)/shard_map/ppermute | solution.py:37
  153.1 8.0 %collective-permute-start.40 = (bf16[272,512]{1,0:T(8,128)(2,1)S(1)}, bf16[272,512]{1,0:T(8,128)(2,1)S(1)}, u32[]{:S(2)}, u32[]{:S(2)}) collective-permute-start(bf16[272,512]{1,0:T(8,128)(2,1)S(1)} %collective-permute-done.38.refs_1_), channel_id=1, source_target_pairs={{8,0},{16,8},{24,16},{28,24},{20,28},{12,20},{4,12},{0,4},{9,1},{1... | collective-permute-start | bytes 835592 | tf_op jit(solution)/shard_map/ppermute | solution.py:42
  161.1 7.1 %collective-permute-start.43 = (bf16[272,512]{1,0:T(8,128)(2,1)S(1)}, bf16[272,512]{1,0:T(8,128)(2,1)S(1)}, u32[]{:S(2)}, u32[]{:S(2)}) collective-permute-start(bf16[272,512]{1,0:T(8,128)(2,1)S(1)} %collective-permute-done.39.refs_0_), channel_id=1, source_target_pairs={{0,8},{8,16},{16,24},{24,28},{28,20},{20,12},{12,4},{4,0},{1,9},{9... | collective-permute-start | bytes 835592 | tf_op jit(solution)/shard_map/ppermute | solution.py:37
  162.6 6.8 %collective-permute-start.44 = (bf16[272,512]{1,0:T(8,128)(2,1)S(1)}, bf16[272,512]{1,0:T(8,128)(2,1)S(1)}, u32[]{:S(2)}, u32[]{:S(2)}) collective-permute-start(bf16[272,512]{1,0:T(8,128)(2,1)S(1)} %collective-permute-done.40.refs_1_), channel_id=1, source_target_pairs={{8,0},{16,8},{24,16},{28,24},{20,28},{12,20},{4,12},{0,4},{9,1},{1... | collective-permute-start | bytes 835592 | tf_op jit(solution)/shard_map/ppermute | solution.py:42
  169.4 6.1 %collective-permute-start.45 = (bf16[272,256]{1,0:T(8,128)(2,1)S(1)}, bf16[272,256]{1,0:T(8,128)(2,1)S(1)}, u32[]{:S(2)}, u32[]{:S(2)}) collective-permute-start(bf16[272,256]{1,0:T(8,128)(2,1)S(1)} %slice.146), channel_id=1, source_target_pairs={{0,8},{8,16},{16,24},{24,28},{28,20},{20,12},{12,4},{4,0},{1,9},{9... | collective-permute-start | bytes 417800 | tf_op jit(solution)/shard_map/ppermute | solution.py:37
  170.7 5.1 %collective-permute-start.46 = (bf16[272,256]{1,0:T(8,128)(2,1)S(1)}, bf16[272,256]{1,0:T(8,128)(2,1)S(1)}, u32[]{:S(2)}, u32[]{:S(2)}) collective-permute-start(bf16[272,256]{1,0:T(8,128)(2,1)S(1)} %slice.147), channel_id=1, source_target_pairs={{8,0},{16,8},{24,16},{28,24},{20,28},{12,20},{4,12},{0,4},{9,1},{1... | collective-permute-start | bytes 417800 | tf_op jit(solution)/shard_map/ppermute | solution.py:42
  180.2 5.3 %collective-permute-start.53 = (bf16[48,768]{1,0:T(8,128)(2,1)S(1)}, bf16[48,768]{1,0:T(8,128)(2,1)S(1)}, u32[]{:S(2)}, u32[]{:S(2)}) collective-permute-start(bf16[48,768]{1,0:T(8,128)(2,1)S(1)} %get-tuple-element.248), channel_id=1, source_target_pairs={{8,0},{16,8},{24,16},{28,24},{20,28},{12,20},{4,12},{0,4},{9,1},{1... | collective-permute-start | bytes 221192 | tf_op jit(solution)/shard_map/ppermute | solution.py:42
  181.0 19.5 %collective-permute-start.59 = (bf16[96,2304]{1,0:T(8,128)(2,1)S(1)}, bf16[96,2304]{1,0:T(8,128)(2,1)S(1)}, u32[]{:S(2)}, u32[]{:S(2)}) collective-permute-start(bf16[96,2304]{1,0:T(8,128)(2,1)S(1)} %add_convert_fusion.2), channel_id=1, source_target_pairs={{8,0},{16,8},{24,16},{28,24},{20,28},{12,20},{4,12},{0,4},{9,1},{1... | collective-permute-start | bytes 1327112 | tf_op jit(solution)/shard_map/ppermute | solution.py:42
  181.5 19.7 %collective-permute-start.57 = (bf16[96,2304]{1,0:T(8,128)(2,1)S(1)}, bf16[96,2304]{1,0:T(8,128)(2,1)S(1)}, u32[]{:S(2)}, u32[]{:S(2)}) collective-permute-start(bf16[96,2304]{1,0:T(8,128)(2,1)S(1)} %add_convert_fusion.3), channel_id=1, source_target_pairs={{0,8},{8,16},{16,24},{24,28},{28,20},{20,12},{12,4},{4,0},{1,9},{9... | collective-permute-start | bytes 1327112 | tf_op jit(solution)/shard_map/ppermute | solution.py:37
  183.0 9.3 %collective-permute-start.49 = (bf16[48,768]{1,0:T(8,128)(2,1)S(1)}, bf16[48,768]{1,0:T(8,128)(2,1)S(1)}, u32[]{:S(2)}, u32[]{:S(2)}) collective-permute-start(bf16[48,768]{1,0:T(8,128)(2,1)S(1)} %get-tuple-element.243), channel_id=1, source_target_pairs={{0,8},{8,16},{16,24},{24,28},{28,20},{20,12},{12,4},{4,0},{1,9},{9... | collective-permute-start | bytes 221192 | tf_op jit(solution)/shard_map/ppermute | solution.py:37
  184.3 22.8 %collective-permute-start.47 = (bf16[256,768]{1,0:T(8,128)(2,1)S(1)}, bf16[256,768]{1,0:T(8,128)(2,1)S(1)}, u32[]{:S(2)}, u32[]{:S(2)}) collective-permute-start(bf16[256,768]{1,0:T(8,128)(2,1)S(1)} %get-tuple-element.241), channel_id=1, source_target_pairs={{0,1},{1,0},{2,3},{3,2},{4,5},{5,4},{6,7},{7,6},{8,9},{9,8},{10,11... | collective-permute-start | bytes 1179656 | tf_op jit(solution)/shard_map/ppermute | solution.py:47
  185.5 8.5 %collective-permute-start.54 = (bf16[96,768]{1,0:T(8,128)(2,1)S(1)}, bf16[96,768]{1,0:T(8,128)(2,1)S(1)}, u32[]{:S(2)}, u32[]{:S(2)}) collective-permute-start(bf16[96,768]{1,0:T(8,128)(2,1)S(1)} %pad_maximum_fusion.12), channel_id=1, source_target_pairs={{8,0},{16,8},{24,16},{28,24},{20,28},{12,20},{4,12},{0,4},{9,1},{1... | collective-permute-start | bytes 442376 | tf_op jit(solution)/shard_map/ppermute | solution.py:42
  192.3 6.6 %collective-permute-start.50 = (bf16[96,768]{1,0:T(8,128)(2,1)S(1)}, bf16[96,768]{1,0:T(8,128)(2,1)S(1)}, u32[]{:S(2)}, u32[]{:S(2)}) collective-permute-start(bf16[96,768]{1,0:T(8,128)(2,1)S(1)} %pad_maximum_fusion.11), channel_id=1, source_target_pairs={{0,8},{8,16},{16,24},{24,28},{28,20},{20,12},{12,4},{4,0},{1,9},{9... | collective-permute-start | bytes 442376 | tf_op jit(solution)/shard_map/ppermute | solution.py:37
  194.1 8.8 %collective-permute-start.55 = (bf16[96,768]{1,0:T(8,128)(2,1)S(1)}, bf16[96,768]{1,0:T(8,128)(2,1)S(1)}, u32[]{:S(2)}, u32[]{:S(2)}) collective-permute-start(bf16[96,768]{1,0:T(8,128)(2,1)S(1)} %add_convert_fusion.11), channel_id=1, source_target_pairs={{8,0},{16,8},{24,16},{28,24},{20,28},{12,20},{4,12},{0,4},{9,1},{1... | collective-permute-start | bytes 442376 | tf_op jit(solution)/shard_map/ppermute | solution.py:42
  199.0 6.5 %collective-permute-start.51 = (bf16[96,768]{1,0:T(8,128)(2,1)S(1)}, bf16[96,768]{1,0:T(8,128)(2,1)S(1)}, u32[]{:S(2)}, u32[]{:S(2)}) collective-permute-start(bf16[96,768]{1,0:T(8,128)(2,1)S(1)} %add_convert_fusion.13), channel_id=1, source_target_pairs={{0,8},{8,16},{16,24},{24,28},{28,20},{20,12},{12,4},{4,0},{1,9},{9... | collective-permute-start | bytes 442376 | tf_op jit(solution)/shard_map/ppermute | solution.py:37
  200.6 13.2 %collective-permute-start.60 = (bf16[96,2304]{1,0:T(8,128)(2,1)S(1)}, bf16[96,2304]{1,0:T(8,128)(2,1)S(1)}, u32[]{:S(2)}, u32[]{:S(2)}) collective-permute-start(bf16[96,2304]{1,0:T(8,128)(2,1)S(1)} %add_convert_fusion), channel_id=1, source_target_pairs={{8,0},{16,8},{24,16},{28,24},{20,28},{12,20},{4,12},{0,4},{9,1},{1... | collective-permute-start | bytes 1327112 | tf_op jit(solution)/shard_map/ppermute | solution.py:42
  201.4 12.4 %collective-permute-start.58 = (bf16[96,2304]{1,0:T(8,128)(2,1)S(1)}, bf16[96,2304]{1,0:T(8,128)(2,1)S(1)}, u32[]{:S(2)}, u32[]{:S(2)}) collective-permute-start(bf16[96,2304]{1,0:T(8,128)(2,1)S(1)} %add_convert_fusion.1), channel_id=1, source_target_pairs={{0,8},{8,16},{16,24},{24,28},{28,20},{20,12},{12,4},{4,0},{1,9},{9... | collective-permute-start | bytes 1327112 | tf_op jit(solution)/shard_map/ppermute | solution.py:37
  202.9 7.7 %collective-permute-start.56 = (bf16[96,768]{1,0:T(8,128)(2,1)S(1)}, bf16[96,768]{1,0:T(8,128)(2,1)S(1)}, u32[]{:S(2)}, u32[]{:S(2)}) collective-permute-start(bf16[96,768]{1,0:T(8,128)(2,1)S(1)} %add_convert_fusion.10), channel_id=1, source_target_pairs={{8,0},{16,8},{24,16},{28,24},{20,28},{12,20},{4,12},{0,4},{9,1},{1... | collective-permute-start | bytes 442376 | tf_op jit(solution)/shard_map/ppermute | solution.py:42
  205.6 6.3 %collective-permute-start.52 = (bf16[96,768]{1,0:T(8,128)(2,1)S(1)}, bf16[96,768]{1,0:T(8,128)(2,1)S(1)}, u32[]{:S(2)}, u32[]{:S(2)}) collective-permute-start(bf16[96,768]{1,0:T(8,128)(2,1)S(1)} %add_convert_fusion.12), channel_id=1, source_target_pairs={{0,8},{8,16},{16,24},{24,28},{28,20},{20,12},{12,4},{4,0},{1,9},{9... | collective-permute-start | bytes 442376 | tf_op jit(solution)/shard_map/ppermute | solution.py:37
  207.3 5.7 %collective-permute-start.48 = (bf16[128,768]{1,0:T(8,128)(2,1)S(1)}, bf16[128,768]{1,0:T(8,128)(2,1)S(1)}, u32[]{:S(2)}, u32[]{:S(2)}) collective-permute-start(bf16[128,768]{1,0:T(8,128)(2,1)S(1)} %slice.169), channel_id=1, source_target_pairs={{0,2},{1,3},{2,0},{3,1},{4,6},{5,7},{6,4},{7,5},{8,10},{9,11},{10,... | collective-permute-start | bytes 589832 | tf_op jit(solution)/shard_map/ppermute | solution.py:47
  (10 other events, 49.4 us)

commit v3 on v2

--- a/solution.py
+++ b/solution.py
@@ -338,7 +338,10 @@
 
 
 def with_terms(q, g):
-    return jnp.concatenate([q[:HEAD], q[HEAD:] + g[HEAD:]], axis=0)
+    extra = g[HEAD:].astype(F32)
+    row = lax.broadcasted_iota(jnp.int32, extra.shape, 0)
+    extra = q[HEAD:].astype(F32) + jnp.where(row < 8, 0.0, extra)
+    return jnp.concatenate([q[:HEAD], extra.astype(BF)], axis=0)
 
 
 def query_grad_kernel(heads, q, g, k, v, out_in, out):
@@ -395,7 +398,8 @@
         dk[h] = dk_in[h] + key if carried else key
 
     for i in range(norms.shape[0]):
-        norms[i] = pieces[i][heads * rows : heads * rows + NORM_ROWS, :NORM_LANES].astype(F32)
+        for h in range(heads):
+            norms[i, 8 * h : 8 * h + 8, :] = pieces[i][h * rows + HEAD : h * rows + HEAD + 8, :NORM_LANES].astype(F32)
 
 
 NORM_LANES = 256
@@ -559,31 +563,28 @@
     g = stacked(pieces, taken)
     rows = HEAD + AUX
     grad = dot(w_out[...], g, NT).astype(BF)
-    index = lax.broadcasted_iota(jnp.int32, (AUX, g.shape[0]), 0)
+
+    def sums(piece):
+        both = piece[taken : taken + 16].astype(F32)
+        return both[:4] + both[4:8]
+
+    total = sums(pieces[0]) + sums(pieces[1])
+    high = total.astype(BF).astype(F32)
+    both = jnp.concatenate([high, total - high], axis=0)
+    index = lax.broadcasted_iota(jnp.int32, (AUX - 8, g.shape[0]), 0)
     for h in range(heads):
         part = grad[h * HEAD : (h + 1) * HEAD]
         package[h * rows : h * rows + HEAD] = part
         delta = jnp.sum(part.astype(F32) * context[h], axis=0, keepdims=True)
         tail = jnp.zeros(index.shape, F32)
-        for at, value in ((8, -log_total[h : h + 1]), (11, -delta)):
+        for at, value in ((0, -log_total[h : h + 1]), (3, -delta)):
             for j in range(3):
                 high = value.astype(BF).astype(F32)
                 tail = jnp.where(index == at + j, high, tail)
                 value = value - high
-        package[h * rows + HEAD : (h + 1) * rows] = tail.astype(BF)
-
-    def sums(piece):
-        both = piece[taken : taken + 16].astype(F32)
-        return both[:4] + both[4:8]
-
-    total = sums(pieces[0]) + sums(pieces[1])
-    high = total.astype(BF).astype(F32)
-    both = jnp.concatenate([high, total - high], axis=0)
-    base = heads * rows
-    package[base:, NORM_LANES:] = jnp.zeros((package.shape[0] - base, package.shape[1] - NORM_LANES), BF)
-    parts = [both[:, i * NORM_LANES : (i + 1) * NORM_LANES] for i in range(both.shape[1] // NORM_LANES)]
-    parts.append(jnp.zeros((package.shape[0] - base - 8 * len(parts), NORM_LANES), F32))
-    package[base:, :NORM_LANES] = jnp.concatenate(parts, axis=0).astype(BF)
+        norm = both[:, h * NORM_LANES : (h + 1) * NORM_LANES]
+        norm = jnp.concatenate([norm, jnp.zeros((8, g.shape[0] - NORM_LANES), F32)], axis=1)
+        package[h * rows + HEAD : (h + 1) * rows] = jnp.concatenate([norm, tail], axis=0).astype(BF)
 
 
 def turn_back(first, second, cosine, sine):
@@ -631,7 +632,7 @@
     total = block[...].astype(F32) + ahead[...].astype(F32) + back[...].astype(F32)
     gu[:, 0, :] = total[:, :units]
     gu[:, 1, :] = total[:, units : 2 * units]
-    dn[...] = total[:, 2 * units :].T
+    dn[...] = total[:, 2 * units :]
 
 
 def finish_mix_kernel(width, block, ahead, back, mix, out):
@@ -907,7 +908,7 @@
         functools.partial(prepare_kernel, heads, taken),
         "prepare",
         [*attn_pieces, full_out, context, log_total],
-        [struct((heads * (HEAD + AUX) + 32, group), BF)],
+        [struct((heads * (HEAD + AUX), group), BF)],
         flops=2 * width * features * group,
     )
     span = min(2 * group, total)
@@ -943,7 +944,8 @@
     norm_out = struct((4, features), F32)
     if ring:
         package_ring.step(early_grad)
-        sums, norms = key_step([after(package, early_grad, package_ring.done[0], sent)], 1, 6, ())
+        sums, norms = key_step([after(package, early_grad, package_ring.done[0])], 1, 6, ())
+        sums = after(sums, sent)
         norm_pieces = [norms]
         for i in range(3):
             sums, norms = key_step(package_ring.done[i], 2, i, sums)
@@ -1002,7 +1004,7 @@
         functools.partial(finish_ffn_kernel, units),
         "finish_ffn",
         ffn_sum.terms(),
-        [struct((share, 2, units), F32), struct((units, share), F32)],
+        [struct((share, 2, units), F32), struct((share, units), F32)],
         cost=20.0,
     )
     grad_tokens = grad_res1 + col_sum(near, far)
@@ -1019,7 +1021,7 @@
         grad_mix.transpose(1, 0, 2),
         grad_out,
         grad_gu,
-        grad_dn,
+        grad_dn.T,
         norm_sums[0],
         norm_sums[1],
         norm_sums[2],

time: 216 us -> 214 us (level)
    unnamed x35 -> x34, local copies, waits for them, and re-layouts: 4.64 us -> 3.76 us
  transfers between devices with their start and end apart: 61 -> 61, of which waited for: 31 -> 30; matrix products, arithmetic and copies ran while one was open for 5% -> 5% of each run, Pallas kernels for 24% -> 24%
where the time goes in v3:
time: 214 us
  waiting for transfers between devices  79.2 us (37%)
  Pallas kernels  66.7 us (31%)
  starting transfers between devices  51.1 us (24%)
  other arithmetic  7.19 us (3%)
  local copies, waits for them, and re-layouts  6.19 us (3%)
  between operations  3.51 us (2%)
    pallas_call x25, Pallas kernels, call(): pl.pallas_call(kernel, grid_spec=pltpu.PrefetchScalarGridSpec(num_scalar_...  66.7 us
    ppermute x20, waiting for transfers between devices, forward_hop(): lax.ppermute(v, 'row', [(CYCLE[i], CYCLE[(i + 1) % n]) for i in range(n)])  34.9 us
    ppermute x20, starting transfers between devices, forward_hop(): lax.ppermute(v, 'row', [(CYCLE[i], CYCLE[(i + 1) % n]) for i in range(n)])  33.4 us
    ppermute x21, waiting for transfers between devices, col_swap(): return lax.ppermute(v, 'col', [(i, i ^ mask) for i in range(count)])  28.7 us
    ppermute x20, waiting for transfers between devices, backward_hop(): lax.ppermute(v, 'row', [(CYCLE[(i + 1) % n], CYCLE[i]) for i in range(n)])  15.5 us
    ppermute x20, starting transfers between devices, backward_hop(): lax.ppermute(v, 'row', [(CYCLE[(i + 1) % n], CYCLE[i]) for i in range(n)])  9.4 us
    ppermute x21, starting transfers between devices, col_swap(): return lax.ppermute(v, 'col', [(i, i ^ mask) for i in range(count)])  8.32 us
  transfers between devices with their start and end apart: 61, of which 30 were waited for; matrix products, arithmetic and copies ran while one was open for 5% of the time, Pallas kernels for 24%

profile of v3, /device:TPU:0, one launch (start us, length us, event | category | flops | bytes accessed | tf_op | source)
XLA Modules:
  0.0 213.9 jit_solution(8417183742710958061)
XLA Ops:
  3.5 3.1 %collective-permute-start = (bf16[224,768]{1,0:T(8,128)(2,1)S(1)}, bf16[224,768]{1,0:T(8,128)(2,1)S(1)}, u32[]{:S(2)}, u32[]{:S(2)}) collective-permute-start(bf16[224,768]{1,0:T(8,128)(2,1)S(1)} %pack.1.refs_0_), channel_id=1, source_target_pairs={{0,8},{8,16},{16,24},{24,28},{28,20},{20,12},{12,4},{4,0},{1,9},{9... | collective-permute-start | bytes 1032200 | tf_op jit(solution)/shard_map/ppermute | solution.py:37
  6.6 2.0 collective-permute-start.20
  10.3 1.4 fusion.50
  17.1 1.6 collective-permute-start.16
  18.7 1.6 collective-permute-start.1
  20.7 1.9 multiply_cosine_fusion
  22.6 4.4 %collective-permute-done.1.refs_3_ = bf16[224,768]{1,0:T(8,128)(2,1)S(1)} collective-permute-done((bf16[224,768]{1,0:T(8,128)(2,1)S(1)}, bf16[224,768]{1,0:T(8,128)(2,1)S(1)}, u32[]{:S(2)}, u32[]{:S(2)}) %collective-permute-start.1) | collective-permute-done | bytes 344096 | tf_op jit(solution)/shard_map/ppermute | solution.py:37
  27.0 1.6 collective-permute-start.2
  29.9 5.3 %collective-permute-done.2.refs_5_ = bf16[224,768]{1,0:T(8,128)(2,1)S(1)} collective-permute-done((bf16[224,768]{1,0:T(8,128)(2,1)S(1)}, bf16[224,768]{1,0:T(8,128)(2,1)S(1)}, u32[]{:S(2)}, u32[]{:S(2)}) %collective-permute-start.2) | collective-permute-done | bytes 344096 | tf_op jit(solution)/shard_map/ppermute | solution.py:37
  35.2 1.6 collective-permute-start.14
  37.4 1.6 collective-permute-start.6
  39.8 2.8 %collective-permute-done.14.refs_7_ = bf16[112,768]{1,0:T(8,128)(2,1)S(1)} collective-permute-done((bf16[112,768]{1,0:T(8,128)(2,1)S(1)}, bf16[112,768]{1,0:T(8,128)(2,1)S(1)}, u32[]{:S(2)}, u32[]{:S(2)}) %collective-permute-start.14) | collective-permute-done | bytes 172064 | tf_op jit(solution)/shard_map/ppermute | solution.py:37
  42.6 1.7 collective-permute-done.15.refs_8_
  45.1 1.1 assemble.1
  47.5 2.7 %attend.5 = (bf16[3,80,4096]{2,1,0:T(8,128)(2,1)S(1)}, bf16[3,80,4096]{2,1,0:T(8,128)(2,1)S(1)}, bf16[3,80,4096]{2,1,0:T(8,128)(2,1)S(1)}, bf16[3,80,512]{2,1,0:...) custom-call(s32[1]{0:T(128)} %constant.49.clone.1.slot.slots, ...), custom_call_target="tpu_custom_call" | custom-call | flops 8053063 | bytes 193249 | tf_op jit(solution)/shard_map/attend/pallas_call | solution.py:150
  50.6 1.9 collective-permute-start.8
  52.7 4.3 %attend.6 = (bf16[3,80,4096]{2,1,0:T(8,128)(2,1)S(1)}, bf16[3,80,4096]{2,1,0:T(8,128)(2,1)S(1)}, bf16[3,80,4096]{2,1,0:T(8,128)(2,1)S(1)}, f32[3,512]{1,0:T(4,12...) custom-call(s32[1]{0:T(128)} %constant.63.clone.1.slot, ...), custom_call_target="tpu_custom_call", output_to_operand_aliasing={{0}: (10, {}), {1}: (11, {}), {2}: (12, {})} | custom-call | flops 16106127 | bytes 335052 | tf_op jit(solution)/shard_map/attend/pallas_call | solution.py:150
  57.1 4.8 %collective-permute-done.19 = bf16[256,768]{1,0:T(8,128)(2,1)S(1)} collective-permute-done((bf16[256,768]{1,0:T(8,128)(2,1)S(1)}, bf16[256,768]{1,0:T(8,128)(2,1)S(1)}, u32[]{:S(2)}, u32[]{:S(2)}) %collective-permute-start.19) | collective-permute-done | bytes 393248 | tf_op jit(solution)/shard_map/ppermute | solution.py:47
  62.0 4.3 %attend.7 = (bf16[3,80,4096]{2,1,0:T(8,128)(2,1)S(1)}, bf16[3,80,4096]{2,1,0:T(8,128)(2,1)S(1)}, bf16[3,80,4096]{2,1,0:T(8,128)(2,1)S(1)}, f32[3,512]{1,0:T(4,12...) custom-call(s32[1]{0:T(128)} %constant.48.clone.1.slot, ...), custom_call_target="tpu_custom_call", output_to_operand_aliasing={{0}: (10, {}), {1}: (11, {}), {2}: (12, {})} | custom-call | flops 16106127 | bytes 335052 | tf_op jit(solution)/shard_map/attend/pallas_call | solution.py:150
  66.5 1.6 collective-permute-start.10
  68.5 4.3 %attend.8 = (bf16[3,80,4096]{2,1,0:T(8,128)(2,1)S(1)}, bf16[3,80,4096]{2,1,0:T(8,128)(2,1)S(1)}, bf16[3,80,4096]{2,1,0:T(8,128)(2,1)S(1)}, f32[3,512]{1,0:T(4,12...) custom-call(s32[1]{0:T(128)} %constant.64.clone.1.slot, ...), custom_call_target="tpu_custom_call", output_to_operand_aliasing={{0}: (10, {}), {1}: (11, {}), {2}: (12, {})} | custom-call | flops 16106127 | bytes 335052 | tf_op jit(solution)/shard_map/attend/pallas_call | solution.py:150
  72.9 3.1 %attend.9 = (bf16[3,80,4096]{2,1,0:T(8,128)(2,1)S(1)}, bf16[3,80,4096]{2,1,0:T(8,128)(2,1)S(1)}, bf16[3,80,4096]{2,1,0:T(8,128)(2,1)S(1)}, bf16[256,768]{1,0:T(8...) custom-call(s32[1]{0:T(128)} %constant.47.clone.1.slot, ...), custom_call_target="tpu_custom_call", output_to_operand_aliasing={{0}: (10, {}), {1}: (11, {}), {2}: (12, {})} | custom-call | flops 8053063 | bytes 344760 | tf_op jit(solution)/shard_map/attend/pallas_call | solution.py:150
  76.1 2.9 %collective-permute-done.10.refs_5_ = bf16[96,2304]{1,0:T(8,128)(2,1)S(1)} collective-permute-done((bf16[96,2304]{1,0:T(8,128)(2,1)S(1)}, bf16[96,2304]{1,0:T(8,128)(2,1)S(1)}, u32[]{:S(2)}, u32[]{:S(2)}) %collective-permute-start.10) | collective-permute-done | bytes 442400 | tf_op jit(solution)/shard_map/ppermute | solution.py:37
  79.0 1.3 collective-permute-done.11.refs_6_
  81.0 1.6 collective-permute-start.12
  83.2 4.3 %collective-permute-done.12.refs_7_ = bf16[48,2304]{1,0:T(8,128)(2,1)S(1)} collective-permute-done((bf16[48,2304]{1,0:T(8,128)(2,1)S(1)}, bf16[48,2304]{1,0:T(8,128)(2,1)S(1)}, u32[]{:S(2)}, u32[]{:S(2)}) %collective-permute-start.12) | collective-permute-done | bytes 221216 | tf_op jit(solution)/shard_map/ppermute | solution.py:37
  87.5 1.4 collective-permute-done.13.refs_8_
  88.8 2.0 collective-permute-done.27.other
  91.3 1.7 collective-permute-done.28.refs_10_.refs_1_
  93.0 3.4 %ffn_forward.1 = (bf16[768,1536]{1,0:T(8,128)(2,1)S(1)}, bf16[768,768]{1,0:T(8,128)(2,1)S(1)}, f32[512,1536]{1,0:T(8,128)S(1)}, bf16[512,768]{1,0:T(8,128)(2,1)S...) custom-call(s32[9]{0:T(128)S(1)} %fusion.16.starts, bf16[96,2304]{1,0:T(8,128)(2,1)S(1)} %pad_maximum_fusion.1.refs_0_, ...), custom_call_target="tpu_custom_call" | custom-call | flops 36238784 | bytes 251658 | tf_op jit(solution)/shard_map/ffn_forward/pallas_call | solution.py:150
  96.6 1.6 collective-permute-done.29
  98.9 10.6 %collective-permute-done.30.other = bf16[256,768]{1,0:T(8,128)(2,1)S(1)} collective-permute-done((bf16[256,768]{1,0:T(8,128)(2,1)S(1)}, bf16[256,768]{1,0:T(8,128)(2,1)S(1)}, u32[]{:S(2)}, u32[]{:S(2)}) %collective-permute-start.30) | collective-permute-done | bytes 393248 | tf_op jit(solution)/shard_map/ppermute | solution.py:47
  109.5 1.4 second_norm.1
  110.9 1.7 collective-permute-done.31.refs_1_.refs_3_
  112.7 3.2 %ffn_backward.1 = (bf16[512,1536]{1,0:T(8,128)(2,1)S(1)}, bf16[256,768]{1,0:T(8,128)(2,1)S(1)}, bf16[256,768]{1,0:T(8,128)(2,1)S(1)}) custom-call(bf16[256,768]{1,0:T(8,128)(2,1)S(1)} %get-tuple-element.191.refs_0_.refs_2_, bf16[256,768]{1,0:T(8,128)(2,1)S(1)} %collective-permute-done.31.refs_1_.refs_3_, bf16[768,1536]{1,0:T(8,128)(2,1)S(1)} %get-tuple-element.192.refs_2_, ...), custom_call_target="tpu_custom_call" | custom-call | flops 36238784 | bytes 196608 | tf_op jit(solution)/shard_map/ffn_backward/pallas_call | solution.py:150
  116.1 2.8 %ffn_grad.1 = (bf16[96,2304]{1,0:T(8,128)(2,1)S(1)}, bf16[96,2304]{1,0:T(8,128)(2,1)S(1)}, bf16[96,2304]{1,0:T(8,128)(2,1)S(1)}, bf16[96,2304]{1,0:T(8,128)(2,1)...) custom-call(s32[9]{0:T(128)S(1)} %fusion.32.starts, ...), custom_call_target="tpu_custom_call" | custom-call | flops 36238784 | bytes 149422 | tf_op jit(solution)/shard_map/ffn_grad/pallas_call | solution.py:150
  119.5 1.6 collective-permute-start.35
  121.8 4.9 %collective-permute-done.36 = bf16[48,2304]{1,0:T(8,128)(2,1)S(1)} collective-permute-done((bf16[48,2304]{1,0:T(8,128)(2,1)S(1)}, bf16[48,2304]{1,0:T(8,128)(2,1)S(1)}, u32[]{:S(2)}, u32[]{:S(2)}) %collective-permute-start.36) | collective-permute-done | bytes 221216 | tf_op jit(solution)/shard_map/ppermute | solution.py:42
  127.3 4.8 %collective-permute-done.33.other = bf16[256,768]{1,0:T(8,128)(2,1)S(1)} collective-permute-done((bf16[256,768]{1,0:T(8,128)(2,1)S(1)}, bf16[256,768]{1,0:T(8,128)(2,1)S(1)}, u32[]{:S(2)}, u32[]{:S(2)}) %collective-permute-start.33) | collective-permute-done | bytes 393248 | tf_op jit(solution)/shard_map/ppermute | solution.py:47
  133.0 1.6 collective-permute-start.41
  135.1 1.6 collective-permute-start.37
  137.1 1.3 collective-permute-done.42
  138.6 11.5 %query_grad.1.refs_4_ = f32[3,64,512]{2,1,0:T(8,128)S(1)} custom-call(bf16[3,80,512]{2,1,0:T(8,128)(2,1)S(1)} %get-tuple-element.153.refs_5_.q, bf16[240,512]{1,0:T(8,128)(2,1)S(1)} %prepare.1.g.refs_0_, bf16[3,80,4096]{2,1,0:T(8,128)(2,1)S(1)} %get-tuple-element.217.k.refs_2_.refs_3_, bf16[3,80,4096]{2,1,0:T(8,128)(2,1)S(1)} %get-tuple-element.218.v.refs_3_.refs_4_, ...), custom_call_target="tpu_custom_call" | custom-call | flops 96636768 | bytes 104202 | tf_op jit(solution)/shard_map/query_grad/pallas_call | solution.py:150
  150.9 1.6 collective-permute-start.39
  153.1 2.4 %key_grad.5 = (f32[3,64,512]{2,1,0:T(8,128)S(1)}, f32[3,64,512]{2,1,0:T(8,128)S(1)}, f32[1,24,256]{2,1,0:T(8,128)S(1)}) custom-call(s32[2]{0:T(128)S(1)} %broadcast_in_dim.210.slots, bf16[240,512]{1,0:T(8,128)(2,1)S(1)} %prepare.1.g.refs_0_, bf16[3,80,4096]{2,1,0:T(8,128)(2,1)S(1)} %get-tuple-element.224.refs_1_.refs_2_, ...), custom_call_target="tpu_custom_call" | custom-call | flops 16106127 | bytes 139100 | tf_op jit(solution)/shard_map/key_grad/pallas_call | solution.py:150
  155.5 3.9 %key_grad.6 = (f32[3,64,512]{2,1,0:T(8,128)S(1)}, f32[3,64,512]{2,1,0:T(8,128)S(1)}, f32[2,24,256]{2,1,0:T(8,128)S(1)}) custom-call(s32[2]{0:T(128)S(1)} %fusion.41.slots, bf16[240,512]{1,0:T(8,128)(2,1)S(1)} %collective-permute-done.37.refs_0_, bf16[240,512]{1,0:T(8,128)(2,1)S(1)} %collective-permute-done.38.refs_1_, ...), custom_call_target="tpu_custom_call" | custom-call | flops 32212254 | bytes 160235 | tf_op jit(solution)/shard_map/key_grad/pallas_call | solution.py:150
  159.7 1.5 collective-permute-start.43
  161.7 3.9 %key_grad.7 = (f32[3,64,512]{2,1,0:T(8,128)S(1)}, f32[3,64,512]{2,1,0:T(8,128)S(1)}, f32[2,24,256]{2,1,0:T(8,128)S(1)}) custom-call(s32[2]{0:T(128)S(1)} %fusion.40.slots, bf16[240,512]{1,0:T(8,128)(2,1)S(1)} %collective-permute-done.39.refs_0_, bf16[240,512]{1,0:T(8,128)(2,1)S(1)} %collective-permute-done.40.refs_1_, ...), custom_call_target="tpu_custom_call" | custom-call | flops 32212254 | bytes 160235 | tf_op jit(solution)/shard_map/key_grad/pallas_call | solution.py:150
  166.5 1.3 collective-permute-done.44.refs_1_
  167.8 1.5 collective-permute-start.45
  169.9 3.9 %key_grad.8 = (f32[3,64,512]{2,1,0:T(8,128)S(1)}, f32[3,64,512]{2,1,0:T(8,128)S(1)}, f32[2,24,256]{2,1,0:T(8,128)S(1)}) custom-call(s32[2]{0:T(128)S(1)} %fusion.39.slots, bf16[240,512]{1,0:T(8,128)(2,1)S(1)} %collective-permute-done.43.refs_0_, bf16[240,512]{1,0:T(8,128)(2,1)S(1)} %collective-permute-done.44.refs_1_, ...), custom_call_target="tpu_custom_call" | custom-call | flops 32212254 | bytes 160235 | tf_op jit(solution)/shard_map/key_grad/pallas_call | solution.py:150
  174.3 2.5 %key_grad.9 = (f32[3,64,512]{2,1,0:T(8,128)S(1)}, f32[3,64,512]{2,1,0:T(8,128)S(1)}, f32[1,24,256]{2,1,0:T(8,128)S(1)}) custom-call(s32[2]{0:T(128)S(1)} %fusion.42.slots, bf16[240,256]{1,0:T(8,128)(2,1)S(1)} %collective-permute-done.45.refs_0_, bf16[240,256]{1,0:T(8,128)(2,1)S(1)} %collective-permute-done.46.refs_1_, ...), custom_call_target="tpu_custom_call" | custom-call | flops 16106127 | bytes 154828 | tf_op jit(solution)/shard_map/key_grad/pallas_call | solution.py:150
  176.7 1.9 late_grad.1
  179.6 1.6 collective-permute-start.57
  181.2 1.5 collective-permute-start.49
  184.5 6.5 %collective-permute-done.49 = bf16[48,768]{1,0:T(8,128)(2,1)S(1)} collective-permute-done((bf16[48,768]{1,0:T(8,128)(2,1)S(1)}, bf16[48,768]{1,0:T(8,128)(2,1)S(1)}, u32[]{:S(2)}, u32[]{:S(2)}) %collective-permute-start.49) | collective-permute-done | bytes 73760 | tf_op jit(solution)/shard_map/ppermute | solution.py:37
  191.0 1.6 collective-permute-start.50
  193.2 4.6 %collective-permute-done.50 = bf16[96,768]{1,0:T(8,128)(2,1)S(1)} collective-permute-done((bf16[96,768]{1,0:T(8,128)(2,1)S(1)}, bf16[96,768]{1,0:T(8,128)(2,1)S(1)}, u32[]{:S(2)}, u32[]{:S(2)}) %collective-permute-start.50) | collective-permute-done | bytes 147488 | tf_op jit(solution)/shard_map/ppermute | solution.py:37
  197.9 1.5 collective-permute-start.51
  200.3 1.5 collective-permute-start.58
  202.4 2.0 collective-permute-done.51
  204.5 1.6 collective-permute-start.52
  208.0 1.5 collective-permute-done.56.back
  209.5 1.3 collective-permute-done.52.ahead
  (195 shorter events, 34.7 us)
Async XLA Ops:
  0.6 14.9 %copy-start.10 = (s32[9]{0:T(128)S(1)}, s32[9]{0:T(128)}, u32[]{:S(2)}) copy-start(s32[9]{0:T(128)} %constant.28.clone) | copy-start | bytes 112
  0.7 14.9 %copy-start.11 = (s32[9]{0:T(128)S(1)}, s32[9]{0:T(128)}, u32[]{:S(2)}) copy-start(s32[9]{0:T(128)} %constant.65.clone) | copy-start | bytes 112
  2.4 13.7 %copy-start.3 = (s32[4096]{0:T(1024)S(1)}, s32[4096]{0:T(1024)}, u32[]{:S(2)}) copy-start(s32[4096]{0:T(1024)} %param.30) | copy-start | bytes 49156
  3.5 12.2 %collective-permute-start = (bf16[224,768]{1,0:T(8,128)(2,1)S(1)}, bf16[224,768]{1,0:T(8,128)(2,1)S(1)}, u32[]{:S(2)}, u32[]{:S(2)}) collective-permute-start(bf16[224,768]{1,0:T(8,128)(2,1)S(1)} %pack.1.refs_0_), channel_id=1, source_target_pairs={{0,8},{8,16},{16,24},{24,28},{28,20},{20,12},{12,4},{4,0},{1,9},{9... | collective-permute-start | bytes 1032200 | tf_op jit(solution)/shard_map/ppermute | solution.py:37
  6.6 9.5 %collective-permute-start.3 = (bf16[224,768]{1,0:T(8,128)(2,1)S(1)}, bf16[224,768]{1,0:T(8,128)(2,1)S(1)}, u32[]{:S(2)}, u32[]{:S(2)}) collective-permute-start(bf16[224,768]{1,0:T(8,128)(2,1)S(1)} %pack.1.refs_0_), channel_id=1, source_target_pairs={{8,0},{16,8},{24,16},{28,24},{20,28},{12,20},{4,12},{0,4},{9,1},{1... | collective-permute-start | bytes 1032200 | tf_op jit(solution)/shard_map/ppermute | solution.py:42
  6.6 9.0 %collective-permute-start.20 = (bf16[128,768]{1,0:T(8,128)(2,1)}, bf16[128,768]{1,0:T(8,128)(2,1)S(1)}, u32[]{:S(2)}, u32[]{:S(2)}) collective-permute-start(bf16[128,768]{1,0:T(8,128)(2,1)} %tokens.1), channel_id=1, source_target_pairs={{0,2},{1,3},{2,0},{3,1},{4,6},{5,7},{6,4},{7,5},{8,10},{9,11},{10,... | collective-permute-start | bytes 589832 | tf_op jit(solution)/shard_map/ppermute | solution.py:47
  17.1 12.0 %collective-permute-start.16 = (bf16[256,768]{1,0:T(8,128)(2,1)S(1)}, bf16[256,768]{1,0:T(8,128)(2,1)S(1)}, u32[]{:S(2)}, u32[]{:S(2)}) collective-permute-start(bf16[256,768]{1,0:T(8,128)(2,1)S(1)} %pad_maximum_fusion.4), channel_id=1, source_target_pairs={{0,2},{1,3},{2,0},{3,1},{4,6},{5,7},{6,4},{7,5},{8,10},{9,11},{10,... | collective-permute-start | bytes 1179656 | tf_op jit(solution)/shard_map/ppermute | solution.py:47
  18.7 8.3 %collective-permute-start.1 = (bf16[224,768]{1,0:T(8,128)(2,1)S(1)}, bf16[224,768]{1,0:T(8,128)(2,1)S(1)}, u32[]{:S(2)}, u32[]{:S(2)}) collective-permute-start(bf16[224,768]{1,0:T(8,128)(2,1)S(1)} %collective-permute-done.refs_1_), channel_id=1, source_target_pairs={{0,8},{8,16},{16,24},{24,28},{28,20},{20,12},{12,4},{4,0},{1,9},{9... | collective-permute-start | bytes 1032200 | tf_op jit(solution)/shard_map/ppermute | solution.py:37
  20.3 8.3 %collective-permute-start.4 = (bf16[224,768]{1,0:T(8,128)(2,1)S(1)}, bf16[224,768]{1,0:T(8,128)(2,1)S(1)}, u32[]{:S(2)}, u32[]{:S(2)}) collective-permute-start(bf16[224,768]{1,0:T(8,128)(2,1)S(1)} %collective-permute-done.3.refs_2_), channel_id=1, source_target_pairs={{8,0},{16,8},{24,16},{28,24},{20,28},{12,20},{4,12},{0,4},{9,1},{1... | collective-permute-start | bytes 1032200 | tf_op jit(solution)/shard_map/ppermute | solution.py:42
  27.0 8.2 %collective-permute-start.2 = (bf16[224,768]{1,0:T(8,128)(2,1)S(1)}, bf16[224,768]{1,0:T(8,128)(2,1)S(1)}, u32[]{:S(2)}, u32[]{:S(2)}) collective-permute-start(bf16[224,768]{1,0:T(8,128)(2,1)S(1)} %collective-permute-done.1.refs_3_), channel_id=1, source_target_pairs={{0,8},{8,16},{16,24},{24,28},{28,20},{20,12},{12,4},{4,0},{1,9},{9... | collective-permute-start | bytes 1032200 | tf_op jit(solution)/shard_map/ppermute | solution.py:37
  28.6 8.2 %collective-permute-start.5 = (bf16[224,768]{1,0:T(8,128)(2,1)S(1)}, bf16[224,768]{1,0:T(8,128)(2,1)S(1)}, u32[]{:S(2)}, u32[]{:S(2)}) collective-permute-start(bf16[224,768]{1,0:T(8,128)(2,1)S(1)} %collective-permute-done.4.refs_4_), channel_id=1, source_target_pairs={{8,0},{16,8},{24,16},{28,24},{20,28},{12,20},{4,12},{0,4},{9,1},{1... | collective-permute-start | bytes 1032200 | tf_op jit(solution)/shard_map/ppermute | solution.py:42
  29.2 10.2 %collective-permute-start.17 = (bf16[256,768]{1,0:T(8,128)(2,1)S(1)}, bf16[256,768]{1,0:T(8,128)(2,1)S(1)}, u32[]{:S(2)}, u32[]{:S(2)}) collective-permute-start(bf16[256,768]{1,0:T(8,128)(2,1)S(1)} %pad_maximum_fusion.5), channel_id=1, source_target_pairs={{0,2},{1,3},{2,0},{3,1},{4,6},{5,7},{6,4},{7,5},{8,10},{9,11},{10,... | collective-permute-start | bytes 1179656 | tf_op jit(solution)/shard_map/ppermute | solution.py:47
  35.2 7.4 %collective-permute-start.14 = (bf16[112,768]{1,0:T(8,128)(2,1)S(1)}, bf16[112,768]{1,0:T(8,128)(2,1)S(1)}, u32[]{:S(2)}, u32[]{:S(2)}) collective-permute-start(bf16[112,768]{1,0:T(8,128)(2,1)S(1)} %slice.160), channel_id=1, source_target_pairs={{0,8},{8,16},{16,24},{24,28},{28,20},{20,12},{12,4},{4,0},{1,9},{9... | collective-permute-start | bytes 516104 | tf_op jit(solution)/shard_map/ppermute | solution.py:37
  36.9 7.4 %collective-permute-start.15 = (bf16[112,768]{1,0:T(8,128)(2,1)S(1)}, bf16[112,768]{1,0:T(8,128)(2,1)S(1)}, u32[]{:S(2)}, u32[]{:S(2)}) collective-permute-start(bf16[112,768]{1,0:T(8,128)(2,1)S(1)} %slice.161), channel_id=1, source_target_pairs={{8,0},{16,8},{24,16},{28,24},{20,28},{12,20},{4,12},{0,4},{9,1},{1... | collective-permute-start | bytes 516104 | tf_op jit(solution)/shard_map/ppermute | solution.py:42
  37.4 12.8 %collective-permute-start.6 = (bf16[96,2304]{1,0:T(8,128)(2,1)S(1)}, bf16[96,2304]{1,0:T(8,128)(2,1)S(1)}, u32[]{:S(2)}, u32[]{:S(2)}) collective-permute-start(bf16[96,2304]{1,0:T(8,128)(2,1)S(1)} %pad_maximum_fusion.1.refs_0_), channel_id=1, source_target_pairs={{0,8},{8,16},{16,24},{24,28},{28,20},{20,12},{12,4},{4,0},{1,9},{9... | collective-permute-start | bytes 1327112 | tf_op jit(solution)/shard_map/ppermute | solution.py:37
  38.9 11.3 %collective-permute-start.7 = (bf16[96,2304]{1,0:T(8,128)(2,1)S(1)}, bf16[96,2304]{1,0:T(8,128)(2,1)S(1)}, u32[]{:S(2)}, u32[]{:S(2)}) collective-permute-start(bf16[96,2304]{1,0:T(8,128)(2,1)S(1)} %pad_maximum_fusion.1.refs_0_), channel_id=1, source_target_pairs={{8,0},{16,8},{24,16},{28,24},{20,28},{12,20},{4,12},{0,4},{9,1},{1... | collective-permute-start | bytes 1327112 | tf_op jit(solution)/shard_map/ppermute | solution.py:42
  39.5 7.8 %collective-permute-start.18 = (bf16[256,768]{1,0:T(8,128)(2,1)S(1)}, bf16[256,768]{1,0:T(8,128)(2,1)S(1)}, u32[]{:S(2)}, u32[]{:S(2)}) collective-permute-start(bf16[256,768]{1,0:T(8,128)(2,1)S(1)} %pad_maximum_fusion.6), channel_id=1, source_target_pairs={{0,2},{1,3},{2,0},{3,1},{4,6},{5,7},{6,4},{7,5},{8,10},{9,11},{10,... | collective-permute-start | bytes 1179656 | tf_op jit(solution)/shard_map/ppermute | solution.py:47
  44.2 3.2 %collective-permute-start.21 = (bf16[256,768]{1,0:T(8,128)(2,1)S(1)}, bf16[256,768]{1,0:T(8,128)(2,1)S(1)}, u32[]{:S(2)}, u32[]{:S(2)}) collective-permute-start(bf16[256,768]{1,0:T(8,128)(2,1)S(1)} %constant_dynamic-update-slice_fusion.15.refs_0_.tokens), channel_id=1, source_target_pairs={{0,1},{1,0},{2,3},{3,2},{4,5},{5,4},{6,7},{7,6},{8,9},{9,8},{10,11... | collective-permute-start | bytes 1179656 | tf_op jit(solution)/shard_map/ppermute | solution.py:47
  44.6 8.1 %collective-permute-start.23 = (bf16[512,768]{1,0:T(8,128)(2,1)S(1)}, bf16[512,768]{1,0:T(8,128)(2,1)S(1)}, u32[]{:S(2)}, u32[]{:S(2)}) collective-permute-start(bf16[512,768]{1,0:T(8,128)(2,1)S(1)} %constant_dynamic-update-slice_fusion.refs_0_), channel_id=1, source_target_pairs={{0,1},{1,0},{2,3},{3,2},{4,5},{5,4},{6,7},{7,6},{8,9},{9,8},{10,11... | collective-permute-start | bytes 2359304 | tf_op jit(solution)/shard_map/ppermute | solution.py:47
  50.2 11.8 %collective-permute-start.22 = (bf16[512,768]{1,0:T(8,128)(2,1)S(1)}, bf16[512,768]{1,0:T(8,128)(2,1)S(1)}, u32[]{:S(2)}, u32[]{:S(2)}) collective-permute-start(bf16[512,768]{1,0:T(8,128)(2,1)S(1)} %constant_dynamic-update-slice_fusion.5.refs_0_), channel_id=1, source_target_pairs={{0,1},{1,0},{2,3},{3,2},{4,5},{5,4},{6,7},{7,6},{8,9},{9,8},{10,11... | collective-permute-start | bytes 2359304 | tf_op jit(solution)/shard_map/ppermute | solution.py:47
  50.4 11.6 %collective-permute-start.19 = (bf16[256,768]{1,0:T(8,128)(2,1)S(1)}, bf16[256,768]{1,0:T(8,128)(2,1)S(1)}, u32[]{:S(2)}, u32[]{:S(2)}) collective-permute-start(bf16[256,768]{1,0:T(8,128)(2,1)S(1)} %pad_maximum_fusion.7), channel_id=1, source_target_pairs={{0,2},{1,3},{2,0},{3,1},{4,6},{5,7},{6,4},{7,5},{8,10},{9,11},{10,... | collective-permute-start | bytes 1179656 | tf_op jit(solution)/shard_map/ppermute | solution.py:47
  50.6 15.7 %collective-permute-start.8 = (bf16[96,2304]{1,0:T(8,128)(2,1)S(1)}, bf16[96,2304]{1,0:T(8,128)(2,1)S(1)}, u32[]{:S(2)}, u32[]{:S(2)}) collective-permute-start(bf16[96,2304]{1,0:T(8,128)(2,1)S(1)} %collective-permute-done.6.refs_1_), channel_id=1, source_target_pairs={{0,8},{8,16},{16,24},{24,28},{28,20},{20,12},{12,4},{4,0},{1,9},{9... | collective-permute-start | bytes 1327112 | tf_op jit(solution)/shard_map/ppermute | solution.py:37
  52.5 13.9 %collective-permute-start.9 = (bf16[96,2304]{1,0:T(8,128)(2,1)S(1)}, bf16[96,2304]{1,0:T(8,128)(2,1)S(1)}, u32[]{:S(2)}, u32[]{:S(2)}) collective-permute-start(bf16[96,2304]{1,0:T(8,128)(2,1)S(1)} %collective-permute-done.7.refs_2_), channel_id=1, source_target_pairs={{8,0},{16,8},{24,16},{28,24},{20,28},{12,20},{4,12},{0,4},{9,1},{1... | collective-permute-start | bytes 1327112 | tf_op jit(solution)/shard_map/ppermute | solution.py:42
  57.0 11.5 %collective-permute-start.25 = (bf16[512,768]{1,0:T(8,128)(2,1)S(1)}, bf16[512,768]{1,0:T(8,128)(2,1)S(1)}, u32[]{:S(2)}, u32[]{:S(2)}) collective-permute-start(bf16[512,768]{1,0:T(8,128)(2,1)S(1)} %constant_dynamic-update-slice_fusion.10.refs_0_), channel_id=1, source_target_pairs={{0,1},{1,0},{2,3},{3,2},{4,5},{5,4},{6,7},{7,6},{8,9},{9,8},{10,11... | collective-permute-start | bytes 2359304 | tf_op jit(solution)/shard_map/ppermute | solution.py:47
  66.4 6.5 %collective-permute-start.24 = (bf16[256,768]{1,0:T(8,128)(2,1)S(1)}, bf16[256,768]{1,0:T(8,128)(2,1)S(1)}, u32[]{:S(2)}, u32[]{:S(2)}) collective-permute-start(bf16[256,768]{1,0:T(8,128)(2,1)S(1)} %pad_maximum_fusion.8.refs_0_), channel_id=1, source_target_pairs={{0,1},{1,0},{2,3},{3,2},{4,5},{5,4},{6,7},{7,6},{8,9},{9,8},{10,11... | collective-permute-start | bytes 1179656 | tf_op jit(solution)/shard_map/ppermute | solution.py:47
  66.5 12.6 %collective-permute-start.10 = (bf16[96,2304]{1,0:T(8,128)(2,1)S(1)}, bf16[96,2304]{1,0:T(8,128)(2,1)S(1)}, u32[]{:S(2)}, u32[]{:S(2)}) collective-permute-start(bf16[96,2304]{1,0:T(8,128)(2,1)S(1)} %collective-permute-done.8.refs_3_), channel_id=1, source_target_pairs={{0,8},{8,16},{16,24},{24,28},{28,20},{20,12},{12,4},{4,0},{1,9},{9... | collective-permute-start | bytes 1327112 | tf_op jit(solution)/shard_map/ppermute | solution.py:37
  68.1 12.2 %collective-permute-start.11 = (bf16[96,2304]{1,0:T(8,128)(2,1)S(1)}, bf16[96,2304]{1,0:T(8,128)(2,1)S(1)}, u32[]{:S(2)}, u32[]{:S(2)}) collective-permute-start(bf16[96,2304]{1,0:T(8,128)(2,1)S(1)} %collective-permute-done.9.refs_4_), channel_id=1, source_target_pairs={{8,0},{16,8},{24,16},{28,24},{20,28},{12,20},{4,12},{0,4},{9,1},{1... | collective-permute-start | bytes 1327112 | tf_op jit(solution)/shard_map/ppermute | solution.py:42
  76.0 4.3 %collective-permute-start.26 = (bf16[256,768]{1,0:T(8,128)(2,1)S(1)}, bf16[256,768]{1,0:T(8,128)(2,1)S(1)}, u32[]{:S(2)}, u32[]{:S(2)}) collective-permute-start(bf16[256,768]{1,0:T(8,128)(2,1)S(1)} %get-tuple-element.184), channel_id=1, source_target_pairs={{0,1},{1,0},{2,3},{3,2},{4,5},{5,4},{6,7},{7,6},{8,9},{9,8},{10,11... | collective-permute-start | bytes 1179656 | tf_op jit(solution)/shard_map/ppermute | solution.py:47
  80.4 10.4 %collective-permute-start.27 = (bf16[256,768]{1,0:T(8,128)(2,1)S(1)}, bf16[256,768]{1,0:T(8,128)(2,1)S(1)}, u32[]{:S(2)}, u32[]{:S(2)}) collective-permute-start(bf16[256,768]{1,0:T(8,128)(2,1)S(1)} %add_convert_fusion.7.mine), channel_id=1, source_target_pairs={{0,2},{1,3},{2,0},{3,1},{4,6},{5,7},{6,4},{7,5},{8,10},{9,11},{10,... | collective-permute-start | bytes 1179656 | tf_op jit(solution)/shard_map/ppermute | solution.py:47
  81.0 6.4 %collective-permute-start.12 = (bf16[48,2304]{1,0:T(8,128)(2,1)S(1)}, bf16[48,2304]{1,0:T(8,128)(2,1)S(1)}, u32[]{:S(2)}, u32[]{:S(2)}) collective-permute-start(bf16[48,2304]{1,0:T(8,128)(2,1)S(1)} %slice.158), channel_id=1, source_target_pairs={{0,8},{8,16},{16,24},{24,28},{28,20},{20,12},{12,4},{4,0},{1,9},{9... | collective-permute-start | bytes 663560 | tf_op jit(solution)/shard_map/ppermute | solution.py:37
  82.7 6.2 %collective-permute-start.13 = (bf16[48,2304]{1,0:T(8,128)(2,1)S(1)}, bf16[48,2304]{1,0:T(8,128)(2,1)S(1)}, u32[]{:S(2)}, u32[]{:S(2)}) collective-permute-start(bf16[48,2304]{1,0:T(8,128)(2,1)S(1)} %slice.159), channel_id=1, source_target_pairs={{8,0},{16,8},{24,16},{28,24},{20,28},{12,20},{4,12},{0,4},{9,1},{1... | collective-permute-start | bytes 663560 | tf_op jit(solution)/shard_map/ppermute | solution.py:42
  91.2 1.8 collective-permute-start.28
  96.4 1.8 collective-permute-start.29
  98.3 11.2 %collective-permute-start.30 = (bf16[256,768]{1,0:T(8,128)(2,1)S(1)}, bf16[256,768]{1,0:T(8,128)(2,1)S(1)}, u32[]{:S(2)}, u32[]{:S(2)}) collective-permute-start(bf16[256,768]{1,0:T(8,128)(2,1)S(1)} %add_convert_fusion.6.mine), channel_id=1, source_target_pairs={{0,2},{1,3},{2,0},{3,1},{4,6},{5,7},{6,4},{7,5},{8,10},{9,11},{10,... | collective-permute-start | bytes 1179656 | tf_op jit(solution)/shard_map/ppermute | solution.py:47
  110.9 1.7 collective-permute-start.31
  115.9 5.2 %collective-permute-start.32 = (bf16[256,768]{1,0:T(8,128)(2,1)S(1)}, bf16[256,768]{1,0:T(8,128)(2,1)S(1)}, u32[]{:S(2)}, u32[]{:S(2)}) collective-permute-start(bf16[256,768]{1,0:T(8,128)(2,1)S(1)} %get-tuple-element.196), channel_id=1, source_target_pairs={{0,1},{1,0},{2,3},{3,2},{4,5},{5,4},{6,7},{7,6},{8,9},{9,8},{10,11... | collective-permute-start | bytes 1179656 | tf_op jit(solution)/shard_map/ppermute | solution.py:47
  118.9 7.8 %collective-permute-start.36 = (bf16[48,2304]{1,0:T(8,128)(2,1)S(1)}, bf16[48,2304]{1,0:T(8,128)(2,1)S(1)}, u32[]{:S(2)}, u32[]{:S(2)}) collective-permute-start(bf16[48,2304]{1,0:T(8,128)(2,1)S(1)} %get-tuple-element.204), channel_id=1, source_target_pairs={{8,0},{16,8},{24,16},{28,24},{20,28},{12,20},{4,12},{0,4},{9,1},{1... | collective-permute-start | bytes 663560 | tf_op jit(solution)/shard_map/ppermute | solution.py:42
  119.5 13.4 %collective-permute-start.35 = (bf16[48,2304]{1,0:T(8,128)(2,1)S(1)}, bf16[48,2304]{1,0:T(8,128)(2,1)S(1)}, u32[]{:S(2)}, u32[]{:S(2)}) collective-permute-start(bf16[48,2304]{1,0:T(8,128)(2,1)S(1)} %get-tuple-element.203), channel_id=1, source_target_pairs={{0,8},{8,16},{16,24},{24,28},{28,20},{20,12},{12,4},{4,0},{1,9},{9... | collective-permute-start | bytes 663560 | tf_op jit(solution)/shard_map/ppermute | solution.py:37
  121.2 10.9 %collective-permute-start.33 = (bf16[256,768]{1,0:T(8,128)(2,1)S(1)}, bf16[256,768]{1,0:T(8,128)(2,1)S(1)}, u32[]{:S(2)}, u32[]{:S(2)}) collective-permute-start(bf16[256,768]{1,0:T(8,128)(2,1)S(1)} %add_convert_fusion.5.mine), channel_id=1, source_target_pairs={{0,2},{1,3},{2,0},{3,1},{4,6},{5,7},{6,4},{7,5},{8,10},{9,11},{10,... | collective-permute-start | bytes 1179656 | tf_op jit(solution)/shard_map/ppermute | solution.py:47
  126.8 11.7 %collective-permute-start.42 = (bf16[96,2304]{1,0:T(8,128)(2,1)S(1)}, bf16[96,2304]{1,0:T(8,128)(2,1)S(1)}, u32[]{:S(2)}, u32[]{:S(2)}) collective-permute-start(bf16[96,2304]{1,0:T(8,128)(2,1)S(1)} %pad_maximum_fusion.3), channel_id=1, source_target_pairs={{8,0},{16,8},{24,16},{28,24},{20,28},{12,20},{4,12},{0,4},{9,1},{1... | collective-permute-start | bytes 1327112 | tf_op jit(solution)/shard_map/ppermute | solution.py:42
  132.8 1.8 collective-permute-start.34
  133.0 20.0 %collective-permute-start.41 = (bf16[96,2304]{1,0:T(8,128)(2,1)S(1)}, bf16[96,2304]{1,0:T(8,128)(2,1)S(1)}, u32[]{:S(2)}, u32[]{:S(2)}) collective-permute-start(bf16[96,2304]{1,0:T(8,128)(2,1)S(1)} %pad_maximum_fusion.2), channel_id=1, source_target_pairs={{0,8},{8,16},{16,24},{24,28},{28,20},{20,12},{12,4},{4,0},{1,9},{9... | collective-permute-start | bytes 1327112 | tf_op jit(solution)/shard_map/ppermute | solution.py:37
  135.1 15.8 %collective-permute-start.37 = (bf16[240,512]{1,0:T(8,128)(2,1)S(1)}, bf16[240,512]{1,0:T(8,128)(2,1)S(1)}, u32[]{:S(2)}, u32[]{:S(2)}) collective-permute-start(bf16[240,512]{1,0:T(8,128)(2,1)S(1)} %prepare.1.g.refs_0_), channel_id=1, source_target_pairs={{0,8},{8,16},{16,24},{24,28},{28,20},{20,12},{12,4},{4,0},{1,9},{9... | collective-permute-start | bytes 737288 | tf_op jit(solution)/shard_map/ppermute | solution.py:37
  136.7 14.2 %collective-permute-start.38 = (bf16[240,512]{1,0:T(8,128)(2,1)S(1)}, bf16[240,512]{1,0:T(8,128)(2,1)S(1)}, u32[]{:S(2)}, u32[]{:S(2)}) collective-permute-start(bf16[240,512]{1,0:T(8,128)(2,1)S(1)} %prepare.1.g.refs_0_), channel_id=1, source_target_pairs={{8,0},{16,8},{24,16},{28,24},{20,28},{12,20},{4,12},{0,4},{9,1},{1... | collective-permute-start | bytes 737288 | tf_op jit(solution)/shard_map/ppermute | solution.py:42
  150.9 8.6 %collective-permute-start.39 = (bf16[240,512]{1,0:T(8,128)(2,1)S(1)}, bf16[240,512]{1,0:T(8,128)(2,1)S(1)}, u32[]{:S(2)}, u32[]{:S(2)}) collective-permute-start(bf16[240,512]{1,0:T(8,128)(2,1)S(1)} %collective-permute-done.37.refs_0_), channel_id=1, source_target_pairs={{0,8},{8,16},{16,24},{24,28},{28,20},{20,12},{12,4},{4,0},{1,9},{9... | collective-permute-start | bytes 737288 | tf_op jit(solution)/shard_map/ppermute | solution.py:37
  152.5 7.2 %collective-permute-start.40 = (bf16[240,512]{1,0:T(8,128)(2,1)S(1)}, bf16[240,512]{1,0:T(8,128)(2,1)S(1)}, u32[]{:S(2)}, u32[]{:S(2)}) collective-permute-start(bf16[240,512]{1,0:T(8,128)(2,1)S(1)} %collective-permute-done.38.refs_1_), channel_id=1, source_target_pairs={{8,0},{16,8},{24,16},{28,24},{20,28},{12,20},{4,12},{0,4},{9,1},{1... | collective-permute-start | bytes 737288 | tf_op jit(solution)/shard_map/ppermute | solution.py:42
  159.7 6.8 %collective-permute-start.43 = (bf16[240,512]{1,0:T(8,128)(2,1)S(1)}, bf16[240,512]{1,0:T(8,128)(2,1)S(1)}, u32[]{:S(2)}, u32[]{:S(2)}) collective-permute-start(bf16[240,512]{1,0:T(8,128)(2,1)S(1)} %collective-permute-done.39.refs_0_), channel_id=1, source_target_pairs={{0,8},{8,16},{16,24},{24,28},{28,20},{20,12},{12,4},{4,0},{1,9},{9... | collective-permute-start | bytes 737288 | tf_op jit(solution)/shard_map/ppermute | solution.py:37
  161.2 6.6 %collective-permute-start.44 = (bf16[240,512]{1,0:T(8,128)(2,1)S(1)}, bf16[240,512]{1,0:T(8,128)(2,1)S(1)}, u32[]{:S(2)}, u32[]{:S(2)}) collective-permute-start(bf16[240,512]{1,0:T(8,128)(2,1)S(1)} %collective-permute-done.40.refs_1_), channel_id=1, source_target_pairs={{8,0},{16,8},{24,16},{28,24},{20,28},{12,20},{4,12},{0,4},{9,1},{1... | collective-permute-start | bytes 737288 | tf_op jit(solution)/shard_map/ppermute | solution.py:42
  167.8 6.1 %collective-permute-start.45 = (bf16[240,256]{1,0:T(8,128)(2,1)S(1)}, bf16[240,256]{1,0:T(8,128)(2,1)S(1)}, u32[]{:S(2)}, u32[]{:S(2)}) collective-permute-start(bf16[240,256]{1,0:T(8,128)(2,1)S(1)} %slice.146), channel_id=1, source_target_pairs={{0,8},{8,16},{16,24},{24,28},{28,20},{20,12},{12,4},{4,0},{1,9},{9... | collective-permute-start | bytes 368648 | tf_op jit(solution)/shard_map/ppermute | solution.py:37
  169.3 4.9 %collective-permute-start.46 = (bf16[240,256]{1,0:T(8,128)(2,1)S(1)}, bf16[240,256]{1,0:T(8,128)(2,1)S(1)}, u32[]{:S(2)}, u32[]{:S(2)}) collective-permute-start(bf16[240,256]{1,0:T(8,128)(2,1)S(1)} %slice.147), channel_id=1, source_target_pairs={{8,0},{16,8},{24,16},{28,24},{20,28},{12,20},{4,12},{0,4},{9,1},{1... | collective-permute-start | bytes 368648 | tf_op jit(solution)/shard_map/ppermute | solution.py:42
  178.6 5.3 %collective-permute-start.53 = (bf16[48,768]{1,0:T(8,128)(2,1)S(1)}, bf16[48,768]{1,0:T(8,128)(2,1)S(1)}, u32[]{:S(2)}, u32[]{:S(2)}) collective-permute-start(bf16[48,768]{1,0:T(8,128)(2,1)S(1)} %get-tuple-element.252), channel_id=1, source_target_pairs={{8,0},{16,8},{24,16},{28,24},{20,28},{12,20},{4,12},{0,4},{9,1},{1... | collective-permute-start | bytes 221192 | tf_op jit(solution)/shard_map/ppermute | solution.py:42
  179.2 20.2 %collective-permute-start.59 = (bf16[96,2304]{1,0:T(8,128)(2,1)S(1)}, bf16[96,2304]{1,0:T(8,128)(2,1)S(1)}, u32[]{:S(2)}, u32[]{:S(2)}) collective-permute-start(bf16[96,2304]{1,0:T(8,128)(2,1)S(1)} %add_convert_fusion.2), channel_id=1, source_target_pairs={{8,0},{16,8},{24,16},{28,24},{20,28},{12,20},{4,12},{0,4},{9,1},{1... | collective-permute-start | bytes 1327112 | tf_op jit(solution)/shard_map/ppermute | solution.py:42
  179.6 20.5 %collective-permute-start.57 = (bf16[96,2304]{1,0:T(8,128)(2,1)S(1)}, bf16[96,2304]{1,0:T(8,128)(2,1)S(1)}, u32[]{:S(2)}, u32[]{:S(2)}) collective-permute-start(bf16[96,2304]{1,0:T(8,128)(2,1)S(1)} %add_convert_fusion.3), channel_id=1, source_target_pairs={{0,8},{8,16},{16,24},{24,28},{28,20},{20,12},{12,4},{4,0},{1,9},{9... | collective-permute-start | bytes 1327112 | tf_op jit(solution)/shard_map/ppermute | solution.py:37
  181.2 9.8 %collective-permute-start.49 = (bf16[48,768]{1,0:T(8,128)(2,1)S(1)}, bf16[48,768]{1,0:T(8,128)(2,1)S(1)}, u32[]{:S(2)}, u32[]{:S(2)}) collective-permute-start(bf16[48,768]{1,0:T(8,128)(2,1)S(1)} %get-tuple-element.247), channel_id=1, source_target_pairs={{0,8},{8,16},{16,24},{24,28},{28,20},{20,12},{12,4},{4,0},{1,9},{9... | collective-permute-start | bytes 221192 | tf_op jit(solution)/shard_map/ppermute | solution.py:37
  182.7 23.3 %collective-permute-start.47 = (bf16[256,768]{1,0:T(8,128)(2,1)S(1)}, bf16[256,768]{1,0:T(8,128)(2,1)S(1)}, u32[]{:S(2)}, u32[]{:S(2)}) collective-permute-start(bf16[256,768]{1,0:T(8,128)(2,1)S(1)} %get-tuple-element.245), channel_id=1, source_target_pairs={{0,1},{1,0},{2,3},{3,2},{4,5},{5,4},{6,7},{7,6},{8,9},{9,8},{10,11... | collective-permute-start | bytes 1179656 | tf_op jit(solution)/shard_map/ppermute | solution.py:47
  183.9 8.8 %collective-permute-start.54 = (bf16[96,768]{1,0:T(8,128)(2,1)S(1)}, bf16[96,768]{1,0:T(8,128)(2,1)S(1)}, u32[]{:S(2)}, u32[]{:S(2)}) collective-permute-start(bf16[96,768]{1,0:T(8,128)(2,1)S(1)} %pad_maximum_fusion.12), channel_id=1, source_target_pairs={{8,0},{16,8},{24,16},{28,24},{20,28},{12,20},{4,12},{0,4},{9,1},{1... | collective-permute-start | bytes 442376 | tf_op jit(solution)/shard_map/ppermute | solution.py:42
  191.0 6.8 %collective-permute-start.50 = (bf16[96,768]{1,0:T(8,128)(2,1)S(1)}, bf16[96,768]{1,0:T(8,128)(2,1)S(1)}, u32[]{:S(2)}, u32[]{:S(2)}) collective-permute-start(bf16[96,768]{1,0:T(8,128)(2,1)S(1)} %pad_maximum_fusion.11), channel_id=1, source_target_pairs={{0,8},{8,16},{16,24},{24,28},{28,20},{20,12},{12,4},{4,0},{1,9},{9... | collective-permute-start | bytes 442376 | tf_op jit(solution)/shard_map/ppermute | solution.py:37
  192.7 9.1 %collective-permute-start.55 = (bf16[96,768]{1,0:T(8,128)(2,1)S(1)}, bf16[96,768]{1,0:T(8,128)(2,1)S(1)}, u32[]{:S(2)}, u32[]{:S(2)}) collective-permute-start(bf16[96,768]{1,0:T(8,128)(2,1)S(1)} %add_convert_fusion.11), channel_id=1, source_target_pairs={{8,0},{16,8},{24,16},{28,24},{20,28},{12,20},{4,12},{0,4},{9,1},{1... | collective-permute-start | bytes 442376 | tf_op jit(solution)/shard_map/ppermute | solution.py:42
  197.9 6.5 %collective-permute-start.51 = (bf16[96,768]{1,0:T(8,128)(2,1)S(1)}, bf16[96,768]{1,0:T(8,128)(2,1)S(1)}, u32[]{:S(2)}, u32[]{:S(2)}) collective-permute-start(bf16[96,768]{1,0:T(8,128)(2,1)S(1)} %add_convert_fusion.13), channel_id=1, source_target_pairs={{0,8},{8,16},{16,24},{24,28},{28,20},{20,12},{12,4},{4,0},{1,9},{9... | collective-permute-start | bytes 442376 | tf_op jit(solution)/shard_map/ppermute | solution.py:37
  199.5 13.2 %collective-permute-start.60 = (bf16[96,2304]{1,0:T(8,128)(2,1)S(1)}, bf16[96,2304]{1,0:T(8,128)(2,1)S(1)}, u32[]{:S(2)}, u32[]{:S(2)}) collective-permute-start(bf16[96,2304]{1,0:T(8,128)(2,1)S(1)} %add_convert_fusion), channel_id=1, source_target_pairs={{8,0},{16,8},{24,16},{28,24},{20,28},{12,20},{4,12},{0,4},{9,1},{1... | collective-permute-start | bytes 1327112 | tf_op jit(solution)/shard_map/ppermute | solution.py:42
  200.3 12.5 %collective-permute-start.58 = (bf16[96,2304]{1,0:T(8,128)(2,1)S(1)}, bf16[96,2304]{1,0:T(8,128)(2,1)S(1)}, u32[]{:S(2)}, u32[]{:S(2)}) collective-permute-start(bf16[96,2304]{1,0:T(8,128)(2,1)S(1)} %add_convert_fusion.1), channel_id=1, source_target_pairs={{0,8},{8,16},{16,24},{24,28},{28,20},{20,12},{12,4},{4,0},{1,9},{9... | collective-permute-start | bytes 1327112 | tf_op jit(solution)/shard_map/ppermute | solution.py:37
  201.8 7.6 %collective-permute-start.56 = (bf16[96,768]{1,0:T(8,128)(2,1)S(1)}, bf16[96,768]{1,0:T(8,128)(2,1)S(1)}, u32[]{:S(2)}, u32[]{:S(2)}) collective-permute-start(bf16[96,768]{1,0:T(8,128)(2,1)S(1)} %add_convert_fusion.10), channel_id=1, source_target_pairs={{8,0},{16,8},{24,16},{28,24},{20,28},{12,20},{4,12},{0,4},{9,1},{1... | collective-permute-start | bytes 442376 | tf_op jit(solution)/shard_map/ppermute | solution.py:42
  204.5 6.3 %collective-permute-start.52 = (bf16[96,768]{1,0:T(8,128)(2,1)S(1)}, bf16[96,768]{1,0:T(8,128)(2,1)S(1)}, u32[]{:S(2)}, u32[]{:S(2)}) collective-permute-start(bf16[96,768]{1,0:T(8,128)(2,1)S(1)} %add_convert_fusion.12), channel_id=1, source_target_pairs={{0,8},{8,16},{16,24},{24,28},{28,20},{20,12},{12,4},{4,0},{1,9},{9... | collective-permute-start | bytes 442376 | tf_op jit(solution)/shard_map/ppermute | solution.py:37
  206.2 5.7 %collective-permute-start.48 = (bf16[128,768]{1,0:T(8,128)(2,1)S(1)}, bf16[128,768]{1,0:T(8,128)(2,1)S(1)}, u32[]{:S(2)}, u32[]{:S(2)}) collective-permute-start(bf16[128,768]{1,0:T(8,128)(2,1)S(1)} %slice.169), channel_id=1, source_target_pairs={{0,2},{1,3},{2,0},{3,1},{4,6},{5,7},{6,4},{7,5},{8,10},{9,11},{10,... | collective-permute-start | bytes 589832 | tf_op jit(solution)/shard_map/ppermute | solution.py:47
  (10 other events, 49.5 us)
